TPU v7x, 32 devices: a whole 2x2x4 slice. The times are simulated.
32 devices in a mesh: seq: 8 (over z, core), fsdp: 4 (over y, x).
Axes of the slice: x: 2, y: 2, z: 4, core: 2. Of those that a mesh axis runs over, the one named last changes fastest.
Arguments:
- tokens: bfloat16 [8, 1024, 2048], P('fsdp', 'seq'), may hold values from -6 to 6
- attn_gain: bfloat16 [2048], P('fsdp'), may hold values from 0.25 to 1.75
- attn_shift: bfloat16 [2048], P('fsdp'), may hold values from -1.5 to 1.5
- qkv_weight: bfloat16 [2048, 6144], P('fsdp'), may hold values from -0.125 to 0.125
- qkv_bias: bfloat16 [6144], P('fsdp'), may hold values from -1.5 to 1.5
- out_weight: bfloat16 [2048, 2048], P('fsdp'), may hold values from -0.375 to 0.375
- ffn_gain: bfloat16 [2048], P('fsdp'), may hold values from 0.25 to 1.75
- ffn_shift: bfloat16 [2048], P('fsdp'), may hold values from -1.5 to 1.5
- gate_weight: bfloat16 [2048, 5632], P('fsdp'), may hold values from -0.125 to 0.125
- up_weight: bfloat16 [2048, 5632], P('fsdp'), may hold values from -0.125 to 0.125
- down_weight: bfloat16 [5632, 2048], P('fsdp'), may hold values from -0.078125 to 0.078125
- cotangent: bfloat16 [8, 1024, 2048], P('fsdp', 'seq'), may hold values from -6 to 6
Outputs:
- layer_out: bfloat16 [8, 1024, 2048], P('fsdp', 'seq')
- tokens_grad: float32 [8, 1024, 2048], P('fsdp', 'seq')
- attn_gain_grad: float32 [2048], P(('seq', 'fsdp'))
- attn_shift_grad: float32 [2048], P(('seq', 'fsdp'))
- qkv_weight_grad: float32 [2048, 6144], P('fsdp', 'seq')
- qkv_bias_grad: float32 [4096], P(('seq', 'fsdp'))
- value_bias_grad: float32 [2048], P(('seq', 'fsdp'))
- out_weight_grad: float32 [2048, 2048], P('fsdp', 'seq')
- ffn_gain_grad: float32 [2048], P(('seq', 'fsdp'))
- ffn_shift_grad: float32 [2048], P(('seq', 'fsdp'))
- gate_weight_grad: float32 [2048, 5632], P('fsdp', 'seq')
- up_weight_grad: float32 [2048, 5632], P('fsdp', 'seq')
- down_weight_grad: float32 [5632, 2048], P('fsdp', 'seq')
All inputs are finite; a program needn't handle non-finite values.
Results may differ from a plain program's by a relative error of at most 0.023.
Values may be sent and summed in bfloat16 or wider, within the bound.
No kernel may reach another device: no remote copies, remote signals or barrier semaphores. Data moves between devices by JAX's collectives and lax.ppermute only.
A program may use at most 448 MiB of HBM per device.

v0:
```python
import jax
import jax.numpy as jnp
from jax import lax
from jax.sharding import PartitionSpec as P

H = 32
HD = 64
ROT = 16


def layer_norm(inputs, gain_vec, offset):
    center = inputs - jnp.mean(inputs, axis=-1, keepdims=True)
    spread_sq = jnp.mean(center * center, axis=-1, keepdims=True)
    return center * lax.rsqrt(spread_sq + 1e-05) * gain_vec + offset


def tables(places):
    ladder = 10000.0 ** (-jnp.arange(0, ROT, 2, dtype=jnp.float32) / ROT)
    angles = places[:, None] * ladder[None, :]
    return (jnp.cos(angles), jnp.sin(angles))


def rotary(inputs, cosine, sine_tab):
    half_rot = ROT // 2
    first_half = inputs[..., :half_rot]
    second_half = inputs[..., half_rot:ROT]
    return jnp.concatenate(
        [
            first_half * cosine - second_half * sine_tab,
            second_half * cosine + first_half * sine_tab,
            inputs[..., ROT:],
        ],
        axis=-1,
    )


def outer(former, latter):
    return lax.dot_general(
        former, latter, (((0,), (0,)), ((), ())), preferred_element_type=jnp.float32
    )


def backproj(former, matrix):
    return lax.dot_general(
        former, matrix, (((1,), (1,)), ((), ())), preferred_element_type=jnp.float32
    )


def column_form(vector, seq_parts):
    return vector.reshape(seq_parts, -1).T


def attend(queries, key_rows, value_rows):
    seq_count, full_len, heads_here, head_dim = queries.shape
    block_rows = min(512, full_len)
    score_scale = head_dim ** (-0.5)
    columns = jnp.arange(full_len)

    def visit(block_num, state_pair):
        outputs, logsums = state_pair
        row_start = block_num * block_rows
        picked = lax.dynamic_slice_in_dim(queries, row_start, block_rows, 1)
        scores = (
            jnp.einsum("sqhd,skhd->shqk", picked, key_rows, preferred_element_type=jnp.float32)
            * score_scale
        )
        allowed = columns[None, :] <= (row_start + jnp.arange(block_rows))[:, None]
        exponent = jnp.where(allowed, jnp.exp(scores), 0.0)
        row_totals = jnp.sum(exponent, axis=-1)
        probability = (exponent / row_totals[..., None]).astype(jnp.bfloat16)
        partial_out = jnp.einsum(
            "shqk,skhd->sqhd", probability, value_rows, preferred_element_type=jnp.float32
        )
        outputs = lax.dynamic_update_slice_in_dim(
            outputs, partial_out.astype(jnp.bfloat16), row_start, 1
        )
        logsums = lax.dynamic_update_slice_in_dim(logsums, jnp.log(row_totals), row_start, 2)
        return (outputs, logsums)

    start_state = (
        jnp.zeros(queries.shape, jnp.bfloat16),
        jnp.zeros((seq_count, heads_here, full_len), jnp.float32),
    )
    return lax.fori_loop(0, full_len // block_rows, visit, start_state)


def attend_back(queries, key_rows, value_rows, logsums, grad_out):
    seq_count, full_len, heads_here, head_dim = queries.shape
    block_rows = min(512, full_len)
    score_scale = head_dim ** (-0.5)
    columns = jnp.arange(full_len)

    def visit(block_num, state_trio):
        grad_query, grad_key, grad_value = state_trio
        row_start = block_num * block_rows
        picked = lax.dynamic_slice_in_dim(queries, row_start, block_rows, 1)
        picked_grad = lax.dynamic_slice_in_dim(grad_out, row_start, block_rows, 1)
        picked_sums = lax.dynamic_slice_in_dim(logsums, row_start, block_rows, 2)
        scores = (
            jnp.einsum("sqhd,skhd->shqk", picked, key_rows, preferred_element_type=jnp.float32)
            * score_scale
        )
        allowed = columns[None, :] <= (row_start + jnp.arange(block_rows))[:, None]
        probability = jnp.where(allowed, jnp.exp(scores - picked_sums[..., None]), 0.0)
        grad_prob = jnp.einsum(
            "sqhd,skhd->shqk", picked_grad, value_rows, preferred_element_type=jnp.float32
        )
        inner = jnp.sum(probability * grad_prob, axis=-1, keepdims=True)
        grad_scores = (probability * (grad_prob - inner)).astype(jnp.bfloat16)
        block_query = (
            jnp.einsum("shqk,skhd->sqhd", grad_scores, key_rows, preferred_element_type=jnp.float32)
            * score_scale
        )
        grad_query = lax.dynamic_update_slice_in_dim(grad_query, block_query, row_start, 1)
        grad_key = grad_key + jnp.einsum(
            "shqk,sqhd->skhd", grad_scores, picked, preferred_element_type=jnp.float32
        )
        grad_value = grad_value + jnp.einsum(
            "shqk,sqhd->skhd",
            probability.astype(jnp.bfloat16),
            picked_grad,
            preferred_element_type=jnp.float32,
        )
        return (grad_query, grad_key, grad_value)

    empty = jnp.zeros(queries.shape, jnp.float32)
    grad_query, grad_key, grad_value = lax.fori_loop(
        0, full_len // block_rows, visit, (empty, empty, empty)
    )
    return (grad_query, grad_key * score_scale, grad_value)


def spread(first_grad, second_grad, third_grad, fourth_grad, fifth_grad):
    summed = (
        lax.psum_scatter(
            first_grad.astype(jnp.bfloat16), "seq", scatter_dimension=1, tiled=True
        ).astype(jnp.float32),
        lax.psum_scatter(
            second_grad.astype(jnp.bfloat16), "seq", scatter_dimension=1, tiled=True
        ).astype(jnp.float32),
        lax.psum_scatter(
            third_grad.astype(jnp.bfloat16), "seq", scatter_dimension=1, tiled=True
        ).astype(jnp.float32),
        lax.psum_scatter(
            fourth_grad.astype(jnp.bfloat16), "seq", scatter_dimension=1, tiled=True
        ).astype(jnp.float32),
        lax.psum_scatter(
            fifth_grad.astype(jnp.bfloat16), "seq", scatter_dimension=1, tiled=True
        ).astype(jnp.float32),
    )
    return (
        lax.psum_scatter(
            summed[0].astype(jnp.bfloat16), "fsdp", scatter_dimension=0, tiled=True
        ).astype(jnp.float32),
        lax.psum_scatter(
            summed[1].astype(jnp.bfloat16), "fsdp", scatter_dimension=0, tiled=True
        ).astype(jnp.float32),
        lax.psum_scatter(
            summed[2].astype(jnp.bfloat16), "fsdp", scatter_dimension=0, tiled=True
        ).astype(jnp.float32),
        lax.psum_scatter(
            summed[3].astype(jnp.bfloat16), "fsdp", scatter_dimension=0, tiled=True
        ).astype(jnp.float32),
        lax.psum_scatter(
            summed[4].astype(jnp.bfloat16), "fsdp", scatter_dimension=0, tiled=True
        ).astype(jnp.float32),
    )


def on_device(
    tokens,
    attn_gain,
    attn_shift,
    qkv_weight,
    qkv_bias,
    out_weight,
    ffn_gain,
    ffn_shift,
    gate_weight,
    up_weight,
    down_weight,
    cotangent,
):
    seq_count, local_len, width = tokens.shape
    seq_parts = lax.axis_size("seq")
    fsdp_parts = lax.axis_size("fsdp")
    device_count = seq_parts * fsdp_parts
    full_len = local_len * seq_parts
    row_count = seq_count * local_len
    heads_here = H // seq_parts
    attn_set = (
        lax.all_gather(attn_gain, "fsdp", axis=0, tiled=True),
        lax.all_gather(attn_shift, "fsdp", axis=0, tiled=True),
        lax.all_gather(qkv_weight, "fsdp", axis=0, tiled=True),
        lax.all_gather(qkv_bias, "fsdp", axis=0, tiled=True),
        lax.all_gather(out_weight, "fsdp", axis=0, tiled=True),
    )
    flat_tokens = tokens.reshape(row_count, width).astype(jnp.float32)
    normed, norm_back = jax.vjp(
        layer_norm, flat_tokens, attn_set[0].astype(jnp.float32), attn_set[1].astype(jnp.float32)
    )
    normed_low = normed.astype(jnp.bfloat16)
    mixed_proj = jnp.dot(normed_low, attn_set[2], preferred_element_type=jnp.float32) + attn_set[
        3
    ].astype(jnp.float32)
    places = (lax.axis_index("seq") * local_len + jnp.arange(local_len)).astype(jnp.float32)
    cosine, sine_tab = tables(places)
    cosine = cosine[:, None, None, :]
    sine_tab = sine_tab[:, None, None, :]
    split_proj = mixed_proj.reshape(seq_count, local_len, 3, H, HD)
    turned, turn_back = jax.vjp(
        lambda inner_qk: rotary(inner_qk, cosine, sine_tab), split_proj[:, :, :2]
    )
    outgoing = (
        jnp.concatenate([turned, split_proj[:, :, 2:]], axis=2)
        .astype(jnp.bfloat16)
        .reshape(seq_count, local_len, 3, H * HD)
    )
    by_heads = lax.all_to_all(outgoing, "seq", split_axis=3, concat_axis=1, tiled=True)
    head_view = by_heads.reshape(seq_count, full_len, 3, heads_here, HD)
    queries = head_view[:, :, 0]
    key_rows = head_view[:, :, 1]
    value_rows = head_view[:, :, 2]
    attended, logsums = attend(queries, key_rows, value_rows)
    back_tokens = lax.all_to_all(
        attended.reshape(seq_count, full_len, heads_here * HD),
        "seq",
        split_axis=1,
        concat_axis=2,
        tiled=True,
    )
    heads_low = back_tokens.reshape(row_count, width)
    middle = flat_tokens + jnp.dot(heads_low, attn_set[4], preferred_element_type=jnp.float32)
    ffn_set = (
        lax.all_gather(ffn_gain, "fsdp", axis=0, tiled=True),
        lax.all_gather(ffn_shift, "fsdp", axis=0, tiled=True),
        lax.all_gather(gate_weight, "fsdp", axis=0, tiled=True),
        lax.all_gather(up_weight, "fsdp", axis=0, tiled=True),
        lax.all_gather(down_weight, "fsdp", axis=0, tiled=True),
    )
    normed_two, norm_two_back = jax.vjp(
        layer_norm, middle, ffn_set[0].astype(jnp.float32), ffn_set[1].astype(jnp.float32)
    )
    normed_two_low = normed_two.astype(jnp.bfloat16)
    gate_proj = jnp.dot(normed_two_low, ffn_set[2], preferred_element_type=jnp.float32)
    upward = jnp.dot(normed_two_low, ffn_set[3], preferred_element_type=jnp.float32)
    hidden_full, act_back = jax.vjp(
        lambda gate_in, up_in: jax.nn.silu(gate_in) * up_in, gate_proj, upward
    )
    hidden = hidden_full.astype(jnp.bfloat16)
    result_rows = middle + jnp.dot(hidden, ffn_set[4], preferred_element_type=jnp.float32)
    layer_out = result_rows.astype(jnp.bfloat16).reshape(tokens.shape)
    gate_full, up_full, down_full = (
        lax.all_gather(gate_weight, "fsdp", axis=0, tiled=True),
        lax.all_gather(up_weight, "fsdp", axis=0, tiled=True),
        lax.all_gather(down_weight, "fsdp", axis=0, tiled=True),
    )
    grad_rows = cotangent.reshape(row_count, width)
    grad_hidden = backproj(grad_rows, down_full)
    grad_gate, grad_up = act_back(grad_hidden)
    grad_gate_low = grad_gate.astype(jnp.bfloat16)
    grad_up_low = grad_up.astype(jnp.bfloat16)
    grad_normed_two = backproj(grad_gate_low, gate_full) + backproj(grad_up_low, up_full)
    grad_middle_part, ffn_gain_part, ffn_shift_part = norm_two_back(grad_normed_two)
    grad_middle = grad_rows.astype(jnp.float32) + grad_middle_part
    gate_grad = outer(normed_two_low, grad_gate_low)
    up_grad = outer(normed_two_low, grad_up_low)
    down_grad = outer(hidden, grad_rows)
    ffn_grads = spread(
        gate_grad,
        up_grad,
        down_grad,
        column_form(ffn_gain_part, seq_parts),
        column_form(ffn_shift_part, seq_parts),
    )
    gate_result, up_result, down_result = (ffn_grads[0], ffn_grads[1], ffn_grads[2])
    qkv_full, out_full = (
        lax.all_gather(qkv_weight, "fsdp", axis=0, tiled=True),
        lax.all_gather(out_weight, "fsdp", axis=0, tiled=True),
    )
    grad_middle_low = grad_middle.astype(jnp.bfloat16)
    grad_heads = (
        backproj(grad_middle_low, out_full)
        .astype(jnp.bfloat16)
        .reshape(seq_count, local_len, width)
    )
    grad_by_heads = lax.all_to_all(
        grad_heads, "seq", split_axis=2, concat_axis=1, tiled=True
    ).reshape(seq_count, full_len, heads_here, HD)
    grad_query, grad_key, grad_value = attend_back(
        queries, key_rows, value_rows, logsums, grad_by_heads
    )
    stacked = (
        jnp.stack([grad_query, grad_key, grad_value], axis=2)
        .astype(jnp.bfloat16)
        .reshape(seq_count, full_len, 3, heads_here * HD)
    )
    grad_tok_side = lax.all_to_all(stacked, "seq", split_axis=1, concat_axis=3, tiled=True).reshape(
        seq_count, local_len, 3, H, HD
    )
    (grad_turned,) = turn_back(grad_tok_side[:, :, :2].astype(jnp.float32))
    grad_mixed = (
        jnp.concatenate([grad_turned, grad_tok_side[:, :, 2:].astype(jnp.float32)], axis=2)
        .reshape(row_count, 3 * width)
        .astype(jnp.bfloat16)
    )
    qkv_bias_part = jnp.sum(grad_mixed, axis=0, dtype=jnp.float32)
    query_key_part = qkv_bias_part[: 2 * width]
    value_part = qkv_bias_part[2 * width :]
    grad_normed = backproj(grad_mixed, qkv_full)
    grad_token_part, attn_gain_part, attn_shift_part = norm_back(grad_normed)
    tokens_grad = (grad_middle + grad_token_part).reshape(tokens.shape)
    qkv_grad = outer(normed_low, grad_mixed)
    out_grad = outer(heads_low, grad_middle_low)
    packed_bias = jnp.concatenate(
        [query_key_part.reshape(device_count, -1), value_part.reshape(device_count, -1)], axis=1
    ).reshape(-1)
    attn_grads = spread(
        qkv_grad,
        out_grad,
        column_form(packed_bias, seq_parts),
        column_form(attn_gain_part, seq_parts),
        column_form(attn_shift_part, seq_parts),
    )
    qkv_result, out_result = (attn_grads[0], attn_grads[1])
    bias_pair = attn_grads[2].reshape(-1)
    query_key_len = 2 * width // device_count
    bias_result = bias_pair[:query_key_len]
    value_bias_result = bias_pair[query_key_len:]
    attn_gain_result = attn_grads[3].reshape(-1)
    attn_shift_result = attn_grads[4].reshape(-1)
    ffn_gain_result = ffn_grads[3].reshape(-1)
    ffn_shift_result = ffn_grads[4].reshape(-1)
    return (
        layer_out,
        tokens_grad,
        attn_gain_result,
        attn_shift_result,
        qkv_result,
        bias_result,
        value_bias_result,
        out_result,
        ffn_gain_result,
        ffn_shift_result,
        gate_result,
        up_result,
        down_result,
    )


def solution(mesh):
    return jax.shard_map(
        on_device,
        mesh=mesh,
        in_specs=(
            P("fsdp", "seq", None),
            P("fsdp"),
            P("fsdp"),
            P("fsdp", None),
            P("fsdp"),
            P("fsdp", None),
            P("fsdp"),
            P("fsdp"),
            P("fsdp", None),
            P("fsdp", None),
            P("fsdp", None),
            P("fsdp", "seq", None),
        ),
        out_specs=(
            P("fsdp", "seq", None),
            P("fsdp", "seq", None),
            P(("seq", "fsdp")),
            P(("seq", "fsdp")),
            P("fsdp", "seq"),
            P(("seq", "fsdp")),
            P(("seq", "fsdp")),
            P("fsdp", "seq"),
            P(("seq", "fsdp")),
            P(("seq", "fsdp")),
            P("fsdp", "seq"),
            P("fsdp", "seq"),
            P("fsdp", "seq"),
        ),
        check_vma=False,
    )
```

profile of v0, /device:TPU:0, one launch (start us, length us, event | category | flops | bytes accessed | tf_op | source)
XLA Modules:
  0.0 2495.8 jit_solution(1748476683243220867)
XLA Ops:
  38.5 201.7 %all-gather.11.cloned.1.call-done = bf16[2048,6144]{1,0:T(8,128)(2,1)} async-done(((bf16[512,6144]{1,0:T(8,128)(2,1)}), bf16[2048,6144]{1,0:T(8,128)(2,1)}) %all-gather.11.cloned.1.call-update) | async-done | bytes 25165840 | tf_op jit(solution)/shard_map/all_gather | solution.py:194
  240.3 13.3 convolution_add_fusion
  282.3 28.8 %copy.82 = bf16[2,128,3,2048]{1,0,2,3:T(2,128)(2,1)} copy(bf16[2,128,3,2048]{1,3,2,0:T(8,128)(2,1)S(1)} %pad_maximum_fusion) | data formatting | bytes 6291456 | tf_op jit(solution)/shard_map/concatenate | solution.py:215
  315.9 71.5 %all-to-all-done = bf16[2,128,3,2048]{1,0,2,3:T(2,128)(2,1)S(1)} async-done(((bf16[2,128,3,2048]{1,0,2,3:T(2,128)(2,1)}), bf16[2,128,3,2048]{1,0,2,3:T(2,128)(2,1)S(1)}, u32[]{:S(2)}, u32[]{:S(2)}) %all-to-all-start) | async-done | bytes 3145760 | tf_op jit(solution)/shard_map/all_to_all | solution.py:219
  397.0 22.2 while.34
  460.4 81.6 %all-gather.15.cloned.1.call-done = bf16[2048,5632]{1,0:T(8,128)(2,1)} async-done(((bf16[512,5632]{1,0:T(8,128)(2,1)}), bf16[2048,5632]{1,0:T(8,128)(2,1)}) %all-gather.15.cloned.1.call-update) | async-done | bytes 23068688 | tf_op jit(solution)/shard_map/all_gather | solution.py:237
  542.0 14.5 fusion.53
  556.5 197.6 %all-gather.17.cloned.1.call-done = bf16[2048,5632]{1,0:T(8,128)(2,1)} async-done(((bf16[512,5632]{1,0:T(8,128)(2,1)}), bf16[2048,5632]{1,0:T(8,128)(2,1)}) %all-gather.17.cloned.1.call-update) | async-done | bytes 23068688 | tf_op jit(solution)/shard_map/all_gather | solution.py:238
  754.1 14.3 fusion.54
  768.3 197.8 %all-gather.19.cloned.1.call-done = bf16[5632,2048]{1,0:T(8,128)(2,1)} async-done(((bf16[1408,2048]{1,0:T(8,128)(2,1)}), bf16[5632,2048]{1,0:T(8,128)(2,1)}) %all-gather.19.cloned.1.call-update) | async-done | bytes 23068688 | tf_op jit(solution)/shard_map/all_gather | solution.py:239
  966.1 25.9 %multiply_convert_fusion.1 = (bf16[256,5632]{1,0:T(8,128)(2,1)}, bf16[256,5632]{1,0:T(8,128)(2,1)}, bf16[256,5632]{1,0:T(8,128)(2,1)}) fusion(f32[256,5632]{1,0:T(8,128)} %fusion.53, f32[256,5632]{1,0:T(8,128)} %fusion.54, bf16[256,2048]{1,0:T(8,128)(2,1)S(1)} %bitcast.190, bf16[5632,2048]{1,0:T(8,128)(2,1)} %all-gather.19.cloned.1.call-done), kind=kOutput, calls=%fused_computation.54 | convolution fusion | flops 5928648704 | bytes 44302336 | tf_op jit(solution)/shard_map/dot_general | solution.py:44
  1004.7 14.3 multiply_reduce_fusion.1
  1029.0 13.1 convolution_convert_fusion.3
  1056.3 13.1 convolution_convert_fusion
  1081.9 43.7 %all-to-all-done.2 = bf16[2,128,2048]{1,0,2:T(2,128)(2,1)S(1)} async-done(((bf16[2,128,2048]{1,0,2:T(2,128)(2,1)}), bf16[2,128,2048]{1,0,2:T(2,128)(2,1)S(1)}, u32[]{:S(2)}, u32[]{:S(2)}) %all-to-all-start.2) | async-done | bytes 1048608 | tf_op jit(solution)/shard_map/all_to_all | solution.py:287
  1128.7 100.1 %while.35 = (s32[]{:T(128)}, bf16[2,1024,4,64]{1,3,2,0:T(8,128)(2,1)}, f32[2,1024,4,64]{1,3,2,0:T(8,128)}, f32[2,1024,4,64]{1,3,2,0:T(8,128)}, bf16[2,1024,4,64]...) while((s32[]{:T(128)}, ...), condition=%wide.region_11.12_spmd.clone, body=%wide.region_9.11_spmd.clone.sunk | while | flops 2750149120 | bytes 297914720 | solution.py:127
  1244.9 122.1 %all-to-all-done.3 = bf16[2,1024,3,256]{3,0,2,1:T(2,128)(2,1)} async-done(((bf16[2,1024,3,256]{3,0,2,1:T(2,128)(2,1)}), bf16[2,1024,3,256]{3,0,2,1:T(2,128)(2,1)}, u32[]{:S(2)}, u32[]{:S(2)}) %all-to-all-start.3) | async-done | bytes 3145760 | tf_op jit(solution)/shard_map/all_to_all | solution.py:298
  1386.3 18.4 fusion.50
  1404.6 13.8 convolution_convert_fusion.1
  1433.6 27.1 %all-reduce.8 = (bf16[256,8]{0,1:T(8,128)(2,1)S(1)}, bf16[256,8]{0,1:T(8,128)(2,1)S(1)}, bf16[768,8]{0,1:T(8,128)(2,1)S(1)}, bf16[256,8]{0,1:T(8,128)(2,1)S(1)}, bf16[256,8]{0,1:T(8,128)(2,1)S(1)}) all-reduce(bf16[256,8]{0,1:T(8,128)(2,1)S(1)} %bitcast.220, ...), channel_id=2, replica_groups=mesh['seq'=8,'fsdp'=4] {'seq'}, use_global_device_ids=true, to_apply=%region_15.16.clone | all-reduce | flops 14336 | bytes 57344
  1469.4 194.1 %reduce-scatter.38.cloned.1.call-done = bf16[2048,704]{0,1:T(8,128)(2,1)} async-done(((bf16[2048,5632]{0,1:T(8,128)(2,1)}), bf16[2048,704]{0,1:T(8,128)(2,1)}) %reduce-scatter.38.cloned.1.call-update) | async-done | bytes 2883600 | tf_op jit(solution)/shard_map/reduce_scatter | solution.py:138
  1663.6 227.8 %reduce-scatter.42.cloned.1.call-done = bf16[5632,256]{1,0:T(8,128)(2,1)} async-done(((bf16[5632,2048]{1,0:T(8,128)(2,1)}), bf16[5632,256]{1,0:T(8,128)(2,1)}) %reduce-scatter.42.cloned.1.call-update) | async-done | bytes 2883600 | tf_op jit(solution)/shard_map/reduce_scatter | solution.py:141
  1891.4 247.7 %reduce-scatter.26.cloned.1.call-done = bf16[2048,768]{1,0:T(8,128)(2,1)} async-done(((bf16[2048,6144]{1,0:T(8,128)(2,1)}), bf16[2048,768]{1,0:T(8,128)(2,1)}) %reduce-scatter.26.cloned.1.call-update) | async-done | bytes 3145744 | tf_op jit(solution)/shard_map/reduce_scatter | solution.py:135
  2165.9 26.5 %reduce-scatter.48.cloned.1.call-done = bf16[64,1]{1,0:T(8,128)(2,1)} async-done(((bf16[256,1]{1,0:T(8,128)(2,1)}), bf16[64,1]{1,0:T(8,128)(2,1)}) %reduce-scatter.48.cloned.1.call-update) | async-done | bytes 144
  2193.2 26.6 %reduce-scatter.52.cloned.1.call-done = bf16[64,1]{1,0:T(8,128)(2,1)} async-done(((bf16[256,1]{1,0:T(8,128)(2,1)}), bf16[64,1]{1,0:T(8,128)(2,1)}) %reduce-scatter.52.cloned.1.call-update) | async-done | bytes 144
  2220.6 26.5 %reduce-scatter.54.cloned.1.call-done = bf16[64,1]{1,0:T(8,128)(2,1)} async-done(((bf16[256,1]{1,0:T(8,128)(2,1)}), bf16[64,1]{1,0:T(8,128)(2,1)}) %reduce-scatter.54.cloned.1.call-update) | async-done | bytes 144
  2249.9 24.6 reduce-scatter.50.cloned.1.call-done
  2276.4 28.8 %reduce-scatter.32.cloned.1.call-done = bf16[512,256]{1,0:T(8,128)(2,1)} async-done(((bf16[2048,256]{1,0:T(8,128)(2,1)}), bf16[512,256]{1,0:T(8,128)(2,1)}) %reduce-scatter.32.cloned.1.call-update) | async-done | bytes 262160 | tf_op jit(solution)/shard_map/reduce_scatter | solution.py:155
  2307.0 42.9 %reduce-scatter.36.cloned.1.call-done = bf16[512,704]{0,1:T(8,128)(2,1)} async-done(((bf16[2048,704]{0,1:T(8,128)(2,1)}), bf16[512,704]{0,1:T(8,128)(2,1)}) %reduce-scatter.36.cloned.1.call-update) | async-done | bytes 720912 | tf_op jit(solution)/shard_map/reduce_scatter | solution.py:152
  2352.3 42.2 %reduce-scatter.40.cloned.1.call-done = bf16[512,704]{0,1:T(8,128)(2,1)} async-done(((bf16[2048,704]{0,1:T(8,128)(2,1)}), bf16[512,704]{0,1:T(8,128)(2,1)}) %reduce-scatter.40.cloned.1.call-update) | async-done | bytes 720912 | tf_op jit(solution)/shard_map/reduce_scatter | solution.py:155
  2396.9 42.4 %reduce-scatter.44.cloned.1.call-done = bf16[1408,256]{1,0:T(8,128)(2,1)} async-done(((bf16[5632,256]{1,0:T(8,128)(2,1)}), bf16[1408,256]{1,0:T(8,128)(2,1)}) %reduce-scatter.44.cloned.1.call-update) | async-done | bytes 720912 | tf_op jit(solution)/shard_map/reduce_scatter | solution.py:158
  2441.7 44.5 %reduce-scatter.28.cloned.1.call-done = bf16[512,768]{1,0:T(8,128)(2,1)} async-done(((bf16[2048,768]{1,0:T(8,128)(2,1)}), bf16[512,768]{1,0:T(8,128)(2,1)}) %reduce-scatter.28.cloned.1.call-update) | async-done | bytes 786448 | tf_op jit(solution)/shard_map/reduce_scatter | solution.py:152
  (309 shorter events, 392.5 us)
Async XLA Ops:
  7.2 233.1 %all-gather.11.cloned.1.call-start = ((), (), s32[]{:S(2)}) async-start(), calls=%async_computation.19 | async-start | bytes 31457280 | tf_op jit(solution)/shard_map/all_gather | solution.py:194
  7.9 444.5 %all-gather.13.cloned.1.call-start = ((), (), s32[]{:S(2)}) async-start(), calls=%async_computation.20 | async-start | bytes 10485760 | tf_op jit(solution)/shard_map/all_gather | solution.py:196
  8.7 533.3 %all-gather.15.cloned.1.call-start = ((), (), s32[]{:S(2)}) async-start(), calls=%async_computation.21 | async-start | bytes 28835840 | tf_op jit(solution)/shard_map/all_gather | solution.py:237
  9.4 744.7 %all-gather.17.cloned.1.call-start = ((), (), s32[]{:S(2)}) async-start(), calls=%async_computation.22 | async-start | bytes 28835840 | tf_op jit(solution)/shard_map/all_gather | solution.py:238
  10.0 956.1 %all-gather.19.cloned.1.call-start = ((), (), s32[]{:S(2)}) async-start(), calls=%async_computation.23 | async-start | bytes 28835840 | tf_op jit(solution)/shard_map/all_gather | solution.py:239
  20.2 233.3 %copy-start.27 = (f32[4,1,512]{2,1,0:T(1,128)}, f32[4,1,512]{2,1,0:T(1,128)S(1)}, u32[]{:S(2)}) copy-start(f32[4,1,512]{2,1,0:T(1,128)S(1)} %convert_element_type.276) | copy-start | bytes 24580
  28.4 225.2 %copy-start.25 = (f32[4,1,512]{2,1,0:T(1,128)}, f32[4,1,512]{2,1,0:T(1,128)S(1)}, u32[]{:S(2)}) copy-start(f32[4,1,512]{2,1,0:T(1,128)S(1)} %convert_element_type.275) | copy-start | bytes 24580
  37.6 239.3 %copy-start.29 = (f32[128,8]{0,1:T(8,128)}, f32[128,8]{0,1:T(8,128)S(1)}, u32[]{:S(2)}) copy-start(f32[128,8]{0,1:T(8,128)S(1)} %get-tuple-element.420) | copy-start | bytes 12292
  37.6 239.3 %copy-start.31 = (f32[128,8]{0,1:T(8,128)}, f32[128,8]{0,1:T(8,128)S(1)}, u32[]{:S(2)}) copy-start(f32[128,8]{0,1:T(8,128)S(1)} %get-tuple-element.421) | copy-start | bytes 12292
  311.2 76.3 %all-to-all-start = ((bf16[2,128,3,2048]{1,0,2,3:T(2,128)(2,1)}), bf16[2,128,3,2048]{1,0,2,3:T(2,128)(2,1)S(1)}, u32[]{:S(2)}, u32[]{:S(2)}) async-start(bf16[2,128,3,2048]{1,0,2,3:T(2,128)(2,1)} %copy.82), calls=%async_computation | async-start | bytes 6291456 | tf_op jit(solution)/shard_map/all_to_all | solution.py:219
  419.2 39.4 %copy-start.5 = (bf16[2,1024,4,64]{1,3,2,0:T(8,128)(2,1)}, bf16[2,1024,4,64]{1,3,2,0:T(8,128)(2,1)S(1)}, u32[]{:S(2)}) copy-start(bf16[2,1024,4,64]{1,3,2,0:T(8,128)(2,1)S(1)} %get-tuple-element.627) | copy-start | bytes 3145732
  421.3 30.1 %all-to-all-start.1 = ((bf16[2,1024,256]{2,0,1:T(2,128)(2,1)}), bf16[2,1024,256]{2,0,1:T(2,128)(2,1)S(1)}, u32[]{:S(2)}, u32[]{:S(2)}) async-start(bf16[2,1024,256]{2,0,1:T(2,128)(2,1)} %copy.85), calls=%async_computation.1 | async-start | bytes 2097152 | tf_op jit(solution)/shard_map/all_to_all | solution.py:225
  424.9 1043.3 %reduce-scatter.30.cloned.1.call-start = ((), (), s32[]{:S(2)}) async-start(), calls=%async_computation.26 | async-start | bytes 9437184 | tf_op jit(solution)/shard_map/reduce_scatter | solution.py:138
  556.5 409.7 %copy-start.15 = (bf16[2,128,2048]{2,1,0:T(8,128)(2,1)S(1)}, bf16[2,128,2048]{2,1,0:T(8,128)(2,1)}, u32[]{:S(2)}) copy-start(bf16[2,128,2048]{2,1,0:T(8,128)(2,1)} %param.27) | copy-start | bytes 3145732
  1029.0 439.9 %reduce-scatter.34.cloned.1.call-start = ((), (), s32[]{:S(2)}) async-start(), calls=%async_computation.28 | async-start | bytes 25952256 | tf_op jit(solution)/shard_map/reduce_scatter | solution.py:135
  1042.1 621.4 %reduce-scatter.38.cloned.1.call-start = ((), (), s32[]{:S(2)}) async-start(), calls=%async_computation.30 | async-start | bytes 25952256 | tf_op jit(solution)/shard_map/reduce_scatter | solution.py:138
  1055.1 836.2 %reduce-scatter.42.cloned.1.call-start = ((), (), s32[]{:S(2)}) async-start(), calls=%async_computation.32 | async-start | bytes 25952256 | tf_op jit(solution)/shard_map/reduce_scatter | solution.py:141
  1077.3 48.3 %all-to-all-start.2 = ((bf16[2,128,2048]{1,0,2:T(2,128)(2,1)}), bf16[2,128,2048]{1,0,2:T(2,128)(2,1)S(1)}, u32[]{:S(2)}, u32[]{:S(2)}) async-start(bf16[2,128,2048]{1,0,2:T(2,128)(2,1)} %copy.88), calls=%async_computation.2 | async-start | bytes 2097152 | tf_op jit(solution)/shard_map/all_to_all | solution.py:287
  1081.8 46.8 %copy-start.24 = (f32[2,4,1024]{2,1,0:T(4,128)S(1)}, f32[2,4,1024]{2,1,0:T(4,128)}, u32[]{:S(2)}) copy-start(f32[2,4,1024]{2,1,0:T(4,128)} %copy-done.23) | copy-start | bytes 98308
  1238.8 128.3 %all-to-all-start.3 = ((bf16[2,1024,3,256]{3,0,2,1:T(2,128)(2,1)}), bf16[2,1024,3,256]{3,0,2,1:T(2,128)(2,1)}, u32[]{:S(2)}, u32[]{:S(2)}) async-start(bf16[2,1024,3,256]{3,0,2,1:T(2,128)(2,1)} %copy.90), calls=%async_computation.3 | async-start | bytes 6291456 | tf_op jit(solution)/shard_map/all_to_all | solution.py:298
  1243.4 895.8 %reduce-scatter.26.cloned.1.call-start = ((), (), s32[]{:S(2)}) async-start(), calls=%async_computation.24 | async-start | bytes 28311552 | tf_op jit(solution)/shard_map/reduce_scatter | solution.py:135
  1418.4 746.6 %reduce-scatter.46.cloned.1.call-start = ((), (), s32[]{:S(2)}) async-start(), calls=%async_computation.34 | async-start | bytes 81920
  1462.1 730.3 %reduce-scatter.48.cloned.1.call-start = ((), (), s32[]{:S(2)}) async-start(), calls=%async_computation.35 | async-start | bytes 81920
  1463.6 756.2 %reduce-scatter.52.cloned.1.call-start = ((), (), s32[]{:S(2)}) async-start(), calls=%async_computation.37 | async-start | bytes 81920
  1465.1 782.0 %reduce-scatter.54.cloned.1.call-start = ((), (), s32[]{:S(2)}) async-start(), calls=%async_computation.38 | async-start | bytes 81920
  1466.6 807.9 %reduce-scatter.50.cloned.1.call-start = ((), (), s32[]{:S(2)}) async-start(), calls=%async_computation.36 | async-start | bytes 245760
  1468.2 837.1 %reduce-scatter.32.cloned.1.call-start = ((), (), s32[]{:S(2)}) async-start(), calls=%async_computation.27 | async-start | bytes 1310720 | tf_op jit(solution)/shard_map/reduce_scatter | solution.py:155
  1468.8 881.1 %reduce-scatter.36.cloned.1.call-start = ((), (), s32[]{:S(2)}) async-start(), calls=%async_computation.29 | async-start | bytes 3604480 | tf_op jit(solution)/shard_map/reduce_scatter | solution.py:152
  1469.4 925.2 %reduce-scatter.40.cloned.1.call-start = ((), (), s32[]{:S(2)}) async-start(), calls=%async_computation.31 | async-start | bytes 3604480 | tf_op jit(solution)/shard_map/reduce_scatter | solution.py:155
  1663.6 775.8 %reduce-scatter.44.cloned.1.call-start = ((), (), s32[]{:S(2)}) async-start(), calls=%async_computation.33 | async-start | bytes 3604480 | tf_op jit(solution)/shard_map/reduce_scatter | solution.py:158
  1891.4 247.8 %copy-start.13 = (f32[256,2048]{1,0:T(8,128)S(1)}, f32[256,2048]{1,0:T(8,128)}, u32[]{:S(2)}) copy-start(f32[256,2048]{1,0:T(8,128)} %copy-done.11) | copy-start | bytes 6291460
  1891.4 594.7 %reduce-scatter.28.cloned.1.call-start = ((), (), s32[]{:S(2)}) async-start(), calls=%async_computation.25 | async-start | bytes 3932160 | tf_op jit(solution)/shard_map/reduce_scatter | solution.py:152
  (48 other events, 350.2 us)
Sparse Core Ops, SparseCore 0:
  9.9 230.3 all-gather.10
  242.1 87.4 all-gather.12
  331.5 210.4 all-gather.14
  543.7 210.3 all-gather.16
  755.8 210.3 all-gather.18
  1029.1 106.3 reduce-scatter.29
  1137.9 281.0 reduce-scatter.33
  1421.3 242.2 reduce-scatter.37
  1665.9 225.4 reduce-scatter.41
  1893.6 245.5 reduce-scatter.25
  2142.5 22.5 reduce-scatter.45
  2168.2 24.1 reduce-scatter.47
  2195.7 24.0 reduce-scatter.51
  2222.9 24.0 reduce-scatter.53
  2250.2 24.2 reduce-scatter.49
  2277.3 27.9 reduce-scatter.31
  2308.1 41.7 reduce-scatter.35
  2352.8 41.7 reduce-scatter.39
  2397.6 41.7 reduce-scatter.43
  2442.2 43.8 reduce-scatter.27
where the time goes:
time: 2510 us; the launch traced here: 2500 us
  waiting for transfers between devices  1920 us (76%)
  matrix products  280 us (11%)
  local copies, waits for them, and re-layouts  112 us (4%)
  other arithmetic  84.3 us (3%)
  blocking collectives  68.5 us (3%)
    reduce_scatter x2, waiting for transfers between devices, spread(): lax.psum_scatter(first_grad.astype(jnp.bfloat16), 'seq', scatter_dimensio...  248 us
    reduce_scatter x1, waiting for transfers between devices, spread(): lax.psum_scatter(third_grad.astype(jnp.bfloat16), 'seq', scatter_dimensio...  228 us
    all_gather x1, waiting for transfers between devices, on_device(): lax.all_gather(qkv_weight, 'fsdp', axis=0, tiled=True)  202 us
    all_gather x1, waiting for transfers between devices, on_device(): lax.all_gather(down_weight, 'fsdp', axis=0, tiled=True)  198 us
    all_gather x1, waiting for transfers between devices, on_device(): lax.all_gather(up_weight, 'fsdp', axis=0, tiled=True)  198 us
    reduce_scatter x2, waiting for transfers between devices, spread(): lax.psum_scatter(second_grad.astype(jnp.bfloat16), 'seq', scatter_dimensi...  194 us
    all_to_all x1, waiting for transfers between devices, on_device(): lax.all_to_all(stacked, 'seq', split_axis=1, concat_axis=3, tiled=True)  122 us
    unnamed x25, waiting for transfers between devices  119 us
  transfers between devices with their start and end apart: 24, of which 21 were waited for; matrix products, arithmetic and copies ran while one was open for 16% of the time, Pallas kernels for 0%

commit v1 on v0

v1 whole, which is shorter than its diff:
```python
import functools

import jax
import jax.numpy as jnp
import numpy as np
from jax import lax
from jax.experimental import pallas as pl
from jax.experimental.pallas import tpu as pltpu
from jax.sharding import PartitionSpec as P

H = 32
HD = 64
ROT = 16
PAIR = 2 * HD
MESH_AXES = ("seq", "fsdp")


def nn(a, b):
    return lax.dot_general(a, b, (((1,), (0,)), ((), ())), preferred_element_type=jnp.float32)


def nt(a, b):
    return lax.dot_general(a, b, (((1,), (1,)), ((), ())), preferred_element_type=jnp.float32)


def tn(a, b):
    return lax.dot_general(a, b, (((0,), (0,)), ((), ())), preferred_element_type=jnp.float32)


def norm_stats(x):
    mean = jnp.mean(x, axis=-1, keepdims=True)
    center = x - mean
    var = jnp.mean(center * center, axis=-1, keepdims=True)
    r = lax.rsqrt(var + 1e-05)
    return center * r, r


def norm_back(dn, xh, r, gain):
    e = dn * gain
    return r * (
        e
        - jnp.mean(e, axis=-1, keepdims=True)
        - xh * jnp.mean(e * xh, axis=-1, keepdims=True)
    )


def rotary_tables(length):
    lane = jnp.arange(PAIR) % HD
    ladder = 10000.0 ** (-jnp.arange(0, ROT, 2, dtype=jnp.float32) / ROT)
    places = jnp.arange(length, dtype=jnp.float32)
    angles = places[:, None] * ladder[None, :]
    cosine = jnp.tile(jnp.cos(angles), (1, PAIR // (ROT // 2)))
    sine = jnp.tile(jnp.sin(angles), (1, PAIR // (ROT // 2)))
    first = lane < ROT // 2
    second = (lane >= ROT // 2) & (lane < ROT)
    turned = first | second
    cos_tab = jnp.where(turned[None, :], cosine, 1.0)
    minus = jnp.where(first[None, :], -sine, 0.0)
    plus = jnp.where(second[None, :], sine, 0.0)
    return cos_tab, minus, plus


def rotate(x, cos_tab, minus, plus):
    ahead = pltpu.roll(x, PAIR - ROT // 2, 1)
    behind = pltpu.roll(x, ROT // 2, 1)
    return x * cos_tab + ahead * minus + behind * plus


def head_lanes(x, head):
    lane = lax.broadcasted_iota(jnp.int32, x.shape, 1)
    return jnp.where((lane < HD) == (head == 0), x, jnp.zeros_like(x))


def transposed(x):
    return x.astype(jnp.float32).T.astype(x.dtype)


def causal_exp(scores, row_block, block):
    e = jnp.exp(scores)
    if row_block:
        done = e[: row_block * block]
    last = e[row_block * block :]
    key = lax.broadcasted_iota(jnp.int32, last.shape, 0)
    query = lax.broadcasted_iota(jnp.int32, last.shape, 1)
    last = jnp.where(key <= query, last, 0.0)
    return jnp.concatenate([done, last], axis=0) if row_block else last


def attend_kernel(block, mq, mk, mv, cos_ref, minus_ref, plus_ref, q_out, k_out, v_out, o_out):
    shape = q_out.shape
    length = shape[0] * shape[2]
    tabs = (cos_ref[...], minus_ref[...], plus_ref[...])
    q = rotate(mq[...].reshape(length, PAIR), *tabs).astype(jnp.bfloat16)
    k = rotate(mk[...].reshape(length, PAIR), *tabs).astype(jnp.bfloat16)
    v = mv[...].reshape(length, PAIR).astype(jnp.bfloat16)
    q_out[...] = q.reshape(shape)
    k_out[...] = k.reshape(shape)
    v_out[...] = v.reshape(shape)
    qs = q * jnp.bfloat16(HD**-0.5)
    vt = transposed(v)
    q_heads = [head_lanes(qs, h) for h in range(2)]
    rows = []
    for i in range(length // block):
        n = (i + 1) * block
        both = []
        for h in range(2):
            e = causal_exp(nt(k[:n], q_heads[h][i * block : n]), i, block)
            inv = 1.0 / jnp.sum(e, axis=0, keepdims=True)
            p = (e * inv).astype(jnp.bfloat16)
            both.append(nn(vt[h * HD : (h + 1) * HD, :n], p))
        rows.append(jnp.concatenate(both, axis=0).T)
    o_out[...] = jnp.concatenate(rows, axis=0).astype(jnp.bfloat16).reshape(shape)


def attend_back_kernel(block, q_ref, k_ref, v_ref, do_ref, cos_ref, minus_ref, plus_ref,
                       dq_out, dk_out, dv_out, dk_acc, dv_acc):
    shape = dq_out.shape
    length = shape[0] * shape[2]
    tabs = (cos_ref[...], -minus_ref[...], -plus_ref[...])
    scale = HD**-0.5
    q = q_ref[...].reshape(length, PAIR) * jnp.bfloat16(scale)
    k = k_ref[...].reshape(length, PAIR)
    v = v_ref[...].reshape(length, PAIR)
    do = do_ref[...].reshape(length, PAIR)
    kt = transposed(k)
    q_heads = [head_lanes(q, h) for h in range(2)]
    do_heads = [head_lanes(do, h) for h in range(2)]
    dk_acc[...] = jnp.zeros_like(dk_acc)
    dv_acc[...] = jnp.zeros_like(dv_acc)
    rows = []
    for i in range(length // block):
        n = (i + 1) * block
        both = []
        for h in range(2):
            q_i = q_heads[h][i * block : n]
            do_i = do_heads[h][i * block : n]
            e = causal_exp(nt(k[:n], q_i), i, block)
            p = e * (1.0 / jnp.sum(e, axis=0, keepdims=True))
            dp = nt(v[:n], do_i)
            inner = jnp.sum(p * dp, axis=0, keepdims=True)
            ds = (p * (dp - inner)).astype(jnp.bfloat16)
            dv_acc[:n] += nn(p.astype(jnp.bfloat16), do_i)
            dk_acc[:n] += nn(ds, q_i)
            both.append(nn(kt[h * HD : (h + 1) * HD, :n], ds))
        rows.append(jnp.concatenate(both, axis=0).T)
    def finish(g):
        return g.astype(jnp.bfloat16).astype(jnp.float32)

    dq = finish(jnp.concatenate(rows, axis=0) * scale)
    dq_out[...] = rotate(dq, *tabs).astype(jnp.bfloat16).reshape(shape)
    dk_out[...] = rotate(finish(dk_acc[...]), *tabs).astype(jnp.bfloat16).reshape(shape)
    dv_out[...] = dv_acc[...].astype(jnp.bfloat16).reshape(shape)


def attention_specs(parts, seqs, local_len, width):
    pairs = width // PAIR

    def spec(offset):
        return pl.BlockSpec((parts, 1, local_len, PAIR), lambda i, j: (0, i, 0, offset * pairs + j))

    length = parts * local_len
    tab = pl.BlockSpec((length, PAIR), lambda i, j: (0, 0))
    return spec, tab, (seqs, pairs), min(256, length)


def attend(m, tabs, width):
    parts, seqs, local_len, _ = m.shape
    spec, tab, grid, block = attention_specs(parts, seqs, local_len, width)
    out = jax.ShapeDtypeStruct((parts, seqs, local_len, width), jnp.bfloat16)
    work = seqs * (width // HD) * (parts * local_len) ** 2
    return pl.pallas_call(
        functools.partial(attend_kernel, block),
        grid=grid,
        in_specs=[spec(0), spec(1), spec(2), tab, tab, tab],
        out_specs=[spec(0)] * 4,
        out_shape=[out] * 4,
        compiler_params=pltpu.CompilerParams(vmem_limit_bytes=48 << 20),
        cost_estimate=pl.CostEstimate(
            flops=work * HD * 4, bytes_accessed=m.size * 4 + out.size * 8, transcendentals=work
        ),
        name="attend",
    )(m, m, m, *tabs)


def attend_back(q, k, v, do, tabs):
    parts, seqs, local_len, width = q.shape
    spec, tab, grid, block = attention_specs(parts, seqs, local_len, width)
    out = jax.ShapeDtypeStruct(q.shape, jnp.bfloat16)
    length = parts * local_len
    work = seqs * (width // HD) * length**2
    return pl.pallas_call(
        functools.partial(attend_back_kernel, block),
        grid=grid,
        in_specs=[spec(0)] * 4 + [tab] * 3,
        out_specs=[spec(0)] * 3,
        out_shape=[out] * 3,
        scratch_shapes=[pltpu.VMEM((length, PAIR), jnp.float32)] * 2,
        compiler_params=pltpu.CompilerParams(vmem_limit_bytes=48 << 20),
        cost_estimate=pl.CostEstimate(
            flops=work * HD * 10, bytes_accessed=out.size * 14, transcendentals=work
        ),
        name="attend_back",
    )(q, k, v, do, *tabs)


def third_rounds(parts):
    left = {s: [(j, (j * parts + s) // 3, (j * parts + s) % 3) for j in range(3)] for s in range(parts)}
    rounds = []
    for _ in range(3):
        owner = {}

        def place(s, seen):
            for edge in left[s]:
                d = edge[1]
                if d in seen:
                    continue
                seen.add(d)
                if d not in owner or place(owner[d][0], seen):
                    owner[d] = (s, edge)
                    return True
            return False

        for s in range(parts):
            place(s, set())
        send = [0] * parts
        slot = [0] * parts
        pairs = []
        for d, (s, edge) in owner.items():
            left[s].remove(edge)
            send[s] = edge[0]
            slot[d] = edge[2]
            pairs.append((s, d))
        rounds.append((sorted(pairs), send, slot))
    return rounds


def contiguous_thirds(block, parts, me):
    rows, _, width = block.shape
    got = []
    slots = []
    for pairs, send, slot in third_rounds(parts):
        piece = lax.dynamic_index_in_dim(block, jnp.array(send)[me], 1, keepdims=False)
        got.append(lax.ppermute(piece, "seq", pairs))
        slots.append(jnp.array(slot)[me])
    out = []
    for k in range(3):
        out.append(jnp.where(slots[0] == k, got[0], jnp.where(slots[1] == k, got[1], got[2])))
    return jnp.concatenate(out, axis=1)


def swap_blocks(block, seq_parts, fsdp_parts, me_seq):
    ratio = seq_parts // fsdp_parts
    got = []
    for r in range(ratio):
        pairs = []
        for s in range(seq_parts):
            for f in range(fsdp_parts):
                h = (r + s) % ratio
                dest = (ratio * f + h, s // ratio)
                pairs.append((s * fsdp_parts + f, dest[0] * fsdp_parts + dest[1]))
        piece = lax.dynamic_index_in_dim(block, (r + me_seq) % ratio, 1, keepdims=False)
        got.append(lax.ppermute(piece, MESH_AXES, pairs))
    out = []
    for b in range(ratio):
        r_of_b = (me_seq - b) % ratio
        pick = got[0]
        for r in range(1, ratio):
            pick = jnp.where(r_of_b == r, got[r], pick)
        out.append(pick)
    return jnp.concatenate(out, axis=0)


def on_device(
    tokens,
    attn_gain,
    attn_shift,
    qkv_weight,
    qkv_bias,
    out_weight,
    ffn_gain,
    ffn_shift,
    gate_weight,
    up_weight,
    down_weight,
    cotangent,
):
    f32, bf16 = jnp.float32, jnp.bfloat16
    seqs, local_len, width = tokens.shape
    S = lax.axis_size("seq")
    F = lax.axis_size("fsdp")
    me = lax.axis_index("seq")
    devices = S * F
    rows = seqs * local_len
    all_rows = S * rows
    head_width = width // S
    ff_rows, _ = down_weight.shape
    shard = width // F

    small = jnp.concatenate([attn_gain, attn_shift, ffn_gain, ffn_shift, qkv_bias])
    small = lax.all_gather(small, "fsdp", axis=0)
    params = [small[:, i * shard : (i + 1) * shard].reshape(width).astype(f32) for i in range(4)]
    gain1, shift1, gain2, shift2 = params
    bias = small[:, 4 * shard :].reshape(3, S, head_width).astype(f32)
    bias = lax.dynamic_index_in_dim(bias, me, 1, keepdims=False).reshape(3 * head_width)

    x_all = lax.all_gather(tokens, "seq", axis=0).reshape(all_rows, width)
    qkv_part = lax.dynamic_index_in_dim(
        qkv_weight.reshape(shard, 3, S, head_width), me, 2, keepdims=False
    ).reshape(shard, 3 * head_width)
    w_qkv = lax.all_gather(qkv_part, "fsdp", axis=0, tiled=True)
    w_out = lax.all_gather(out_weight, "fsdp", axis=0, tiled=True)
    dy_all = lax.all_gather(cotangent.reshape(rows, width), "fsdp", axis=0, tiled=True)
    w_gate = lax.all_to_all(gate_weight, "fsdp", split_axis=1, concat_axis=0, tiled=True)
    w_up = lax.all_to_all(up_weight, "fsdp", split_axis=1, concat_axis=0, tiled=True)

    tabs = rotary_tables(S * local_len)
    xh_all, _ = norm_stats(x_all.astype(f32))
    a1 = (xh_all * gain1 + shift1).astype(bf16)
    m = nn(a1, w_qkv) + bias
    q, k, v, o = attend(m.reshape(S, seqs, local_len, 3 * head_width), tabs, head_width)
    o_loc = lax.all_to_all(o, "seq", split_axis=0, concat_axis=0, tiled=True)
    o_loc = o_loc.transpose(1, 2, 0, 3).reshape(rows, width)

    x = tokens.reshape(rows, width).astype(f32)
    x1 = x + nn(o_loc, w_out)
    xh2, r2 = norm_stats(x1)
    a2 = (xh2 * gain2 + shift2).astype(bf16)
    a2_all = lax.all_gather(a2, "fsdp", axis=0, tiled=True)

    g = nn(a2_all, w_gate)
    u = nn(a2_all, w_up)
    dh = nt(dy_all, down_weight)
    sig = jax.nn.sigmoid(g)
    silu = g * sig
    hid = (silu * u).astype(bf16)
    dg = (dh * u * sig * (1.0 + g * (1.0 - sig))).astype(bf16)
    du = (dh * silu).astype(bf16)
    dn2_part = (nt(dg, w_gate) + nt(du, w_up)).astype(bf16)
    dn2 = lax.psum_scatter(dn2_part, "fsdp", scatter_dimension=0, tiled=True).astype(f32)
    down_part = nn(hid, down_weight).astype(bf16)
    down_sum = lax.psum_scatter(down_part, "fsdp", scatter_dimension=0, tiled=True)
    layer_out = (x1 + down_sum.astype(f32)).astype(bf16).reshape(tokens.shape)

    dy = cotangent.reshape(rows, width).astype(f32)
    dx1 = dy + norm_back(dn2, xh2, r2, gain2)
    ffn_gain_part = jnp.sum(dn2 * xh2, axis=0)
    ffn_shift_part = jnp.sum(dn2, axis=0)
    dxl = dx1.astype(bf16)
    do_loc = nt(dxl, w_out).astype(bf16)
    do = lax.all_to_all(
        do_loc.reshape(seqs, local_len, S, head_width).transpose(2, 0, 1, 3),
        "seq",
        split_axis=0,
        concat_axis=0,
        tiled=True,
    )

    gate_part = tn(a2_all, dg).astype(bf16)
    up_part = tn(a2_all, du).astype(bf16)
    down_grad_part = tn(hid, dy_all).astype(bf16)
    ratio = S // F
    ff_block = ff_rows // ratio

    def ffn_grad(part):
        part = lax.psum_scatter(part, "seq", scatter_dimension=0, tiled=True)
        return swap_blocks(part.reshape(-1, ratio, ff_block), S, F, me).astype(f32)

    gate_result = ffn_grad(gate_part)
    up_result = ffn_grad(up_part)
    down_result = lax.psum_scatter(
        down_grad_part, "seq", scatter_dimension=1, tiled=True
    ).astype(f32)
    out_part = tn(o_loc, dxl).astype(bf16)
    out_part = lax.psum_scatter(out_part, "seq", scatter_dimension=1, tiled=True)
    out_result = lax.psum_scatter(out_part, "fsdp", scatter_dimension=0, tiled=True).astype(f32)

    dq, dk, dv = attend_back(q, k, v, do, tabs)
    dm = jnp.concatenate([dq, dk, dv], axis=-1).reshape(all_rows, 3 * head_width)
    dn1_part = nt(dm, w_qkv).astype(bf16)
    dn1 = lax.psum_scatter(dn1_part, "seq", scatter_dimension=0, tiled=True).astype(f32)
    qkv_part_grad = tn(a1, dm).astype(bf16)
    qkv_sum = lax.psum_scatter(qkv_part_grad, "fsdp", scatter_dimension=0, tiled=True)
    qkv_result = contiguous_thirds(qkv_sum.reshape(shard, 3, head_width), S, me).astype(f32)

    bias_part = jnp.sum(dm, axis=0, dtype=f32).reshape(3, 1, head_width)
    bias_full = lax.dynamic_update_slice_in_dim(
        jnp.zeros((3, S, head_width), f32), bias_part, me, 1
    ).reshape(3 * width)
    attn_gain_part = jnp.sum(dn1_part.astype(f32) * xh_all, axis=0)
    attn_shift_part = jnp.sum(dn1_part.astype(f32), axis=0)
    small_parts = [
        attn_gain_part,
        attn_shift_part,
        bias_full[: 2 * width],
        bias_full[2 * width :],
        ffn_gain_part,
        ffn_shift_part,
    ]
    packed = jnp.concatenate([p.reshape(devices, -1) for p in small_parts], axis=1)
    packed = lax.all_to_all(packed, MESH_AXES, split_axis=0, concat_axis=0, tiled=True)
    packed = jnp.sum(packed, axis=0)
    results = []
    start = 0
    for p in small_parts:
        size = p.shape[0] // devices
        results.append(packed[start : start + size])
        start += size
    gain1_result, shift1_result, bias_result, value_result, gain2_result, shift2_result = results

    xh, r = norm_stats(x)
    tokens_grad = (dx1 + norm_back(dn1, xh, r, gain1)).reshape(tokens.shape)
    return (
        layer_out,
        tokens_grad,
        gain1_result,
        shift1_result,
        qkv_result,
        bias_result,
        value_result,
        out_result,
        gain2_result,
        shift2_result,
        gate_result,
        up_result,
        down_result,
    )


def solution(mesh):
    return jax.shard_map(
        on_device,
        mesh=mesh,
        in_specs=(
            P("fsdp", "seq", None),
            P("fsdp"),
            P("fsdp"),
            P("fsdp", None),
            P("fsdp"),
            P("fsdp", None),
            P("fsdp"),
            P("fsdp"),
            P("fsdp", None),
            P("fsdp", None),
            P("fsdp", None),
            P("fsdp", "seq", None),
        ),
        out_specs=(
            P("fsdp", "seq", None),
            P("fsdp", "seq", None),
            P(("seq", "fsdp")),
            P(("seq", "fsdp")),
            P("fsdp", "seq"),
            P(("seq", "fsdp")),
            P(("seq", "fsdp")),
            P("fsdp", "seq"),
            P(("seq", "fsdp")),
            P(("seq", "fsdp")),
            P("fsdp", "seq"),
            P("fsdp", "seq"),
            P("fsdp", "seq"),
        ),
        check_vma=False,
    )
```

time: 2510 us -> 1190 us (0.47)
  waiting for transfers between devices: 1920 us -> 688 us
  matrix products: 280 us -> 158 us
  Pallas kernels: 0 us -> 42.6 us
  starting transfers between devices: 18.3 us -> 56.6 us
  other arithmetic: 84.3 us -> 54.4 us
    all_gather x5, waiting for transfers between devices: 679 us -> 172 us  [the longest x1 67.6 us: on_device(): w_out = lax.all_gather(out_weight, 'fsdp', axis=0, tiled=True)]
    reduce_scatter x10 -> x9, waiting for transfers between devices: 870 us -> 403 us  [the longest x1 89.4 us: on_device(): lax.psum_scatter(out_part, 'seq', scatter_dimension=1, tiled=True)]
    all_to_all x4, waiting for transfers between devices: 248 us -> 99.1 us  [the longest x1 81 us: on_device(): lax.all_to_all(up_weight, 'fsdp', split_axis=1, concat_axis=0, tiled=True)]
    dot_general x29 -> x15, matrix products: 280 us -> 158 us  [the longest x5 57.8 us: nt(): lax.dot_general(a, b, (((1,), (1,)), ((), ())), preferred_element_type=jn...]
    unnamed x25 -> x14, waiting for transfers between devices: 119 us -> 2.07 us
    all_to_all x0 -> x1, blocking collectives: none -> 48.1 us  [on_device(): lax.all_to_all(do_loc.reshape(seqs, local_len, S, head_width).transpose(2...]
    pallas_call x0 -> x2, Pallas kernels: none -> 42.6 us  [the longest x1 24.5 us: attend_back(): pl.pallas_call(functools.partial(attend_back_kernel, block), grid=grid, i...]
    ppermute x0 -> x7, starting transfers between devices: none -> 37.7 us  [the longest x4 30.9 us: swap_blocks(): got.append(lax.ppermute(piece, MESH_AXES, pairs))]
  transfers between devices with their start and end apart: 24 -> 25, of which waited for: 21 -> 15; matrix products, arithmetic and copies ran while one was open for 16% -> 22% of each run, Pallas kernels for 0% -> 4%
where the time goes in v1:
time: 1190 us; the launch traced here: 1180 us
  waiting for transfers between devices  688 us (58%)
  matrix products  158 us (13%)
  local copies, waits for them, and re-layouts  94.6 us (8%)
  blocking collectives  58 us (5%)
  starting transfers between devices  56.6 us (5%)
  other arithmetic  54.4 us (5%)
  Pallas kernels  42.6 us (4%)
  between operations  24.6 us (2%)
    reduce_scatter x1, waiting for transfers between devices, on_device(): lax.psum_scatter(out_part, 'seq', scatter_dimension=1, tiled=True)  89.4 us
    all_to_all x1, waiting for transfers between devices, on_device(): lax.all_to_all(up_weight, 'fsdp', split_axis=1, concat_axis=0, tiled=True)  81 us
    all_gather x1, waiting for transfers between devices, on_device(): w_out = lax.all_gather(out_weight, 'fsdp', axis=0, tiled=True)  67.6 us
    reduce_scatter x1, waiting for transfers between devices, on_device(): lax.psum_scatter(dn1_part, 'seq', scatter_dimension=0, tiled=True)  65.9 us
    all_gather x1, waiting for transfers between devices, on_device(): x_all = lax.all_gather(tokens, 'seq', axis=0).reshape(all_rows, width)  63 us
    reduce_scatter x1, waiting for transfers between devices, on_device(): lax.psum_scatter(down_grad_part, 'seq', scatter_dimension=1, tiled=True)  60 us
    dot_general x5, matrix products, nt(): lax.dot_general(a, b, (((1,), (1,)), ((), ())), preferred_element_type=jn...  57.8 us
    reduce_scatter x2, waiting for transfers between devices, ffn_grad(): part = lax.psum_scatter(part, 'seq', scatter_dimension=0, tiled=True)  57.4 us
  transfers between devices with their start and end apart: 25, of which 15 were waited for; matrix products, arithmetic and copies ran while one was open for 22% of the time, Pallas kernels for 4%

profile of v1, /device:TPU:0, one launch (start us, length us, event | category | flops | bytes accessed | tf_op | source)
XLA Modules:
  0.0 1176.1 jit_solution(15740390427132755428)
XLA Ops:
  20.5 9.8 all-gather.2
  31.4 63.0 %all-gather.17.cloned.1.call-done = bf16[16,128,2048]{2,1,0:T(8,128)(2,1)} async-done(((bf16[2,128,2048]{2,1,0:T(8,128)(2,1)}), bf16[16,128,2048]{2,1,0:T(8,128)(2,1)}) %all-gather.17.cloned.1.call-update) | async-done | bytes 8388624 | tf_op jit(solution)/shard_map/all_gather | solution.py:306
  94.4 12.7 %copy.64 = f32[8,2,128,2048]{2,3,1,0:T(8,128)} copy(bf16[8,2,128,2048]{3,2,1,0:T(8,128)(2,1)} %bitcast.124) | data formatting | bytes 25165824 | tf_op jit(solution)/shard_map/convert_element_type | solution.py:317
  119.2 8.7 add_convert_fusion.1
  127.9 11.1 all-gather.9.cloned.1.call-done
  139.0 11.7 broadcast_add_fusion
  150.7 18.1 %attend.1 = (bf16[8,2,128,256]{3,2,1,0:T(8,128)(2,1)S(1)}, bf16[8,2,128,256]{3,2,1,0:T(8,128)(2,1)S(1)}, bf16[8,2,128,256]{3,2,1,0:T(8,128)(2,1)S(1)}, bf16[8,2,128,256]{3,2,1,0:T(8,128)(2,1)}) custom-call(f32[8,2,128,768]{3,2,1,0:T(8,128)} %bitcast.125, f32[8,2,128,768]{3,2,1,0:T(8,128)} %bitcast.126, f32[8,2,128,768]{3,2,1,0:T(8,128)} %bitcast.127, ...), custom_call_target="tpu_custom_call" | custom-call | flops 2147483648 | bytes 10485760 | tf_op jit(solution)/shard_map/attend/pallas_call | solution.py:171
  183.8 18.0 %all-to-all-done = bf16[8,2,128,256]{3,2,1,0:T(8,128)(2,1)} async-done(((bf16[8,2,128,256]{3,2,1,0:T(8,128)(2,1)}), bf16[8,2,128,256]{3,2,1,0:T(8,128)(2,1)}, u32[]{:S(2)}, u32[]{:S(2)}) %all-to-all-start) | async-done | bytes 1048608 | tf_op jit(solution)/shard_map/all_to_all | solution.py:321
  210.3 67.6 %all-gather.11.cloned.1.call-done = bf16[2048,2048]{1,0:T(8,128)(2,1)} async-done(((bf16[512,2048]{1,0:T(8,128)(2,1)}), bf16[2048,2048]{1,0:T(8,128)(2,1)}) %all-gather.11.cloned.1.call-update) | async-done | bytes 8388624 | tf_op jit(solution)/shard_map/all_gather | solution.py:311
  309.6 81.0 %all-to-all-done.2 = bf16[512,4,1408]{0,2,1:T(8,128)(2,1)} async-done(((bf16[512,4,1408]{0,2,1:T(8,128)(2,1)}), bf16[512,4,1408]{0,2,1:T(8,128)(2,1)}, u32[]{:S(2)}, u32[]{:S(2)}) %all-to-all-start.2) | async-done | bytes 5767200 | tf_op jit(solution)/shard_map/all_to_all | solution.py:314
  398.9 11.8 %fusion.27 = f32[1024,1408]{1,0:T(8,128)} fusion(bf16[1024,2048]{1,0:T(8,128)(2,1)} %all-gather.13.cloned.1.call-done, bf16[2048,1408]{1,0:T(8,128)(2,1)} %bitcast.134), kind=kOutput, calls=%fused_computation.113 | convolution fusion | flops 5905580032 | bytes 15728640 | tf_op jit(solution)/shard_map/dot_general | solution.py:19
  419.2 30.4 %all-gather.15.cloned.1.call-done = bf16[1024,2048]{1,0:T(8,128)(2,1)} async-done(((bf16[256,2048]{1,0:T(8,128)(2,1)}), bf16[1024,2048]{1,0:T(8,128)(2,1)}) %all-gather.15.cloned.1.call-update) | async-done | bytes 4194320 | tf_op jit(solution)/shard_map/all_gather | solution.py:312
  449.5 15.6 %multiply_convert_fusion = (bf16[1024,1408]{1,0:T(8,128)(2,1)S(1)}, bf16[1024,1408]{1,0:T(8,128)(2,1)S(1)}, bf16[1024,1408]{1,0:T(8,128)(2,1)}) fusion(f32[1024,1408]{1,0:T(8,128)} %fusion.27, f32[1024,1408]{1,0:T(8,128)} %fusion.28, bf16[1024,2048]{1,0:T(8,128)(2,1)} %all-gather.15.cloned.1.call-done, bf16[1408,2048]{1,0:T(8,128)(2,1)} %param.27), kind=kOutput, calls=%fused_computation.22 | convolution fusion | flops 5927206912 | bytes 30146560 | tf_op jit(solution)/shard_map/dot_general | solution.py:23
  465.1 10.8 fusion.29
  476.0 11.2 add_convert_fusion.3
  487.3 11.0 convolution_convert_fusion.5
  498.3 11.1 convolution_convert_fusion.1
  509.5 11.0 convolution_convert_fusion.2
  520.6 10.9 convolution_convert_fusion
  542.9 52.7 %reduce-scatter.10.cloned.1.call-done = bf16[256,2048]{1,0:T(8,128)(2,1)} async-done(((bf16[1024,2048]{1,0:T(8,128)(2,1)}), bf16[256,2048]{1,0:T(8,128)(2,1)}) %reduce-scatter.10.cloned.1.call-update) | async-done | bytes 1048592 | tf_op jit(solution)/shard_map/reduce_scatter | solution.py:341
  607.4 48.1 %all_to_all.57.do_ref = bf16[8,2,128,256]{3,2,1,0:T(8,128)(2,1)} all-to-all(bf16[8,2,128,256]{3,2,1,0:T(8,128)(2,1)S(1)} %bitcast.142), channel_id=1, replica_groups=mesh['seq'=8,'fsdp'=4] {'seq'}, dimensions={0} | all-to-all | bytes 2097152 | tf_op jit(solution)/shard_map/all_to_all | solution.py:350
  655.6 24.5 %attend_back.1 = (bf16[8,2,128,256]{3,2,1,0:T(8,128)(2,1)S(1)}, bf16[8,2,128,256]{3,2,1,0:T(8,128)(2,1)S(1)}, bf16[8,2,128,256]{3,2,1,0:T(8,128)(2,1)S(1)}) custom-call(bf16[8,2,128,256]{3,2,1,0:T(8,128)(2,1)S(1)} %get-tuple-element.21.q_ref, bf16[8,2,128,256]{3,2,1,0:T(8,128)(2,1)} %copy-done, bf16[8,2,128,256]{3,2,1,0:T(8,128)(2,1)} %copy-done.1, ...), custom_call_target="tpu_custom_call" | custom-call | flops 5368709120 | bytes 7340032 | tf_op jit(solution)/shard_map/attend_back/pallas_call | solution.py:191
  682.1 11.9 %bitcast_convert_fusion = bf16[2048,768]{1,0:T(8,128)(2,1)} fusion(bf16[8,2,128,768]{3,2,1,0:T(8,128)(2,1)S(1)} %constant_dynamic-update-slice_fusion, f32[8,2,128,2048]{2,3,1,0:T(8,128)} %copy.64, f32[2048]{0:T(1024)S(1)} %bitcast.165, f32[2048]{0:T(1024)S(1)} %bitcast.154, f32[8,2,128]{2,1,0:T(2,128)S(1)} %copy-done.19, f32[8,2,128]{2,1,0:T(2,128)S(1)} %bitcast.163), kind=kOutput, calls=%fused_computation.20 | convolution fusion | flops 6464995328 | bytes 23101440 | tf_op jit(solution)/shard_map/dot_general | solution.py:27
  702.0 13.4 %convert_reduce_fusion = (f32[2048]{0:T(1024)S(1)}, f32[2048]{0:T(1024)S(1)}, bf16[2048,2048]{1,0:T(8,128)(2,1)}) fusion(f32[2048]{0:T(1024)S(1)} %bitcast.167, f32[2048]{0:T(1024)S(1)} %copy-done.15, bf16[16,128,2048]{2,1,0:T(8,128)(2,1)} %all-gather.17.cloned.1.call-done, bf16[2048,768]{1,0:T(8,128)(2,1)} %bitcast.138, ...), kind=kOutput, calls=%fused_computation | convolution fusion | flops 6476001280 | bytes 23101440 | tf_op jit(solution)/shard_map/dot_general | solution.py:23
  746.7 57.4 %reduce-scatter.22.cloned.1.call-done = bf16[256,1408]{1,0:T(8,128)(2,1)} async-done(((bf16[2048,1408]{1,0:T(8,128)(2,1)}), bf16[256,1408]{1,0:T(8,128)(2,1)}) %reduce-scatter.22.cloned.1.call-update) | async-done | bytes 720912 | tf_op jit(solution)/shard_map/reduce_scatter | solution.py:365
  808.3 22.1 %collective-permute-start.3 = (bf16[256,704]{0,1:T(8,128)(2,1)}, bf16[256,704]{0,1:T(8,128)(2,1)}, u32[]{:S(2)}, u32[]{:S(2)}) collective-permute-start(bf16[256,704]{0,1:T(8,128)(2,1)} %get-tuple-element.53), channel_id=1, source_target_pairs={{0,4},{1,12},{2,20},{3,28},{4,0},{5,8},{6,16},{7,24},{8,5},{9,13},... | collective-permute-start | bytes 1081352 | tf_op jit(solution)/shard_map/ppermute | solution.py:262
  835.8 60.0 %reduce-scatter.26.cloned.1.call-done = bf16[1408,256]{1,0:T(8,128)(2,1)} async-done(((bf16[1408,2048]{1,0:T(8,128)(2,1)}), bf16[1408,256]{1,0:T(8,128)(2,1)}) %reduce-scatter.26.cloned.1.call-update) | async-done | bytes 720912 | tf_op jit(solution)/shard_map/reduce_scatter | solution.py:370
  902.7 43.0 %reduce-scatter.16.cloned.1.call-done = bf16[512,768]{1,0:T(8,128)(2,1)} async-done(((bf16[2048,768]{1,0:T(8,128)(2,1)}), bf16[512,768]{1,0:T(8,128)(2,1)}) %reduce-scatter.16.cloned.1.call-update) | async-done | bytes 786448 | tf_op jit(solution)/shard_map/reduce_scatter | solution.py:382
  948.0 89.4 %reduce-scatter.18.cloned.1.call-done = bf16[2048,256]{1,0:T(8,128)(2,1)} async-done(((bf16[2048,2048]{1,0:T(8,128)(2,1)}), bf16[2048,256]{1,0:T(8,128)(2,1)}) %reduce-scatter.18.cloned.1.call-update) | async-done | bytes 1048592 | tf_op jit(solution)/shard_map/reduce_scatter | solution.py:374
  1056.4 11.9 %collective-permute-done.1 = bf16[512,256]{1,0:T(8,128)(2,1)} collective-permute-done((bf16[512,256]{1,0:T(8,128)(2,1)}, bf16[512,256]{1,0:T(8,128)(2,1)}, u32[]{:S(2)}, u32[]{:S(2)}) %collective-permute-start.1) | collective-permute-done | bytes 262176 | tf_op jit(solution)/shard_map/ppermute | solution.py:243
  1070.7 65.9 %reduce-scatter.14.cloned.1.call-done = bf16[256,2048]{1,0:T(8,128)(2,1)} async-done(((bf16[2048,2048]{1,0:T(8,128)(2,1)}), bf16[256,2048]{1,0:T(8,128)(2,1)}) %reduce-scatter.14.cloned.1.call-update) | async-done | bytes 1048592 | tf_op jit(solution)/shard_map/reduce_scatter | solution.py:380
  1141.8 25.7 %reduce-scatter.20.cloned.1.call-done = bf16[512,256]{1,0:T(8,128)(2,1)} async-done(((bf16[2048,256]{1,0:T(8,128)(2,1)}), bf16[512,256]{1,0:T(8,128)(2,1)}) %reduce-scatter.20.cloned.1.call-update) | async-done | bytes 262160 | tf_op jit(solution)/shard_map/reduce_scatter | solution.py:375
  (217 shorter events, 199.9 us)
Async XLA Ops:
  7.2 87.2 %all-gather.17.cloned.1.call-start = ((), (), s32[]{:S(2)}) async-start(), calls=%async_computation.27 | async-start | bytes 9437184 | tf_op jit(solution)/shard_map/all_gather | solution.py:306
  7.9 131.1 %all-gather.9.cloned.1.call-start = ((), (), s32[]{:S(2)}) async-start(), calls=%async_computation.14 | async-start | bytes 3932160 | tf_op jit(solution)/shard_map/all_gather | solution.py:310
  18.8 259.1 %all-gather.11.cloned.1.call-start = ((), (), s32[]{:S(2)}) async-start(), calls=%async_computation.15 | async-start | bytes 10485760 | tf_op jit(solution)/shard_map/all_gather | solution.py:311
  30.4 88.8 %copy-start.10 = (f32[1,4,4,128]{3,1,2,0:T(4,128)}, f32[1,4,4,128]{3,1,2,0:T(4,128)S(1)}, u32[]{:S(2)}) copy-start(f32[1,4,4,128]{3,1,2,0:T(4,128)S(1)} %copy.83) | copy-start | bytes 24580
  30.4 88.8 %copy-start.16 = (f32[1,4,4,128]{3,1,2,0:T(4,128)}, f32[1,4,4,128]{3,1,2,0:T(4,128)S(1)}, u32[]{:S(2)}) copy-start(f32[1,4,4,128]{3,1,2,0:T(4,128)S(1)} %copy.84) | copy-start | bytes 24580
  170.7 31.1 %all-to-all-start = ((bf16[8,2,128,256]{3,2,1,0:T(8,128)(2,1)}), bf16[8,2,128,256]{3,2,1,0:T(8,128)(2,1)}, u32[]{:S(2)}, u32[]{:S(2)}) async-start(bf16[8,2,128,256]{3,2,1,0:T(8,128)(2,1)} %get-tuple-element.20), calls=%async_computation | async-start | bytes 2097152 | tf_op jit(solution)/shard_map/all_to_all | solution.py:321
  201.8 93.5 %all-to-all-start.1 = ((bf16[512,4,1408]{0,2,1:T(8,128)(2,1)}), bf16[512,4,1408]{0,2,1:T(8,128)(2,1)}, u32[]{:S(2)}, u32[]{:S(2)}) async-start(bf16[512,4,1408]{0,2,1:T(8,128)(2,1)} %bitcast.129), calls=%async_computation.1 | async-start | bytes 11534336 | tf_op jit(solution)/shard_map/all_to_all | solution.py:313
  207.0 191.9 %all-gather.13.cloned.1.call-start = ((), (), s32[]{:S(2)}) async-start(), calls=%async_computation.16 | async-start | bytes 5242880 | tf_op jit(solution)/shard_map/all_gather | solution.py:328
  295.3 95.3 %all-to-all-start.2 = ((bf16[512,4,1408]{0,2,1:T(8,128)(2,1)}), bf16[512,4,1408]{0,2,1:T(8,128)(2,1)}, u32[]{:S(2)}, u32[]{:S(2)}) async-start(bf16[512,4,1408]{0,2,1:T(8,128)(2,1)} %bitcast.130), calls=%async_computation.2 | async-start | bytes 11534336 | tf_op jit(solution)/shard_map/all_to_all | solution.py:314
  300.6 148.9 %all-gather.15.cloned.1.call-start = ((), (), s32[]{:S(2)}) async-start(), calls=%async_computation.18 | async-start | bytes 5242880 | tf_op jit(solution)/shard_map/all_gather | solution.py:312
  301.2 238.8 %reduce-scatter.12.cloned.1.call-start = ((), (), s32[]{:S(2)}) async-start(), calls=%async_computation.19 | async-start | bytes 5242880 | tf_op jit(solution)/shard_map/reduce_scatter | solution.py:339
  487.2 108.4 %reduce-scatter.10.cloned.1.call-start = ((), (), s32[]{:S(2)}) async-start(), calls=%async_computation.17 | async-start | bytes 5242880 | tf_op jit(solution)/shard_map/reduce_scatter | solution.py:341
  498.3 226.0 %reduce-scatter.24.cloned.1.call-start = ((), (), s32[]{:S(2)}) async-start(), calls=%async_computation.25 | async-start | bytes 6488064 | tf_op jit(solution)/shard_map/reduce_scatter | solution.py:365
  509.4 294.6 %reduce-scatter.22.cloned.1.call-start = ((), (), s32[]{:S(2)}) async-start(), calls=%async_computation.24 | async-start | bytes 6488064 | tf_op jit(solution)/shard_map/reduce_scatter | solution.py:365
  520.5 375.3 %reduce-scatter.26.cloned.1.call-start = ((), (), s32[]{:S(2)}) async-start(), calls=%async_computation.26 | async-start | bytes 6488064 | tf_op jit(solution)/shard_map/reduce_scatter | solution.py:370
  531.5 414.2 %reduce-scatter.16.cloned.1.call-start = ((), (), s32[]{:S(2)}) async-start(), calls=%async_computation.21 | async-start | bytes 3932160 | tf_op jit(solution)/shard_map/reduce_scatter | solution.py:382
  694.0 343.4 %reduce-scatter.18.cloned.1.call-start = ((), (), s32[]{:S(2)}) async-start(), calls=%async_computation.22 | async-start | bytes 9437184 | tf_op jit(solution)/shard_map/reduce_scatter | solution.py:374
  701.3 435.3 %reduce-scatter.14.cloned.1.call-start = ((), (), s32[]{:S(2)}) async-start(), calls=%async_computation.20 | async-start | bytes 9437184 | tf_op jit(solution)/shard_map/reduce_scatter | solution.py:380
  716.6 16.4 %copy-start.30 = (s32[8]{0:T(128)S(1)}, s32[8]{0:T(128)}, u32[]{:S(2)}) copy-start(s32[8]{0:T(128)} %constant.136.clone) | copy-start | bytes 100
  716.6 18.3 %copy-start.29 = (s32[8]{0:T(128)S(1)}, s32[8]{0:T(128)}, u32[]{:S(2)}) copy-start(s32[8]{0:T(128)} %constant.138.clone) | copy-start | bytes 100
  716.6 20.2 %copy-start.28 = (s32[8]{0:T(128)S(1)}, s32[8]{0:T(128)}, u32[]{:S(2)}) copy-start(s32[8]{0:T(128)} %constant.140.clone) | copy-start | bytes 100
  716.6 22.1 %copy-start.27 = (s32[8]{0:T(128)S(1)}, s32[8]{0:T(128)}, u32[]{:S(2)}) copy-start(s32[8]{0:T(128)} %constant.137.clone) | copy-start | bytes 100
  716.6 22.7 %copy-start.26 = (s32[8]{0:T(128)S(1)}, s32[8]{0:T(128)}, u32[]{:S(2)}) copy-start(s32[8]{0:T(128)} %constant.139.clone) | copy-start | bytes 100
  720.9 24.8 %all-to-all-start.4 = ((f32[32,1,448]{2,1,0:T(1,128)}), f32[32,1,448]{2,1,0:T(1,128)}, u32[]{:S(2)}, u32[]{:S(2)}) async-start(f32[32,1,448]{2,1,0:T(1,128)} %all_to_all.50), calls=%async_computation.7 | async-start | bytes 131072 | tf_op jit(solution)/shard_map/all_to_all | solution.py:400
  724.2 443.3 %reduce-scatter.20.cloned.1.call-start = ((), (), s32[]{:S(2)}) async-start(), calls=%async_computation.23 | async-start | bytes 1310720 | tf_op jit(solution)/shard_map/reduce_scatter | solution.py:375
  728.6 169.5 %collective-permute-start.5 = (bf16[256,704]{0,1:T(8,128)(2,1)}, bf16[256,704]{0,1:T(8,128)(2,1)S(1)}, u32[]{:S(2)}, u32[]{:S(2)}) collective-permute-start(bf16[256,704]{0,1:T(8,128)(2,1)} %get-tuple-element.49), channel_id=1, source_target_pairs={{0,4},{1,12},{2,20},{3,28},{4,0},{5,8},{6,16},{7,24},{8,5},{9,13},... | collective-permute-start | bytes 1081352 | tf_op jit(solution)/shard_map/ppermute | solution.py:262
  728.6 170.2 %collective-permute-start.6 = (bf16[256,704]{0,1:T(8,128)(2,1)}, bf16[256,704]{0,1:T(8,128)(2,1)}, u32[]{:S(2)}, u32[]{:S(2)}) collective-permute-start(bf16[256,704]{0,1:T(8,128)(2,1)} %get-tuple-element.48), channel_id=1, source_target_pairs={{0,0},{1,8},{2,16},{3,24},{4,4},{5,12},{6,20},{7,28},{8,1},{9,9},{... | collective-permute-start | bytes 1081352 | tf_op jit(solution)/shard_map/ppermute | solution.py:262
  808.3 92.5 %collective-permute-start.3 = (bf16[256,704]{0,1:T(8,128)(2,1)}, bf16[256,704]{0,1:T(8,128)(2,1)}, u32[]{:S(2)}, u32[]{:S(2)}) collective-permute-start(bf16[256,704]{0,1:T(8,128)(2,1)} %get-tuple-element.53), channel_id=1, source_target_pairs={{0,4},{1,12},{2,20},{3,28},{4,0},{5,8},{6,16},{7,24},{8,5},{9,13},... | collective-permute-start | bytes 1081352 | tf_op jit(solution)/shard_map/ppermute | solution.py:262
  830.3 70.4 %collective-permute-start.4 = (bf16[256,704]{0,1:T(8,128)(2,1)}, bf16[256,704]{0,1:T(8,128)(2,1)}, u32[]{:S(2)}, u32[]{:S(2)}) collective-permute-start(bf16[256,704]{0,1:T(8,128)(2,1)} %get-tuple-element.52), channel_id=1, source_target_pairs={{0,0},{1,8},{2,16},{3,24},{4,4},{5,12},{6,20},{7,28},{8,1},{9,9},{... | collective-permute-start | bytes 1081352 | tf_op jit(solution)/shard_map/ppermute | solution.py:262
  1041.2 15.1 %collective-permute-start = (bf16[512,256]{1,0:T(8,128)(2,1)}, bf16[512,256]{1,0:T(8,128)(2,1)}, u32[]{:S(2)}, u32[]{:S(2)}) collective-permute-start(bf16[512,256]{1,0:T(8,128)(2,1)} %bitcast.150), channel_id=1, source_target_pairs={{0,20},{4,0},{8,24},{12,12},{16,4},{20,28},{24,16},{28,8},{1,21},{... | collective-permute-start | bytes 786440 | tf_op jit(solution)/shard_map/ppermute | solution.py:243
  1045.3 22.9 %collective-permute-start.1 = (bf16[512,256]{1,0:T(8,128)(2,1)}, bf16[512,256]{1,0:T(8,128)(2,1)}, u32[]{:S(2)}, u32[]{:S(2)}) collective-permute-start(bf16[512,256]{1,0:T(8,128)(2,1)} %bitcast.151), channel_id=1, source_target_pairs={{0,8},{4,12},{8,0},{12,24},{16,16},{20,4},{24,28},{28,20},{1,9},{5... | collective-permute-start | bytes 786440 | tf_op jit(solution)/shard_map/ppermute | solution.py:243
  1050.1 18.2 %collective-permute-start.2 = (bf16[512,256]{1,0:T(8,128)(2,1)}, bf16[512,256]{1,0:T(8,128)(2,1)S(1)}, u32[]{:S(2)}, u32[]{:S(2)}) collective-permute-start(bf16[512,256]{1,0:T(8,128)(2,1)} %bitcast.152), channel_id=1, source_target_pairs={{0,0},{4,20},{8,12},{12,4},{16,24},{20,16},{24,8},{28,28},{1,1},{5... | collective-permute-start | bytes 786440 | tf_op jit(solution)/shard_map/ppermute | solution.py:243
  (26 other events, 121.5 us)
Sparse Core Ops, SparseCore 0:
  9.6 84.7 all-gather.16
  96.8 42.1 all-gather.8
  140.9 136.9 all-gather.10
  287.1 108.0 all-gather.12
  396.9 52.5 all-gather.14
  487.3 52.5 reduce-scatter.11
  542.9 52.5 reduce-scatter.9
  597.9 81.6 reduce-scatter.23
  681.9 122.1 reduce-scatter.21
  806.2 89.5 reduce-scatter.25
  898.8 46.8 reduce-scatter.15
  947.8 89.5 reduce-scatter.17
  1039.7 96.8 reduce-scatter.13
  1139.3 28.1 reduce-scatter.19

commit v2 on v1

--- a/solution.py
+++ b/solution.py
@@ -2,13 +2,12 @@
 
 import jax
 import jax.numpy as jnp
-import numpy as np
 from jax import lax
 from jax.experimental import pallas as pl
 from jax.experimental.pallas import tpu as pltpu
 from jax.sharding import PartitionSpec as P
 
-H = 32
+
 HD = 64
 ROT = 16
 PAIR = 2 * HD
@@ -48,16 +47,12 @@
     lane = jnp.arange(PAIR) % HD
     ladder = 10000.0 ** (-jnp.arange(0, ROT, 2, dtype=jnp.float32) / ROT)
     places = jnp.arange(length, dtype=jnp.float32)
-    angles = places[:, None] * ladder[None, :]
-    cosine = jnp.tile(jnp.cos(angles), (1, PAIR // (ROT // 2)))
-    sine = jnp.tile(jnp.sin(angles), (1, PAIR // (ROT // 2)))
-    first = lane < ROT // 2
-    second = (lane >= ROT // 2) & (lane < ROT)
-    turned = first | second
-    cos_tab = jnp.where(turned[None, :], cosine, 1.0)
-    minus = jnp.where(first[None, :], -sine, 0.0)
-    plus = jnp.where(second[None, :], sine, 0.0)
-    return cos_tab, minus, plus
+    angles = places[:, None] * jnp.tile(ladder, PAIR // (ROT // 2))[None, :]
+    first = (lane < ROT // 2)[None, :]
+    second = ((lane >= ROT // 2) & (lane < ROT))[None, :]
+    cos_tab = jnp.where(first | second, jnp.cos(angles), 1.0)
+    sine = jnp.sin(angles)
+    return cos_tab, jnp.where(first, -sine, 0.0), jnp.where(second, sine, 0.0)
 
 
 def rotate(x, cos_tab, minus, plus):
@@ -143,6 +138,7 @@
             dk_acc[:n] += nn(ds, q_i)
             both.append(nn(kt[h * HD : (h + 1) * HD, :n], ds))
         rows.append(jnp.concatenate(both, axis=0).T)
+
     def finish(g):
         return g.astype(jnp.bfloat16).astype(jnp.float32)
 
@@ -203,6 +199,146 @@
     )(q, k, v, do, *tabs)
 
 
+def mid_kernel(core_ref, o_ref, mine_ref, other_ref, x_ref, gain_ref, shift_ref, x1_out, a_out):
+    step = pl.program_id(0)
+    core = core_ref[0]
+
+    @pl.when(step == 0)
+    def _():
+        x1_out[...] = x_ref[...].astype(jnp.float32)
+
+    x1_out[...] += nn(o_ref[core], mine_ref[0]) + nn(o_ref[1 - core], other_ref[0])
+
+    @pl.when(step == pl.num_programs(0) - 1)
+    def _():
+        xh, _ = norm_stats(x1_out[...])
+        a_out[...] = (xh * gain_ref[...] + shift_ref[...]).astype(jnp.bfloat16)
+
+
+def mid(core, o, mine, other, x, gain, shift):
+    parts, rows, head_width = o.shape
+    width = x.shape[1]
+    whole = lambda shape: pl.BlockSpec(shape, lambda i, c: (0, 0))
+    return pl.pallas_call(
+        mid_kernel,
+        grid_spec=pltpu.PrefetchScalarGridSpec(
+            num_scalar_prefetch=1,
+            grid=(parts // 2,),
+            in_specs=[
+                pl.BlockSpec((2, rows, head_width), lambda i, c: (i, 0, 0)),
+                pl.BlockSpec((1, head_width, width), lambda i, c: (i, 0, 0)),
+                pl.BlockSpec((1, head_width, width), lambda i, c: (i, 0, 0)),
+                whole((rows, width)),
+                whole((1, width)),
+                whole((1, width)),
+            ],
+            out_specs=[whole((rows, width)), whole((rows, width))],
+        ),
+        out_shape=[
+            jax.ShapeDtypeStruct((rows, width), jnp.float32),
+            jax.ShapeDtypeStruct((rows, width), jnp.bfloat16),
+        ],
+        compiler_params=pltpu.CompilerParams(vmem_limit_bytes=48 << 20),
+        cost_estimate=pl.CostEstimate(
+            flops=2 * rows * width * width,
+            bytes_accessed=2 * width * width + 10 * rows * width,
+            transcendentals=0,
+        ),
+        name="mid",
+    )(core, o, mine, other, x, gain[None, :], shift[None, :])
+
+
+def mid_back_kernel(count, core_ref, *refs):
+    pieces = refs[:count]
+    x1_ref, dy_ref, gain_ref, mine_ref, other_ref = refs[count : count + 5]
+    dx1_out, dxl_out, do_out, gain_out, shift_out = refs[count + 5 :]
+    core = core_ref[0]
+
+    @pl.when(pl.program_id(0) == 0)
+    def _():
+        dn = pieces[0][...].astype(jnp.float32)
+        for piece in pieces[1:]:
+            dn = dn + piece[...].astype(jnp.float32)
+        xh, r = norm_stats(x1_ref[...])
+        gain_out[...] = jnp.sum(dn * xh, axis=0, keepdims=True)
+        shift_out[...] = jnp.sum(dn, axis=0, keepdims=True)
+        dx1 = dy_ref[...].astype(jnp.float32) + norm_back(dn, xh, r, gain_ref[...])
+        dx1_out[...] = dx1
+        dxl_out[...] = dx1.astype(jnp.bfloat16)
+
+    dxl = dxl_out[...]
+    do_out[core] = nt(dxl, mine_ref[0]).astype(jnp.bfloat16)
+    do_out[1 - core] = nt(dxl, other_ref[0]).astype(jnp.bfloat16)
+
+
+def mid_back(core, pieces, x1, dy, gain, mine, other):
+    rows, width = x1.shape
+    halves, head_width, _ = mine.shape
+    whole = lambda shape: pl.BlockSpec(shape, lambda i, c: (0, 0))
+    full = whole((rows, width))
+    weight = pl.BlockSpec((1, head_width, width), lambda i, c: (i, 0, 0))
+    return pl.pallas_call(
+        functools.partial(mid_back_kernel, len(pieces)),
+        grid_spec=pltpu.PrefetchScalarGridSpec(
+            num_scalar_prefetch=1,
+            grid=(halves,),
+            in_specs=[full] * (len(pieces) + 2) + [whole((1, width)), weight, weight],
+            out_specs=[
+                full,
+                full,
+                pl.BlockSpec((2, rows, head_width), lambda i, c: (i, 0, 0)),
+                whole((1, width)),
+                whole((1, width)),
+            ],
+        ),
+        out_shape=[
+            jax.ShapeDtypeStruct((rows, width), jnp.float32),
+            jax.ShapeDtypeStruct((rows, width), jnp.bfloat16),
+            jax.ShapeDtypeStruct((2 * halves, rows, head_width), jnp.bfloat16),
+            jax.ShapeDtypeStruct((1, width), jnp.float32),
+            jax.ShapeDtypeStruct((1, width), jnp.float32),
+        ],
+        compiler_params=pltpu.CompilerParams(vmem_limit_bytes=56 << 20),
+        cost_estimate=pl.CostEstimate(
+            flops=2 * rows * width * width,
+            bytes_accessed=2 * width * width + 20 * rows * width,
+            transcendentals=0,
+        ),
+        name="mid_back",
+    )(core, *pieces, x1, dy, gain[None, :], mine, other)
+
+
+def back_project_kernel(dm_ref, w_ref, side_ref, out_ref):
+    width = w_ref.shape[0]
+    out_ref[:, :width] = nt(dm_ref[...], w_ref[...]).astype(jnp.bfloat16)
+    out_ref[:, width:] = side_ref[...]
+
+
+def back_project(dm, w, side):
+    rows, cols = dm.shape
+    width = w.shape[0]
+    extra = side.shape[1]
+    block = min(256, rows)
+    return pl.pallas_call(
+        back_project_kernel,
+        grid=(rows // block,),
+        in_specs=[
+            pl.BlockSpec((block, cols), lambda i: (i, 0)),
+            pl.BlockSpec((width, cols), lambda i: (0, 0)),
+            pl.BlockSpec((block, extra), lambda i: (i, 0)),
+        ],
+        out_specs=pl.BlockSpec((block, width + extra), lambda i: (i, 0)),
+        out_shape=jax.ShapeDtypeStruct((rows, width + extra), jnp.bfloat16),
+        compiler_params=pltpu.CompilerParams(vmem_limit_bytes=48 << 20),
+        cost_estimate=pl.CostEstimate(
+            flops=2 * rows * width * cols,
+            bytes_accessed=2 * rows * (width + cols + 2 * extra) + 2 * width * cols,
+            transcendentals=0,
+        ),
+        name="back_project",
+    )(dm, w, side)
+
+
 def third_rounds(parts):
     left = {s: [(j, (j * parts + s) // 3, (j * parts + s) % 3) for j in range(3)] for s in range(parts)}
     rounds = []
@@ -235,7 +371,6 @@
 
 
 def contiguous_thirds(block, parts, me):
-    rows, _, width = block.shape
     got = []
     slots = []
     for pairs, send, slot in third_rounds(parts):
@@ -248,26 +383,94 @@
     return jnp.concatenate(out, axis=1)
 
 
-def swap_blocks(block, seq_parts, fsdp_parts, me_seq):
+def after(x, *done):
+    return lax.optimization_barrier((x, *done))[0]
+
+
+def flip_pairs(parts, j):
+    return [(i, i ^ j) for i in range(parts)]
+
+
+def gather_flips(block, parts):
+    return [block] + [lax.ppermute(block, "fsdp", flip_pairs(parts, j)) for j in range(1, parts)]
+
+
+def send_flips(pieces, parts):
+    return [pieces[0]] + [
+        lax.ppermute(pieces[j], "fsdp", flip_pairs(parts, j)) for j in range(1, parts)
+    ]
+
+
+def total(pieces):
+    out = pieces[0].astype(jnp.float32)
+    for piece in pieces[1:]:
+        out = out + piece.astype(jnp.float32)
+    return out
+
+
+def project_kernel(x_ref, gain_ref, shift_ref, w_ref, bias_ref, m_out, a_out):
+    x = x_ref[...].astype(jnp.float32)
+    xh, _ = norm_stats(x)
+    a = (xh * gain_ref[...] + shift_ref[...]).astype(jnp.bfloat16)
+    a_out[...] = a
+    m_out[...] = nn(a, w_ref[...]) + bias_ref[...]
+
+
+def project(x, gain, shift, w, bias):
+    rows, width = x.shape
+    cols = w.shape[1]
+    block = min(256, rows)
+    whole = lambda shape: pl.BlockSpec(shape, lambda i: (0, 0))
+    return pl.pallas_call(
+        project_kernel,
+        grid=(rows // block,),
+        in_specs=[
+            pl.BlockSpec((block, width), lambda i: (i, 0)),
+            whole((1, width)),
+            whole((1, width)),
+            whole((width, cols)),
+            whole((1, cols)),
+        ],
+        out_specs=[
+            pl.BlockSpec((block, cols), lambda i: (i, 0)),
+            pl.BlockSpec((block, width), lambda i: (i, 0)),
+        ],
+        out_shape=[
+            jax.ShapeDtypeStruct((rows, cols), jnp.float32),
+            jax.ShapeDtypeStruct((rows, width), jnp.bfloat16),
+        ],
+        compiler_params=pltpu.CompilerParams(vmem_limit_bytes=48 << 20),
+        cost_estimate=pl.CostEstimate(
+            flops=2 * rows * width * cols,
+            bytes_accessed=rows * width * 4 + rows * cols * 4 + width * cols * 2,
+            transcendentals=0,
+        ),
+        name="project",
+    )(x, gain[None, :], shift[None, :], w, bias[None, :])
+
+
+def to_rows(block, fsdp_parts, here):
+    rows = block.shape[2] // fsdp_parts
+    pieces = []
+    for j in range(fsdp_parts):
+        piece = lax.dynamic_slice_in_dim(block, (here ^ j) * rows, rows, 2)
+        pieces.append(lax.ppermute(piece, "fsdp", flip_pairs(fsdp_parts, j)) if j else piece)
+    return pieces
+
+
+def to_columns(blocks, seq_parts, me_seq):
+    fsdp_parts = blocks.shape[0]
     ratio = seq_parts // fsdp_parts
-    got = []
-    for r in range(ratio):
-        pairs = []
-        for s in range(seq_parts):
-            for f in range(fsdp_parts):
-                h = (r + s) % ratio
-                dest = (ratio * f + h, s // ratio)
-                pairs.append((s * fsdp_parts + f, dest[0] * fsdp_parts + dest[1]))
-        piece = lax.dynamic_index_in_dim(block, (r + me_seq) % ratio, 1, keepdims=False)
-        got.append(lax.ppermute(piece, MESH_AXES, pairs))
-    out = []
-    for b in range(ratio):
-        r_of_b = (me_seq - b) % ratio
-        pick = got[0]
-        for r in range(1, ratio):
-            pick = jnp.where(r_of_b == r, got[r], pick)
-        out.append(pick)
-    return jnp.concatenate(out, axis=0)
+    out = jnp.zeros_like(blocks)
+    for r in range(fsdp_parts):
+        pairs = [
+            (s, ratio * (s % fsdp_parts ^ r) + s // fsdp_parts) for s in range(seq_parts)
+        ]
+        piece = lax.dynamic_index_in_dim(blocks, me_seq % fsdp_parts ^ r, 0, keepdims=False)
+        got = lax.ppermute(piece, "seq", pairs)
+        out = lax.dynamic_update_index_in_dim(out, got, me_seq // ratio ^ r, 0)
+    _, count, part, rows = blocks.shape
+    return out.transpose(1, 0, 2, 3).reshape(count, fsdp_parts * part, rows)
 
 
 def on_device(
@@ -296,105 +499,157 @@
     ff_rows, _ = down_weight.shape
     shard = width // F
 
+    ratio = S // F
+    if ratio != 2 or F & (F - 1):
+        raise ValueError("unsupported mesh")
+    even = me % 2 == 0
+    core = (me % 2).reshape(1).astype(jnp.int32)
+    mate = flip_pairs(S, 1)
+    here = lax.axis_index("fsdp")
+
+    def natural(pieces):
+        out = jnp.zeros((F, *pieces[0].shape), pieces[0].dtype)
+        for j, piece in enumerate(pieces):
+            out = lax.dynamic_update_index_in_dim(out, piece, here ^ j, 0)
+        return out
+
+    x_all = lax.all_gather(tokens, "seq", axis=0).reshape(all_rows, width)
     small = jnp.concatenate([attn_gain, attn_shift, ffn_gain, ffn_shift, qkv_bias])
-    small = lax.all_gather(small, "fsdp", axis=0)
+    small = natural(gather_flips(small, F))
     params = [small[:, i * shard : (i + 1) * shard].reshape(width).astype(f32) for i in range(4)]
     gain1, shift1, gain2, shift2 = params
     bias = small[:, 4 * shard :].reshape(3, S, head_width).astype(f32)
     bias = lax.dynamic_index_in_dim(bias, me, 1, keepdims=False).reshape(3 * head_width)
-
-    x_all = lax.all_gather(tokens, "seq", axis=0).reshape(all_rows, width)
-    qkv_part = lax.dynamic_index_in_dim(
-        qkv_weight.reshape(shard, 3, S, head_width), me, 2, keepdims=False
-    ).reshape(shard, 3 * head_width)
-    w_qkv = lax.all_gather(qkv_part, "fsdp", axis=0, tiled=True)
-    w_out = lax.all_gather(out_weight, "fsdp", axis=0, tiled=True)
-    dy_all = lax.all_gather(cotangent.reshape(rows, width), "fsdp", axis=0, tiled=True)
-    w_gate = lax.all_to_all(gate_weight, "fsdp", split_axis=1, concat_axis=0, tiled=True)
-    w_up = lax.all_to_all(up_weight, "fsdp", split_axis=1, concat_axis=0, tiled=True)
+    qkv_part = jnp.concatenate(
+        [
+            lax.dynamic_slice_in_dim(qkv_weight, j * width + me * head_width, head_width, 1)
+            for j in range(3)
+        ],
+        axis=1,
+    )
+    w_qkv = natural(gather_flips(qkv_part, F)).reshape(width, 3 * head_width)
+
+    fetched = jnp.stack(
+        [
+            jnp.where(
+                even,
+                gate_weight[:, f * ff_rows : (f + 1) * ff_rows],
+                up_weight[:, f * ff_rows : (f + 1) * ff_rows],
+            )
+            for f in range(F)
+        ]
+    )
+    fetched = after(fetched, qkv_part)
+    w_mine = lax.all_to_all(fetched, "fsdp", split_axis=0, concat_axis=0, tiled=True)
+    w_mine = w_mine.reshape(width, ff_rows)
+    w_other = lax.ppermute(w_mine, "seq", mate)
+    out_half = lax.dynamic_slice_in_dim(out_weight, me % 2 * head_width, head_width, 0)
+    out_mine = lax.all_gather(out_half, "fsdp", axis=0)
 
     tabs = rotary_tables(S * local_len)
-    xh_all, _ = norm_stats(x_all.astype(f32))
-    a1 = (xh_all * gain1 + shift1).astype(bf16)
-    m = nn(a1, w_qkv) + bias
+    m, a1 = project(x_all, gain1, shift1, w_qkv, bias)
     q, k, v, o = attend(m.reshape(S, seqs, local_len, 3 * head_width), tabs, head_width)
-    o_loc = lax.all_to_all(o, "seq", split_axis=0, concat_axis=0, tiled=True)
-    o_loc = o_loc.transpose(1, 2, 0, 3).reshape(rows, width)
-
-    x = tokens.reshape(rows, width).astype(f32)
-    x1 = x + nn(o_loc, w_out)
-    xh2, r2 = norm_stats(x1)
-    a2 = (xh2 * gain2 + shift2).astype(bf16)
+    o_got = lax.all_to_all(o, "seq", split_axis=0, concat_axis=0, tiled=True)
+    out_other = lax.ppermute(out_mine, "seq", mate)
+    dy_own = cotangent.reshape(rows, width)
+    dy_early = after(dy_own, o)
+    dy_pieces = [dy_own]
+    for j in range(1, F - 1):
+        dy_pieces.append(lax.ppermute(dy_early, "fsdp", flip_pairs(F, j)))
+    o_got = o_got.reshape(S, rows, head_width)
+
+    x_own = tokens.reshape(rows, width)
+    x1, a2 = mid(core, o_got, out_mine, out_other, x_own, gain2, shift2)
     a2_all = lax.all_gather(a2, "fsdp", axis=0, tiled=True)
-
-    g = nn(a2_all, w_gate)
-    u = nn(a2_all, w_up)
-    dh = nt(dy_all, down_weight)
+    dy_pieces.append(lax.ppermute(after(dy_own, a2_all), "fsdp", flip_pairs(F, F - 1)))
+    dy_all = natural(dy_pieces).reshape(F * rows, width)
+
+    first = nn(a2_all, w_mine)
+    second = nn(a2_all, w_other)
+    g = jnp.where(even, first, second)
+    u = jnp.where(even, second, first)
     sig = jax.nn.sigmoid(g)
     silu = g * sig
     hid = (silu * u).astype(bf16)
+    down_grad_part = tn(dy_all, hid).astype(bf16)
+    down_grad = lax.psum_scatter(down_grad_part, "seq", scatter_dimension=0, tiled=True)
+    dh = nt(after(dy_all, down_grad_part), down_weight)
     dg = (dh * u * sig * (1.0 + g * (1.0 - sig))).astype(bf16)
     du = (dh * silu).astype(bf16)
-    dn2_part = (nt(dg, w_gate) + nt(du, w_up)).astype(bf16)
-    dn2 = lax.psum_scatter(dn2_part, "fsdp", scatter_dimension=0, tiled=True).astype(f32)
-    down_part = nn(hid, down_weight).astype(bf16)
-    down_sum = lax.psum_scatter(down_part, "fsdp", scatter_dimension=0, tiled=True)
-    layer_out = (x1 + down_sum.astype(f32)).astype(bf16).reshape(tokens.shape)
-
-    dy = cotangent.reshape(rows, width).astype(f32)
-    dx1 = dy + norm_back(dn2, xh2, r2, gain2)
-    ffn_gain_part = jnp.sum(dn2 * xh2, axis=0)
-    ffn_shift_part = jnp.sum(dn2, axis=0)
-    dxl = dx1.astype(bf16)
-    do_loc = nt(dxl, w_out).astype(bf16)
-    do = lax.all_to_all(
-        do_loc.reshape(seqs, local_len, S, head_width).transpose(2, 0, 1, 3),
-        "seq",
-        split_axis=0,
-        concat_axis=0,
-        tiled=True,
+    d_first = jnp.where(even, dg, du)
+    d_second = jnp.where(even, du, dg)
+    dn2_part = (nt(d_first, w_mine) + nt(d_second, w_other)).astype(bf16)
+    dn2_part = dn2_part.reshape(F, rows, width)
+    dn2_pieces = []
+    for j in range(F):
+        dn2_pieces.append(lax.dynamic_index_in_dim(dn2_part, here ^ j, 0, keepdims=False))
+    dgu = after(jnp.concatenate([dg, du], axis=1), dn2_pieces)
+    for j in range(1, F):
+        dn2_pieces[j] = lax.ppermute(dn2_pieces[j], "fsdp", flip_pairs(F, j))
+    both_part = tn(dgu, a2_all).astype(bf16).reshape(2, ff_rows, width)
+    both = lax.psum_scatter(both_part, "seq", scatter_dimension=1, tiled=True)
+    hid_late = after(hid, both_part)
+    down_part = nn(hid_late, down_weight).astype(bf16)
+
+    dn2_pieces = after(dn2_pieces, down_part)
+    dx1, dxl, do_two, gain2_part, shift2_part = mid_back(
+        core, dn2_pieces, x1, dy_own, gain2, out_mine, out_other
     )
-
-    gate_part = tn(a2_all, dg).astype(bf16)
-    up_part = tn(a2_all, du).astype(bf16)
-    down_grad_part = tn(hid, dy_all).astype(bf16)
-    ratio = S // F
-    ff_block = ff_rows // ratio
-
-    def ffn_grad(part):
-        part = lax.psum_scatter(part, "seq", scatter_dimension=0, tiled=True)
-        return swap_blocks(part.reshape(-1, ratio, ff_block), S, F, me).astype(f32)
-
-    gate_result = ffn_grad(gate_part)
-    up_result = ffn_grad(up_part)
-    down_result = lax.psum_scatter(
-        down_grad_part, "seq", scatter_dimension=1, tiled=True
-    ).astype(f32)
-    out_part = tn(o_loc, dxl).astype(bf16)
-    out_part = lax.psum_scatter(out_part, "seq", scatter_dimension=1, tiled=True)
-    out_result = lax.psum_scatter(out_part, "fsdp", scatter_dimension=0, tiled=True).astype(f32)
+    do = lax.all_to_all(do_two, "seq", split_axis=0, concat_axis=0, tiled=True)
+    do = do.reshape(S, seqs, local_len, head_width)
+
+    dxl_all = natural(gather_flips(dxl, F)).reshape(F * rows, width)
+    o_got = after(o_got, dxl)
+    o_pieces = []
+    for j in range(F):
+        piece = lax.dynamic_slice_in_dim(o_got, 2 * (here ^ j), 2, 0)
+        o_pieces.append(lax.ppermute(piece, "fsdp", flip_pairs(F, j)) if j else piece)
+    o_cols = natural(o_pieces).transpose(1, 0, 2, 3).reshape(2, F * rows, head_width)
+    out_part = jnp.concatenate([tn(dxl_all, o_cols[h]) for h in range(2)], axis=1).astype(bf16)
 
     dq, dk, dv = attend_back(q, k, v, do, tabs)
     dm = jnp.concatenate([dq, dk, dv], axis=-1).reshape(all_rows, 3 * head_width)
-    dn1_part = nt(dm, w_qkv).astype(bf16)
-    dn1 = lax.psum_scatter(dn1_part, "seq", scatter_dimension=0, tiled=True).astype(f32)
-    qkv_part_grad = tn(a1, dm).astype(bf16)
-    qkv_sum = lax.psum_scatter(qkv_part_grad, "fsdp", scatter_dimension=0, tiled=True)
+    down_part = after(down_part, dm).reshape(F, rows, width)
+    down_pieces = send_flips(
+        [lax.dynamic_index_in_dim(down_part, here ^ j, 0, keepdims=False) for j in range(F)], F
+    )
+    joint_part = back_project(dm, w_qkv, out_part)
+    joint = lax.psum_scatter(joint_part, "seq", scatter_dimension=0, tiled=True)
+    dn1 = joint[:, :width].astype(f32)
+    out_result = joint[:, width:].T.astype(f32)
+    a1_late, both = after((a1, both), joint_part)
+    both_pieces = to_rows(both, F, here)
+    qkv_part_grad = tn(a1_late, dm).astype(bf16)
+    qkv_part_grad = qkv_part_grad.reshape(F, shard, 3 * head_width)
+    qkv_pieces = [
+        lax.dynamic_index_in_dim(qkv_part_grad, here ^ j, 0, keepdims=False) for j in range(F)
+    ]
+    dm, dn1_late, x_late, down_grad, both_pieces, down_pieces = after(
+        (dm, joint_part, x_all, down_grad, both_pieces, down_pieces), qkv_pieces
+    )
+    qkv_got = send_flips(qkv_pieces, F)
+    qkv_sum = total(qkv_got).astype(bf16)
     qkv_result = contiguous_thirds(qkv_sum.reshape(shard, 3, head_width), S, me).astype(f32)
+    both = to_columns(natural(both_pieces), S, me).astype(f32)
+    gate_result, up_result = both[0].T, both[1].T
+    layer_out = (x1 + total(down_pieces)).astype(bf16).reshape(tokens.shape)
+    down_result = down_grad.T.astype(f32)
 
     bias_part = jnp.sum(dm, axis=0, dtype=f32).reshape(3, 1, head_width)
     bias_full = lax.dynamic_update_slice_in_dim(
         jnp.zeros((3, S, head_width), f32), bias_part, me, 1
     ).reshape(3 * width)
-    attn_gain_part = jnp.sum(dn1_part.astype(f32) * xh_all, axis=0)
-    attn_shift_part = jnp.sum(dn1_part.astype(f32), axis=0)
+    xh_all, _ = norm_stats(x_late.astype(f32))
+    dn1_late = dn1_late[:, :width].astype(f32)
+    attn_gain_part = jnp.sum(dn1_late * xh_all, axis=0)
+    attn_shift_part = jnp.sum(dn1_late, axis=0)
     small_parts = [
         attn_gain_part,
         attn_shift_part,
         bias_full[: 2 * width],
         bias_full[2 * width :],
-        ffn_gain_part,
-        ffn_shift_part,
+        gain2_part[0],
+        shift2_part[0],
     ]
     packed = jnp.concatenate([p.reshape(devices, -1) for p in small_parts], axis=1)
     packed = lax.all_to_all(packed, MESH_AXES, split_axis=0, concat_axis=0, tiled=True)
@@ -407,7 +662,7 @@
         start += size
     gain1_result, shift1_result, bias_result, value_result, gain2_result, shift2_result = results
 
-    xh, r = norm_stats(x)
+    xh, r = norm_stats(x_own.astype(f32))
     tokens_grad = (dx1 + norm_back(dn1, xh, r, gain1)).reshape(tokens.shape)
     return (
         layer_out,

time: 1190 us -> 856 us (0.72)
  waiting for transfers between devices: 688 us -> 398 us
  blocking collectives: 58 us -> 0 us
  Pallas kernels: 42.6 us -> 88.2 us
  matrix products: 158 us -> 113 us
  starting transfers between devices: 56.6 us -> 96.1 us
  local copies, waits for them, and re-layouts: 94.6 us -> 71.8 us
    reduce_scatter x9 -> x3, waiting for transfers between devices: 403 us -> 0.01 us  [the longest x1 0.01 us: on_device(): both = lax.psum_scatter(both_part, 'seq', scatter_dimension=1, tiled=True)]
    ppermute x4 -> x33, waiting for transfers between devices: 0.01 us -> 188 us  [the longest x3 45.8 us: on_device(): lax.ppermute(piece, 'fsdp', flip_pairs(F, j))]
    all_gather x3 -> x1, waiting for transfers between devices: 109 us -> 26.2 us  [on_device(): out_mine = lax.all_gather(out_half, 'fsdp', axis=0)]
    all_to_all x1 -> x0, blocking collectives: 48.1 us -> none  [on_device(): lax.all_to_all(do_loc.reshape(seqs, local_len, S, head_width).transpose(2...]
    pallas_call x0 -> x4, Pallas kernels: none -> 45.4 us  [the longest x1 15.8 us: project(): pl.pallas_call(project_kernel, grid=(rows // block,), in_specs=[pl.BlockS...]
    ppermute x4 -> x33, starting transfers between devices: 30.9 us -> 66.9 us  [the longest x4 32.7 us: to_columns(): got = lax.ppermute(piece, 'seq', pairs)]
    unnamed x83 -> x107, local copies, waits for them, and re-layouts: 36.9 us -> 15.4 us
    all_gather x1, waiting for transfers between devices: 63 us -> 83 us  [on_device(): x_all = lax.all_gather(tokens, 'seq', axis=0).reshape(all_rows, width)]
  transfers between devices with their start and end apart: 25 -> 46, of which waited for: 15 -> 17; matrix products, arithmetic and copies ran while one was open for 22% -> 18% of each run, Pallas kernels for 4% -> 10%
where the time goes in v2:
time: 856 us; the launch traced here: 845 us
  waiting for transfers between devices  398 us (46%)
  matrix products  113 us (13%)
  starting transfers between devices  96.1 us (11%)
  Pallas kernels  88.2 us (10%)
  local copies, waits for them, and re-layouts  71.8 us (8%)
  other arithmetic  52.7 us (6%)
  between operations  25.3 us (3%)
    all_gather x1, waiting for transfers between devices, on_device(): x_all = lax.all_gather(tokens, 'seq', axis=0).reshape(all_rows, width)  83 us
    all_to_all x1, waiting for transfers between devices, on_device(): lax.all_to_all(fetched, 'fsdp', split_axis=0, concat_axis=0, tiled=True)  81.2 us
    ppermute x3, waiting for transfers between devices, on_device(): lax.ppermute(piece, 'fsdp', flip_pairs(F, j))  45.8 us
    dot_general x5, matrix products, tn(): lax.dot_general(a, b, (((0,), (0,)), ((), ())), preferred_element_type=jn...  38.9 us
    dot_general x3, matrix products, nt(): lax.dot_general(a, b, (((1,), (1,)), ((), ())), preferred_element_type=jn...  38.3 us
    dot_general x3, matrix products, nn(): lax.dot_general(a, b, (((1,), (0,)), ((), ())), preferred_element_type=jn...  35.8 us
    ppermute x6, waiting for transfers between devices, send_flips(): lax.ppermute(pieces[j], 'fsdp', flip_pairs(parts, j))  34.8 us
    ppermute x3, waiting for transfers between devices, on_device(): dn2_pieces[j] = lax.ppermute(dn2_pieces[j], 'fsdp', flip_pairs(F, j))  33.1 us
  transfers between devices with their start and end apart: 46, of which 17 were waited for; matrix products, arithmetic and copies ran while one was open for 18% of the time, Pallas kernels for 10%

profile of v2, /device:TPU:0, one launch (start us, length us, event | category | flops | bytes accessed | tf_op | source)
XLA Modules:
  0.0 845.3 jit_solution(10197009864826000027)
XLA Ops:
  28.3 20.9 %collective-permute-done.3 = bf16[512,768]{1,0:T(8,128)(2,1)} collective-permute-done((bf16[512,768]{1,0:T(8,128)(2,1)S(1)}, bf16[512,768]{1,0:T(8,128)(2,1)}, u32[]{:S(2)}, u32[]{:S(2)}) %collective-permute-start.3) | collective-permute-done | bytes 786464 | tf_op jit(solution)/shard_map/ppermute | solution.py:395
  51.3 8.9 %collective-permute-done.4 = bf16[512,768]{1,0:T(8,128)(2,1)} collective-permute-done((bf16[512,768]{1,0:T(8,128)(2,1)S(1)}, bf16[512,768]{1,0:T(8,128)(2,1)}, u32[]{:S(2)}, u32[]{:S(2)}) %collective-permute-start.4) | collective-permute-done | bytes 786464 | tf_op jit(solution)/shard_map/ppermute | solution.py:395
  62.3 26.2 %all-gather.10.cloned.1.call-done = bf16[1024,2048]{1,0:T(8,128)(2,1)} async-done(((bf16[256,2048]{1,0:T(8,128)(2,1)}), bf16[1024,2048]{1,0:T(8,128)(2,1)}) %all-gather.10.cloned.1.call-update) | async-done | bytes 4194320 | tf_op jit(solution)/shard_map/all_gather | solution.py:547
  89.4 83.0 %all-gather.8.cloned.1.call-done = bf16[16,128,2048]{2,1,0:T(8,128)(2,1)} async-done(((bf16[2,128,2048]{2,1,0:T(8,128)(2,1)}), bf16[16,128,2048]{2,1,0:T(8,128)(2,1)}) %all-gather.8.cloned.1.call-update) | async-done | bytes 8388624 | tf_op jit(solution)/shard_map/all_gather | solution.py:516
  172.4 15.8 %project.1 = (f32[2048,768]{1,0:T(8,128)}, bf16[2048,2048]{1,0:T(8,128)(2,1)}) custom-call(bf16[2048,2048]{1,0:T(8,128)(2,1)} %bitcast.200, f32[1,2048]{1,0:T(1,128)S(1)} %bitcast.197, f32[1,2048]{1,0:T(1,128)S(1)} %bitcast.198, bf16[2048,768]{1,0:T(8,128)(2,1)} %bitcast.6.w_ref, f32[1,768]{1,0:T(1,128)S(1)} %bitcast.199), custom_call_target="tpu_custom_call" | custom-call | flops 6442450944 | bytes 26214400 | tf_op jit(solution)/shard_map/project/pallas_call | solution.py:424
  188.2 17.9 %attend.1 = (bf16[8,2,128,256]{3,2,1,0:T(8,128)(2,1)S(1)}, bf16[8,2,128,256]{3,2,1,0:T(8,128)(2,1)S(1)}, bf16[8,2,128,256]{3,2,1,0:T(8,128)(2,1)S(1)}, bf16[8,2,128,256]{3,2,1,0:T(8,128)(2,1)}) custom-call(f32[8,2,128,768]{3,2,1,0:T(8,128)} %bitcast.206, f32[8,2,128,768]{3,2,1,0:T(8,128)} %bitcast.207, f32[8,2,128,768]{3,2,1,0:T(8,128)} %bitcast.208, ...), custom_call_target="tpu_custom_call" | custom-call | flops 2147483648 | bytes 10485760 | tf_op jit(solution)/shard_map/attend/pallas_call | solution.py:167
  219.5 18.6 %all-to-all-done = bf16[8,2,128,256]{3,2,1,0:T(8,128)(2,1)S(1)} async-done(((bf16[8,2,128,256]{3,2,1,0:T(8,128)(2,1)}), bf16[8,2,128,256]{3,2,1,0:T(8,128)(2,1)S(1)}, u32[]{:S(2)}, u32[]{:S(2)}) %all-to-all-start) | async-done | bytes 1048608 | tf_op jit(solution)/shard_map/all_to_all | solution.py:552
  243.4 7.2 mid.1
  252.4 81.2 %all-to-all-done.1 = bf16[4,512,1408]{2,1,0:T(8,128)(2,1)} async-done(((bf16[4,512,1408]{2,1,0:T(8,128)(2,1)}), bf16[4,512,1408]{2,1,0:T(8,128)(2,1)}, u32[]{:S(2)}, u32[]{:S(2)}) %all-to-all-start.1) | async-done | bytes 5767200 | tf_op jit(solution)/shard_map/all_to_all | solution.py:543
  338.8 24.8 %collective-permute-done.7 = bf16[256,2048]{1,0:T(8,128)(2,1)S(1)} collective-permute-done((bf16[256,2048]{1,0:T(8,128)(2,1)}, bf16[256,2048]{1,0:T(8,128)(2,1)S(1)}, u32[]{:S(2)}, u32[]{:S(2)}) %collective-permute-start.7) | collective-permute-done | bytes 1048608 | tf_op jit(solution)/shard_map/ppermute | solution.py:558
  367.1 11.1 %fusion.20 = f32[1024,1408]{1,0:T(8,128)S(1)} fusion(bf16[1024,2048]{1,0:T(8,128)(2,1)} %all-gather.6.cloned.1.call-done, bf16[2048,1408]{1,0:T(8,128)(2,1)} %bitcast.22), kind=kOutput, calls=%fused_computation.137 | convolution fusion | flops 5905580032 | bytes 15728640 | tf_op jit(solution)/shard_map/dot_general | solution.py:18
  378.2 13.3 %multiply_convert_fusion.2 = (bf16[1024,1408]{1,0:T(8,128)(2,1)S(1)}, f32[1024,1408]{1,0:T(8,128)}) fusion(f32[1024,1408]{1,0:T(8,128)S(1)} %fusion.20, pred[]{:T(512)S(6)} %eq.49, bf16[1024,2048]{1,0:T(8,128)(2,1)S(1)} %copy-done.37, bf16[2048,1408]{1,0:T(8,128)(2,1)} %collective-permute-done.10), kind=kOutput, calls=%fused_computation.16 | convolution fusion | flops 5917114368 | bytes 24379392 | tf_op jit(solution)/shard_map/dot_general | solution.py:18
  393.4 10.9 %convolution_convert_fusion.1 = bf16[2048,1408]{1,0:T(8,128)(2,1)} fusion(bf16[1024,2048]{1,0:T(8,128)(2,1)} %bitcast.17, bf16[1024,1408]{1,0:T(8,128)(2,1)S(1)} %get-tuple-element.67), kind=kOutput, calls=%fused_computation.10 | convolution fusion | flops 5908463616 | bytes 12845056 | tf_op jit(solution)/shard_map/dot_general | solution.py:26
  404.3 14.6 %multiply_convert_fusion = (bf16[1024,1408]{1,0:T(8,128)(2,1)S(1)}, bf16[1024,1408]{1,0:T(8,128)(2,1)S(1)}) fusion(f32[1024,1408]{1,0:T(8,128)} %copy-done.45, f32[1024,1408]{1,0:T(8,128)} %get-tuple-element.211, pred[]{:T(512)S(6)} %eq.49, bf16[1024,2048]{1,0:T(8,128)(2,1)} %bitcast.17, bf16[1408,2048]{1,0:T(8,128)(2,1)} %param.27), kind=kOutput, calls=%fused_computation.14 | convolution fusion | flops 5927206912 | bytes 27262976 | tf_op jit(solution)/shard_map/dot_general | solution.py:22
  419.0 12.8 %fusion.6 = f32[1024,2048]{1,0:T(8,128)} fusion(bf16[2048,1408]{1,0:T(8,128)(2,1)} %bitcast.22, bf16[1024,1408]{1,0:T(8,128)(2,1)S(1)} %get-tuple-element.154, bf16[1024,1408]{1,0:T(8,128)(2,1)S(1)} %get-tuple-element.153, pred[]{:T(512)S(6)} %eq.49), kind=kOutput, calls=%fused_computation.24 | convolution fusion | flops 5907021824 | bytes 19922944 | tf_op jit(solution)/shard_map/dot_general | solution.py:22
  432.2 10.9 %add_convert_fusion = bf16[1024,2048]{1,0:T(8,128)(2,1)S(1)} fusion(f32[1024,2048]{1,0:T(8,128)} %fusion.6, bf16[2048,1408]{1,0:T(8,128)(2,1)} %collective-permute-done.10, bf16[1024,1408]{1,0:T(8,128)(2,1)} %copy-done.19, bf16[1024,1408]{1,0:T(8,128)(2,1)} %copy-done.20, pred[]{:T(512)S(6)} %eq.49), kind=kOutput, calls=%fused_computation.9 | convolution fusion | flops 5911216128 | bytes 24117248 | tf_op jit(solution)/shard_map/dot_general | solution.py:22
  446.8 14.9 %convolution_convert_fusion = bf16[2816,2048]{1,0:T(8,128)(2,1)} fusion(bf16[1024,2816]{1,0:T(8,128)(2,1)S(1)} %pad_maximum_fusion.1, bf16[1024,2048]{1,0:T(8,128)(2,1)S(1)} %copy-done.38), kind=kOutput, calls=%fused_computation.8 | convolution fusion | flops 11816927232 | bytes 21495808 | tf_op jit(solution)/shard_map/dot_general | solution.py:26
  465.8 11.4 %convolution_convert_fusion.2 = bf16[1024,2048]{1,0:T(8,128)(2,1)} fusion(bf16[1024,1408]{1,0:T(8,128)(2,1)} %copy-done.44, bf16[1408,2048]{1,0:T(8,128)(2,1)} %param.27), kind=kOutput, calls=%fused_computation.19 | convolution fusion | flops 5907677184 | bytes 12845056 | tf_op jit(solution)/shard_map/dot_general | solution.py:18
  477.3 11.3 %collective-permute-done.11.refs_1_ = bf16[256,2048]{1,0:T(8,128)(2,1)S(1)} collective-permute-done((bf16[256,2048]{1,0:T(8,128)(2,1)}, bf16[256,2048]{1,0:T(8,128)(2,1)S(1)}, u32[]{:S(2)}, u32[]{:S(2)}) %collective-permute-start.11) | collective-permute-done | bytes 1048608 | tf_op jit(solution)/shard_map/ppermute | solution.py:588
  488.6 21.8 %collective-permute-done.12.refs_2_ = bf16[256,2048]{1,0:T(8,128)(2,1)S(1)} collective-permute-done((bf16[256,2048]{1,0:T(8,128)(2,1)}, bf16[256,2048]{1,0:T(8,128)(2,1)S(1)}, u32[]{:S(2)}, u32[]{:S(2)}) %collective-permute-start.12) | collective-permute-done | bytes 1048608 | tf_op jit(solution)/shard_map/ppermute | solution.py:588
  511.7 11.1 %mid_back.1 = (f32[256,2048]{1,0:T(8,128)}, bf16[256,2048]{1,0:T(8,128)(2,1)}, bf16[8,256,256]{2,1,0:T(8,128)(2,1)}, f32[1,2048]{1,0:T(1,128)}, f32[1,2048]{1,0:T(1,128)}) custom-call(s32[1]{0:T(128)} %bitcast.core_ref, bf16[256,2048]{1,0:T(8,128)(2,1)} %get-tuple-element.68.refs_0_, bf16[256,2048]{1,0:T(8,128)(2,1)} %copy-done.22, ...), custom_call_target="tpu_custom_call" | custom-call | flops 2147483648 | bytes 18874368 | tf_op jit(solution)/shard_map/mid_back/pallas_call | solution.py:280
  533.3 40.6 %collective-permute-done.17 = bf16[2,256,256]{2,1,0:T(8,128)(2,1)S(1)} collective-permute-done((bf16[2,256,256]{2,1,0:T(8,128)(2,1)S(1)}, bf16[2,256,256]{2,1,0:T(8,128)(2,1)S(1)}, u32[]{:S(2)}, u32[]{:S(2)}) %collective-permute-start.17) | collective-permute-done | bytes 262176 | tf_op jit(solution)/shard_map/ppermute | solution.py:606
  590.7 25.0 %attend_back.1 = (bf16[8,2,128,256]{3,2,1,0:T(8,128)(2,1)S(1)}, bf16[8,2,128,256]{3,2,1,0:T(8,128)(2,1)S(1)}, bf16[8,2,128,256]{3,2,1,0:T(8,128)(2,1)S(1)}) custom-call(bf16[8,2,128,256]{3,2,1,0:T(8,128)(2,1)S(1)} %get-tuple-element.58.q_ref, bf16[8,2,128,256]{3,2,1,0:T(8,128)(2,1)} %copy-done.15, bf16[8,2,128,256]{3,2,1,0:T(8,128)(2,1)} %copy-done.16, ...), custom_call_target="tpu_custom_call" | custom-call | flops 5368709120 | bytes 7340032 | tf_op jit(solution)/shard_map/attend_back/pallas_call | solution.py:187
  617.3 11.3 %back_project.1 = bf16[2048,2560]{1,0:T(8,128)(2,1)} custom-call(bf16[2048,768]{1,0:T(8,128)(2,1)S(1)} %bitcast.188, bf16[2048,768]{1,0:T(8,128)(2,1)} %bitcast.6.w_ref, bf16[2048,512]{1,0:T(8,128)(2,1)S(1)} %copy-done.13), custom_call_target="tpu_custom_call" | custom-call | flops 6442450944 | bytes 18874368 | tf_op jit(solution)/shard_map/back_project/pallas_call | solution.py:322
  663.1 10.5 %convolution_convert_fusion.3 = bf16[2048,768]{1,0:T(8,128)(2,1)S(1)} fusion(bf16[2048,2048]{1,0:T(8,128)(2,1)} %get-tuple-element.81, bf16[2048,768]{1,0:T(8,128)(2,1)} %bitcast.189), kind=kOutput, calls=%fused_computation.20 | convolution fusion | flops 6444023808 | bytes 14680064 | tf_op jit(solution)/shard_map/dot_general | solution.py:26
  683.2 32.6 %collective-permute-done.24 = bf16[256,2048]{1,0:T(8,128)(2,1)} collective-permute-done((bf16[256,2048]{1,0:T(8,128)(2,1)}, bf16[256,2048]{1,0:T(8,128)(2,1)}, u32[]{:S(2)}, u32[]{:S(2)}) %collective-permute-start.24) | collective-permute-done | bytes 1048608 | tf_op jit(solution)/shard_map/ppermute | solution.py:400
  719.3 12.7 %collective-permute-done.21 = bf16[2,176,512]{2,1,0:T(8,128)(2,1)} collective-permute-done((bf16[2,176,512]{2,1,0:T(8,128)(2,1)}, bf16[2,176,512]{2,1,0:T(8,128)(2,1)}, u32[]{:S(2)}, u32[]{:S(2)}) %collective-permute-start.21) | collective-permute-done | bytes 360480 | tf_op jit(solution)/shard_map/ppermute | solution.py:457
  745.2 7.0 convert_reduce_fusion.1
  773.5 10.5 %collective-permute-start.34 = (bf16[2,176,512]{2,1,0:T(8,128)(2,1)S(1)}, bf16[2,176,512]{2,1,0:T(8,128)(2,1)S(1)}, u32[]{:S(2)}, u32[]{:S(2)}) collective-permute-start(bf16[2,176,512]{2,1,0:T(8,128)(2,1)S(1)} %copy-done.28), channel_id=1, source_target_pairs={{0,16},{4,24},{8,0},{12,8},{16,20},{20,28},{24,4},{28,12},{1,17},{... | collective-permute-start | bytes 1081352 | tf_op jit(solution)/shard_map/ppermute | solution.py:470
  785.2 17.1 %collective-permute-start.35 = (bf16[2,176,512]{2,1,0:T(8,128)(2,1)S(1)}, bf16[2,176,512]{2,1,0:T(8,128)(2,1)S(1)}, u32[]{:S(2)}, u32[]{:S(2)}) collective-permute-start(bf16[2,176,512]{2,1,0:T(8,128)(2,1)S(1)} %copy-done.27), channel_id=1, source_target_pairs={{0,24},{4,16},{8,8},{12,0},{16,28},{20,20},{24,12},{28,4},{1,25},{... | collective-permute-start | bytes 1081352 | tf_op jit(solution)/shard_map/ppermute | solution.py:470
  803.3 6.3 collective-permute-done.35
  817.1 6.7 collective-permute-start.30
  (311 shorter events, 191.1 us)
Async XLA Ops:
  7.2 81.2 %all-gather.10.cloned.1.call-start = ((), (), s32[]{:S(2)}) async-start(), calls=%async_computation.12 | async-start | bytes 5242880 | tf_op jit(solution)/shard_map/all_gather | solution.py:547
  9.9 162.5 %all-gather.8.cloned.1.call-start = ((), (), s32[]{:S(2)}) async-start(), calls=%async_computation.11 | async-start | bytes 9437184 | tf_op jit(solution)/shard_map/all_gather | solution.py:516
  17.4 31.8 %collective-permute-start.3 = (bf16[512,768]{1,0:T(8,128)(2,1)S(1)}, bf16[512,768]{1,0:T(8,128)(2,1)}, u32[]{:S(2)}, u32[]{:S(2)}) collective-permute-start(bf16[512,768]{1,0:T(8,128)(2,1)S(1)} %pad_maximum_fusion.4), channel_id=1, source_target_pairs={{0,1},{1,0},{2,3},{3,2},{4,5},{5,4},{6,7},{7,6},{8,9},{9,8},{10,11... | collective-permute-start | bytes 2359304 | tf_op jit(solution)/shard_map/ppermute | solution.py:395
  19.4 40.8 %collective-permute-start.4 = (bf16[512,768]{1,0:T(8,128)(2,1)S(1)}, bf16[512,768]{1,0:T(8,128)(2,1)}, u32[]{:S(2)}, u32[]{:S(2)}) collective-permute-start(bf16[512,768]{1,0:T(8,128)(2,1)S(1)} %pad_maximum_fusion.4), channel_id=1, source_target_pairs={{0,2},{1,3},{2,0},{3,1},{4,6},{5,7},{6,4},{7,5},{8,10},{9,11},{10,... | collective-permute-start | bytes 2359304 | tf_op jit(solution)/shard_map/ppermute | solution.py:395
  26.9 61.5 %collective-permute-start.5 = (bf16[512,768]{1,0:T(8,128)(2,1)S(1)}, bf16[512,768]{1,0:T(8,128)(2,1)S(1)}, u32[]{:S(2)}, u32[]{:S(2)}) collective-permute-start(bf16[512,768]{1,0:T(8,128)(2,1)S(1)} %pad_maximum_fusion.4), channel_id=1, source_target_pairs={{0,3},{1,2},{2,1},{3,0},{4,7},{5,6},{6,5},{7,4},{8,11},{9,10},{10,... | collective-permute-start | bytes 2359304 | tf_op jit(solution)/shard_map/ppermute | solution.py:395
  88.4 154.9 %collective-permute-start.6 = (bf16[4,256,2048]{2,1,0:T(8,128)(2,1)}, bf16[4,256,2048]{2,1,0:T(8,128)(2,1)}, u32[]{:S(2)}, u32[]{:S(2)}) collective-permute-start(bf16[4,256,2048]{2,1,0:T(8,128)(2,1)} %bitcast.209), channel_id=1, source_target_pairs={{0,4},{4,0},{8,12},{12,8},{16,20},{20,16},{24,28},{28,24},{1,5},{5... | collective-permute-start | bytes 12582920 | tf_op jit(solution)/shard_map/ppermute | solution.py:553
  208.1 30.1 %all-to-all-start = ((bf16[8,2,128,256]{3,2,1,0:T(8,128)(2,1)}), bf16[8,2,128,256]{3,2,1,0:T(8,128)(2,1)S(1)}, u32[]{:S(2)}, u32[]{:S(2)}) async-start(bf16[8,2,128,256]{3,2,1,0:T(8,128)(2,1)} %get-tuple-element.56), calls=%async_computation | async-start | bytes 2097152 | tf_op jit(solution)/shard_map/all_to_all | solution.py:552
  238.1 95.5 %all-to-all-start.1 = ((bf16[4,512,1408]{2,1,0:T(8,128)(2,1)}), bf16[4,512,1408]{2,1,0:T(8,128)(2,1)}, u32[]{:S(2)}, u32[]{:S(2)}) async-start(bf16[4,512,1408]{2,1,0:T(8,128)(2,1)} %pad_maximum_fusion), calls=%async_computation.1 | async-start | bytes 11534336 | tf_op jit(solution)/shard_map/all_to_all | solution.py:543
  243.2 122.4 %all-gather.6.cloned.1.call-start = ((), (), s32[]{:S(2)}) async-start(), calls=%async_computation.7 | async-start | bytes 5242880 | tf_op jit(solution)/shard_map/all_gather | solution.py:563
  251.9 401.6 %reduce-scatter.6.cloned.1.call-start = ((), (), s32[]{:S(2)}) async-start(), calls=%async_computation.9 | async-start | bytes 12976128 | tf_op jit(solution)/shard_map/reduce_scatter | solution.py:590
  333.6 44.5 %collective-permute-start.10 = (bf16[2048,1408]{1,0:T(8,128)(2,1)}, bf16[2048,1408]{1,0:T(8,128)(2,1)}, u32[]{:S(2)}, u32[]{:S(2)}) collective-permute-start(bf16[2048,1408]{1,0:T(8,128)(2,1)} %bitcast.22), channel_id=1, source_target_pairs={{0,4},{4,0},{8,12},{12,8},{16,20},{20,16},{24,28},{28,24},{1,5},{5... | collective-permute-start | bytes 17301512 | tf_op jit(solution)/shard_map/ppermute | solution.py:545
  333.6 29.9 %collective-permute-start.7 = (bf16[256,2048]{1,0:T(8,128)(2,1)}, bf16[256,2048]{1,0:T(8,128)(2,1)S(1)}, u32[]{:S(2)}, u32[]{:S(2)}) collective-permute-start(bf16[256,2048]{1,0:T(8,128)(2,1)} %bitcast.213), channel_id=1, source_target_pairs={{0,1},{1,0},{2,3},{3,2},{4,5},{5,4},{6,7},{7,6},{8,9},{9,8},{10,11... | collective-permute-start | bytes 3145736 | tf_op jit(solution)/shard_map/ppermute | solution.py:558
  335.1 29.5 %collective-permute-start.8 = (bf16[256,2048]{1,0:T(8,128)(2,1)}, bf16[256,2048]{1,0:T(8,128)(2,1)S(1)}, u32[]{:S(2)}, u32[]{:S(2)}) collective-permute-start(bf16[256,2048]{1,0:T(8,128)(2,1)} %bitcast.214), channel_id=1, source_target_pairs={{0,2},{1,3},{2,0},{3,1},{4,6},{5,7},{6,4},{7,5},{8,10},{9,11},{10,... | collective-permute-start | bytes 3145736 | tf_op jit(solution)/shard_map/ppermute | solution.py:558
  461.7 257.6 %reduce-scatter.4.cloned.1.call-start = ((), (), s32[]{:S(2)}) async-start(), calls=%async_computation.8 | async-start | bytes 6488064 | tf_op jit(solution)/shard_map/reduce_scatter | solution.py:575
  463.2 47.2 %collective-permute-start.12 = (bf16[256,2048]{1,0:T(8,128)(2,1)}, bf16[256,2048]{1,0:T(8,128)(2,1)S(1)}, u32[]{:S(2)}, u32[]{:S(2)}) collective-permute-start(bf16[256,2048]{1,0:T(8,128)(2,1)} %get-tuple-element.167), channel_id=1, source_target_pairs={{0,2},{1,3},{2,0},{3,1},{4,6},{5,7},{6,4},{7,5},{8,10},{9,11},{10,... | collective-permute-start | bytes 3145736 | tf_op jit(solution)/shard_map/ppermute | solution.py:588
  464.3 46.1 %collective-permute-start.13 = (bf16[256,2048]{1,0:T(8,128)(2,1)}, bf16[256,2048]{1,0:T(8,128)(2,1)S(1)}, u32[]{:S(2)}, u32[]{:S(2)}) collective-permute-start(bf16[256,2048]{1,0:T(8,128)(2,1)} %get-tuple-element.166), channel_id=1, source_target_pairs={{0,3},{1,2},{2,1},{3,0},{4,7},{5,6},{6,5},{7,4},{8,11},{9,10},{10,... | collective-permute-start | bytes 3145736 | tf_op jit(solution)/shard_map/ppermute | solution.py:588
  522.8 58.5 %collective-permute-start.14 = (bf16[256,2048]{1,0:T(8,128)(2,1)}, bf16[256,2048]{1,0:T(8,128)(2,1)}, u32[]{:S(2)}, u32[]{:S(2)}) collective-permute-start(bf16[256,2048]{1,0:T(8,128)(2,1)} %get-tuple-element.76), channel_id=1, source_target_pairs={{0,1},{1,0},{2,3},{3,2},{4,5},{5,4},{6,7},{7,6},{8,9},{9,8},{10,11... | collective-permute-start | bytes 3145736 | tf_op jit(solution)/shard_map/ppermute | solution.py:395
  524.0 58.7 %collective-permute-start.15 = (bf16[256,2048]{1,0:T(8,128)(2,1)}, bf16[256,2048]{1,0:T(8,128)(2,1)}, u32[]{:S(2)}, u32[]{:S(2)}) collective-permute-start(bf16[256,2048]{1,0:T(8,128)(2,1)} %get-tuple-element.76), channel_id=1, source_target_pairs={{0,2},{1,3},{2,0},{3,1},{4,6},{5,7},{6,4},{7,5},{8,10},{9,11},{10,... | collective-permute-start | bytes 3145736 | tf_op jit(solution)/shard_map/ppermute | solution.py:395
  524.1 59.9 %collective-permute-start.16 = (bf16[256,2048]{1,0:T(8,128)(2,1)}, bf16[256,2048]{1,0:T(8,128)(2,1)}, u32[]{:S(2)}, u32[]{:S(2)}) collective-permute-start(bf16[256,2048]{1,0:T(8,128)(2,1)} %get-tuple-element.76), channel_id=1, source_target_pairs={{0,3},{1,2},{2,1},{3,0},{4,7},{5,6},{6,5},{7,4},{8,11},{9,10},{10,... | collective-permute-start | bytes 3145736 | tf_op jit(solution)/shard_map/ppermute | solution.py:395
  526.3 63.3 %all-to-all-start.2 = ((bf16[8,256,256]{2,1,0:T(8,128)(2,1)}), bf16[8,256,256]{2,1,0:T(8,128)(2,1)}, u32[]{:S(2)}, u32[]{:S(2)}) async-start(bf16[8,256,256]{2,1,0:T(8,128)(2,1)} %get-tuple-element.72), calls=%async_computation.2 | async-start | bytes 2097152 | tf_op jit(solution)/shard_map/all_to_all | solution.py:598
  530.6 297.7 %reduce-scatter.8.cloned.1.call-start = ((), (), s32[]{:S(2)}) async-start(), calls=%async_computation.10 | async-start | bytes 11796480 | tf_op jit(solution)/shard_map/reduce_scatter | solution.py:617
  530.7 43.2 %collective-permute-start.17 = (bf16[2,256,256]{2,1,0:T(8,128)(2,1)S(1)}, bf16[2,256,256]{2,1,0:T(8,128)(2,1)S(1)}, u32[]{:S(2)}, u32[]{:S(2)}) collective-permute-start(bf16[2,256,256]{2,1,0:T(8,128)(2,1)S(1)} %get-tuple-element.188), channel_id=1, source_target_pairs={{0,1},{1,0},{2,3},{3,2},{4,5},{5,4},{6,7},{7,6},{8,9},{9,8},{10,11... | collective-permute-start | bytes 786440 | tf_op jit(solution)/shard_map/ppermute | solution.py:606
  532.6 45.6 %collective-permute-start.18 = (bf16[2,256,256]{2,1,0:T(8,128)(2,1)S(1)}, bf16[2,256,256]{2,1,0:T(8,128)(2,1)S(1)}, u32[]{:S(2)}, u32[]{:S(2)}) collective-permute-start(bf16[2,256,256]{2,1,0:T(8,128)(2,1)S(1)} %get-tuple-element.187), channel_id=1, source_target_pairs={{0,2},{1,3},{2,0},{3,1},{4,6},{5,7},{6,4},{7,5},{8,10},{9,11},{10,... | collective-permute-start | bytes 786440 | tf_op jit(solution)/shard_map/ppermute | solution.py:606
  651.7 64.0 %collective-permute-start.24 = (bf16[256,2048]{1,0:T(8,128)(2,1)}, bf16[256,2048]{1,0:T(8,128)(2,1)}, u32[]{:S(2)}, u32[]{:S(2)}) collective-permute-start(bf16[256,2048]{1,0:T(8,128)(2,1)} %get-tuple-element.163), channel_id=1, source_target_pairs={{0,2},{1,3},{2,0},{3,1},{4,6},{5,7},{6,4},{7,5},{8,10},{9,11},{10,... | collective-permute-start | bytes 3145736 | tf_op jit(solution)/shard_map/ppermute | solution.py:400
  652.8 64.2 %collective-permute-start.25 = (bf16[256,2048]{1,0:T(8,128)(2,1)}, bf16[256,2048]{1,0:T(8,128)(2,1)}, u32[]{:S(2)}, u32[]{:S(2)}) collective-permute-start(bf16[256,2048]{1,0:T(8,128)(2,1)} %get-tuple-element.162), channel_id=1, source_target_pairs={{0,3},{1,2},{2,1},{3,0},{4,7},{5,6},{6,5},{7,4},{8,11},{9,10},{10,... | collective-permute-start | bytes 3145736 | tf_op jit(solution)/shard_map/ppermute | solution.py:400
  655.8 62.6 %collective-permute-start.20 = (bf16[2,176,512]{2,1,0:T(8,128)(2,1)}, bf16[2,176,512]{2,1,0:T(8,128)(2,1)}, u32[]{:S(2)}, u32[]{:S(2)}) collective-permute-start(bf16[2,176,512]{2,1,0:T(8,128)(2,1)} %get-tuple-element.182), channel_id=1, source_target_pairs={{0,1},{1,0},{2,3},{3,2},{4,5},{5,4},{6,7},{7,6},{8,9},{9,8},{10,11... | collective-permute-start | bytes 1081352 | tf_op jit(solution)/shard_map/ppermute | solution.py:457
  657.6 74.3 %collective-permute-start.21 = (bf16[2,176,512]{2,1,0:T(8,128)(2,1)}, bf16[2,176,512]{2,1,0:T(8,128)(2,1)}, u32[]{:S(2)}, u32[]{:S(2)}) collective-permute-start(bf16[2,176,512]{2,1,0:T(8,128)(2,1)} %get-tuple-element.181), channel_id=1, source_target_pairs={{0,2},{1,3},{2,0},{3,1},{4,6},{5,7},{6,4},{7,5},{8,10},{9,11},{10,... | collective-permute-start | bytes 1081352 | tf_op jit(solution)/shard_map/ppermute | solution.py:457
  660.9 71.0 %collective-permute-start.22 = (bf16[2,176,512]{2,1,0:T(8,128)(2,1)}, bf16[2,176,512]{2,1,0:T(8,128)(2,1)}, u32[]{:S(2)}, u32[]{:S(2)}) collective-permute-start(bf16[2,176,512]{2,1,0:T(8,128)(2,1)} %get-tuple-element.180), channel_id=1, source_target_pairs={{0,3},{1,2},{2,1},{3,0},{4,7},{5,6},{6,5},{7,4},{8,11},{9,10},{10,... | collective-permute-start | bytes 1081352 | tf_op jit(solution)/shard_map/ppermute | solution.py:457
  715.8 96.2 %collective-permute-start.28 = (bf16[512,768]{0,1:T(8,128)(2,1)}, bf16[512,768]{0,1:T(8,128)(2,1)}, u32[]{:S(2)}, u32[]{:S(2)}) collective-permute-start(bf16[512,768]{0,1:T(8,128)(2,1)} %bitcast.231), channel_id=1, source_target_pairs={{0,3},{1,2},{2,1},{3,0},{4,7},{5,6},{6,5},{7,4},{8,11},{9,10},{10,... | collective-permute-start | bytes 2359304 | tf_op jit(solution)/shard_map/ppermute | solution.py:400
  717.0 94.9 %collective-permute-start.27 = (bf16[512,768]{0,1:T(8,128)(2,1)}, bf16[512,768]{0,1:T(8,128)(2,1)}, u32[]{:S(2)}, u32[]{:S(2)}) collective-permute-start(bf16[512,768]{0,1:T(8,128)(2,1)} %bitcast.230), channel_id=1, source_target_pairs={{0,2},{1,3},{2,0},{3,1},{4,6},{5,7},{6,4},{7,5},{8,10},{9,11},{10,... | collective-permute-start | bytes 2359304 | tf_op jit(solution)/shard_map/ppermute | solution.py:400
  718.5 93.4 %collective-permute-start.26 = (bf16[512,768]{0,1:T(8,128)(2,1)}, bf16[512,768]{0,1:T(8,128)(2,1)}, u32[]{:S(2)}, u32[]{:S(2)}) collective-permute-start(bf16[512,768]{0,1:T(8,128)(2,1)} %bitcast.229), channel_id=1, source_target_pairs={{0,1},{1,0},{2,3},{3,2},{4,5},{5,4},{6,7},{7,6},{8,9},{9,8},{10,11... | collective-permute-start | bytes 2359304 | tf_op jit(solution)/shard_map/ppermute | solution.py:400
  773.5 29.8 %collective-permute-start.34 = (bf16[2,176,512]{2,1,0:T(8,128)(2,1)S(1)}, bf16[2,176,512]{2,1,0:T(8,128)(2,1)S(1)}, u32[]{:S(2)}, u32[]{:S(2)}) collective-permute-start(bf16[2,176,512]{2,1,0:T(8,128)(2,1)S(1)} %copy-done.28), channel_id=1, source_target_pairs={{0,16},{4,24},{8,0},{12,8},{16,20},{20,28},{24,4},{28,12},{1,17},{... | collective-permute-start | bytes 1081352 | tf_op jit(solution)/shard_map/ppermute | solution.py:470
  (62 other events, 931.8 us)
Sparse Core Ops, SparseCore 0:
  10.5 77.9 all-gather.9
  90.0 82.3 all-gather.7
  252.0 93.2 all-gather.5
  461.8 134.4 reduce-scatter.5
  598.5 67.9 reduce-scatter.3
  668.6 115.7 reduce-scatter.7

commit v3 on v2

--- a/solution.py
+++ b/solution.py
@@ -308,35 +308,93 @@
     )(core, *pieces, x1, dy, gain[None, :], mine, other)
 
 
-def back_project_kernel(dm_ref, w_ref, side_ref, out_ref):
-    width = w_ref.shape[0]
-    out_ref[:, :width] = nt(dm_ref[...], w_ref[...]).astype(jnp.bfloat16)
-    out_ref[:, width:] = side_ref[...]
-
-
-def back_project(dm, w, side):
-    rows, cols = dm.shape
-    width = w.shape[0]
-    extra = side.shape[1]
-    block = min(256, rows)
+def joint_kernel(count, *refs):
+    dq_ref, dk_ref, dv_ref, w_ref = refs[:4]
+    x_refs = refs[4 : 4 + count]
+    o_refs = refs[4 + count : 4 + 2 * count]
+    out_ref = refs[-1]
+    width, cols = w_ref.shape
+    part = cols // 3
+    w = w_ref[...]
+    total = nt(dq_ref[...], w[:, :part])
+    total = total + nt(dk_ref[...], w[:, part : 2 * part])
+    total = total + nt(dv_ref[...], w[:, 2 * part :])
+    out_ref[:, :width] = total.astype(jnp.bfloat16)
+    for h in range(2):
+        side = tn(x_refs[0][...], o_refs[0][h])
+        for x_ref, o_ref in zip(x_refs[1:], o_refs[1:]):
+            side = side + tn(x_ref[...], o_ref[h])
+        start = width + h * part
+        out_ref[:, start : start + part] = side.astype(jnp.bfloat16)
+
+
+def joint(dq, dk, dv, w, xs, os):
+    all_rows, part = dq.shape
+    width, cols = w.shape
+    rows = xs[0].shape[0]
+    count = len(xs)
+    parts = width // part
+    block = all_rows // parts
+    if block != part:
+        raise ValueError("unsupported shape")
+    row_block = pl.BlockSpec((block, part), lambda i: (i, 0))
     return pl.pallas_call(
-        back_project_kernel,
-        grid=(rows // block,),
-        in_specs=[
-            pl.BlockSpec((block, cols), lambda i: (i, 0)),
-            pl.BlockSpec((width, cols), lambda i: (0, 0)),
-            pl.BlockSpec((block, extra), lambda i: (i, 0)),
-        ],
-        out_specs=pl.BlockSpec((block, width + extra), lambda i: (i, 0)),
-        out_shape=jax.ShapeDtypeStruct((rows, width + extra), jnp.bfloat16),
+        functools.partial(joint_kernel, count),
+        grid=(parts,),
+        in_specs=[row_block] * 3
+        + [pl.BlockSpec((width, cols), lambda i: (0, 0))]
+        + [pl.BlockSpec((rows, part), lambda i: (0, i))] * count
+        + [pl.BlockSpec((2, rows, part), lambda i: (0, 0, 0))] * count,
+        out_specs=pl.BlockSpec((block, width + 2 * part), lambda i: (i, 0)),
+        out_shape=jax.ShapeDtypeStruct((all_rows, width + 2 * part), jnp.bfloat16),
         compiler_params=pltpu.CompilerParams(vmem_limit_bytes=48 << 20),
         cost_estimate=pl.CostEstimate(
-            flops=2 * rows * width * cols,
-            bytes_accessed=2 * rows * (width + cols + 2 * extra) + 2 * width * cols,
+            flops=2 * all_rows * width * cols + 4 * count * rows * width * part,
+            bytes_accessed=4 * all_rows * (width + cols) + 2 * width * cols,
             transcendentals=0,
         ),
-        name="back_project",
-    )(dm, w, side)
+        name="joint",
+    )(dq, dk, dv, w, *xs, *os)
+
+
+def pick_kernel(counts, core_ref, gate_ref, up_ref, out_ref):
+    blocks, fsdp_parts, part = counts
+
+    def pick(source):
+        rows = source[...]
+        for f in range(fsdp_parts):
+            starts = [(t * fsdp_parts + f) * part for t in range(blocks)]
+            out_ref[f] = jnp.concatenate([rows[:, a : a + part] for a in starts], axis=1)
+
+    @pl.when(core_ref[0] == 0)
+    def _():
+        pick(gate_ref)
+
+    @pl.when(core_ref[0] != 0)
+    def _():
+        pick(up_ref)
+
+
+def pick(core, gate, up, blocks, fsdp_parts):
+    rows, cols = gate.shape
+    part = cols // (blocks * fsdp_parts)
+    block = min(64, rows)
+    return pl.pallas_call(
+        functools.partial(pick_kernel, (blocks, fsdp_parts, part)),
+        grid_spec=pltpu.PrefetchScalarGridSpec(
+            num_scalar_prefetch=1,
+            grid=(rows // block,),
+            in_specs=[
+                pl.BlockSpec((block, cols), lambda i, c: (jnp.where(c[0] == 0, i, 0), 0)),
+                pl.BlockSpec((block, cols), lambda i, c: (jnp.where(c[0] == 0, 0, i), 0)),
+            ],
+            out_specs=pl.BlockSpec((fsdp_parts, block, blocks * part), lambda i, c: (0, i, 0)),
+        ),
+        out_shape=jax.ShapeDtypeStruct((fsdp_parts, rows, blocks * part), gate.dtype),
+        compiler_params=pltpu.CompilerParams(vmem_limit_bytes=32 << 20),
+        cost_estimate=pl.CostEstimate(flops=0, bytes_accessed=4 * rows * cols, transcendentals=0),
+        name="pick",
+    )(core, gate, up)
 
 
 def third_rounds(parts):
@@ -393,6 +451,22 @@
 
 def gather_flips(block, parts):
     return [block] + [lax.ppermute(block, "fsdp", flip_pairs(parts, j)) for j in range(1, parts)]
+
+
+def relay_near(block, parts):
+    if parts != 4:
+        return gather_flips(block, parts)[1:]
+    return [lax.ppermute(block, "fsdp", flip_pairs(parts, j)) for j in (1, 2)]
+
+
+def relay_far(block, near, parts):
+    if parts != 4:
+        return [block, *near]
+    one, two = near
+    half = block.shape[0] // 2
+    head = lax.ppermute(two[:half], "fsdp", flip_pairs(parts, 1))
+    tail = lax.ppermute(one[half:], "fsdp", flip_pairs(parts, 2))
+    return [block, one, two, (head, tail)]
 
 
 def send_flips(pieces, parts):
@@ -458,21 +532,6 @@
     return pieces
 
 
-def to_columns(blocks, seq_parts, me_seq):
-    fsdp_parts = blocks.shape[0]
-    ratio = seq_parts // fsdp_parts
-    out = jnp.zeros_like(blocks)
-    for r in range(fsdp_parts):
-        pairs = [
-            (s, ratio * (s % fsdp_parts ^ r) + s // fsdp_parts) for s in range(seq_parts)
-        ]
-        piece = lax.dynamic_index_in_dim(blocks, me_seq % fsdp_parts ^ r, 0, keepdims=False)
-        got = lax.ppermute(piece, "seq", pairs)
-        out = lax.dynamic_update_index_in_dim(out, got, me_seq // ratio ^ r, 0)
-    _, count, part, rows = blocks.shape
-    return out.transpose(1, 0, 2, 3).reshape(count, fsdp_parts * part, rows)
-
-
 def on_device(
     tokens,
     attn_gain,
@@ -502,6 +561,8 @@
     ratio = S // F
     if ratio != 2 or F & (F - 1):
         raise ValueError("unsupported mesh")
+    ff_block = F * ff_rows // S
+    ff_part = ff_block // F
     even = me % 2 == 0
     core = (me % 2).reshape(1).astype(jnp.int32)
     mate = flip_pairs(S, 1)
@@ -509,8 +570,12 @@
 
     def natural(pieces):
         out = jnp.zeros((F, *pieces[0].shape), pieces[0].dtype)
+        rest = (0,) * (pieces[0].ndim - 1)
         for j, piece in enumerate(pieces):
-            out = lax.dynamic_update_index_in_dim(out, piece, here ^ j, 0)
+            start = 0
+            for part in piece if isinstance(piece, tuple) else (piece,):
+                out = lax.dynamic_update_slice(out, part[None], (here ^ j, start, *rest))
+                start += part.shape[0]
         return out
 
     x_all = lax.all_gather(tokens, "seq", axis=0).reshape(all_rows, width)
@@ -527,69 +592,67 @@
         ],
         axis=1,
     )
-    w_qkv = natural(gather_flips(qkv_part, F)).reshape(width, 3 * head_width)
-
-    fetched = jnp.stack(
-        [
-            jnp.where(
-                even,
-                gate_weight[:, f * ff_rows : (f + 1) * ff_rows],
-                up_weight[:, f * ff_rows : (f + 1) * ff_rows],
-            )
-            for f in range(F)
-        ]
-    )
-    fetched = after(fetched, qkv_part)
+    qkv_near = relay_near(qkv_part, F)
+    qkv_got = relay_far(qkv_part, qkv_near, F)
+    w_qkv = natural(qkv_got).reshape(width, 3 * head_width)
+
+    out_half = lax.dynamic_slice_in_dim(out_weight, me % 2 * head_width, head_width, 0)
+    out_mine = lax.all_gather(out_half, "fsdp", axis=0)
+    fetched = after(pick(core, gate_weight, up_weight, S, F), qkv_near)
     w_mine = lax.all_to_all(fetched, "fsdp", split_axis=0, concat_axis=0, tiled=True)
     w_mine = w_mine.reshape(width, ff_rows)
     w_other = lax.ppermute(w_mine, "seq", mate)
-    out_half = lax.dynamic_slice_in_dim(out_weight, me % 2 * head_width, head_width, 0)
-    out_mine = lax.all_gather(out_half, "fsdp", axis=0)
 
     tabs = rotary_tables(S * local_len)
     m, a1 = project(x_all, gain1, shift1, w_qkv, bias)
     q, k, v, o = attend(m.reshape(S, seqs, local_len, 3 * head_width), tabs, head_width)
     o_got = lax.all_to_all(o, "seq", split_axis=0, concat_axis=0, tiled=True)
+    dy_own = cotangent.reshape(rows, width)
+    dy_near = relay_near(after(dy_own, o), F)
     out_other = lax.ppermute(out_mine, "seq", mate)
-    dy_own = cotangent.reshape(rows, width)
-    dy_early = after(dy_own, o)
-    dy_pieces = [dy_own]
-    for j in range(1, F - 1):
-        dy_pieces.append(lax.ppermute(dy_early, "fsdp", flip_pairs(F, j)))
     o_got = o_got.reshape(S, rows, head_width)
 
     x_own = tokens.reshape(rows, width)
     x1, a2 = mid(core, o_got, out_mine, out_other, x_own, gain2, shift2)
     a2_all = lax.all_gather(a2, "fsdp", axis=0, tiled=True)
-    dy_pieces.append(lax.ppermute(after(dy_own, a2_all), "fsdp", flip_pairs(F, F - 1)))
-    dy_all = natural(dy_pieces).reshape(F * rows, width)
-
+    dy_got = relay_far(dy_own, after(dy_near, a2_all), F)
     first = nn(a2_all, w_mine)
+    dy_all = natural(dy_got).reshape(F * rows, width)
+    down_half = lax.dynamic_index_in_dim(
+        down_weight.reshape(ratio, F, ff_part, width), me % 2, 0, keepdims=False
+    )
+    down_half = after(down_half, first)
+    down_mine = lax.all_to_all(down_half, "fsdp", split_axis=0, concat_axis=0, tiled=True)
+    down_other = lax.ppermute(down_mine, "seq", mate)
     second = nn(a2_all, w_other)
     g = jnp.where(even, first, second)
     u = jnp.where(even, second, first)
     sig = jax.nn.sigmoid(g)
     silu = g * sig
     hid = (silu * u).astype(bf16)
-    down_grad_part = tn(dy_all, hid).astype(bf16)
-    down_grad = lax.psum_scatter(down_grad_part, "seq", scatter_dimension=0, tiled=True)
-    dh = nt(after(dy_all, down_grad_part), down_weight)
+    down_grad_part = tn(hid, dy_all).astype(bf16)
+    down_grad = lax.psum_scatter(down_grad_part, "seq", scatter_dimension=1, tiled=True)
+    down_mine, down_other, dy_late = after((down_mine, down_other, dy_all), down_grad_part)
+    w_down = jnp.stack(
+        [jnp.where(even, down_mine, down_other), jnp.where(even, down_other, down_mine)], axis=1
+    ).reshape(ff_rows, width)
+    dh = nt(dy_late, w_down)
     dg = (dh * u * sig * (1.0 + g * (1.0 - sig))).astype(bf16)
     du = (dh * silu).astype(bf16)
     d_first = jnp.where(even, dg, du)
     d_second = jnp.where(even, du, dg)
     dn2_part = (nt(d_first, w_mine) + nt(d_second, w_other)).astype(bf16)
     dn2_part = dn2_part.reshape(F, rows, width)
-    dn2_pieces = []
-    for j in range(F):
-        dn2_pieces.append(lax.dynamic_index_in_dim(dn2_part, here ^ j, 0, keepdims=False))
+    dn2_pieces = [
+        lax.dynamic_index_in_dim(dn2_part, here ^ j, 0, keepdims=False) for j in range(F)
+    ]
     dgu = after(jnp.concatenate([dg, du], axis=1), dn2_pieces)
-    for j in range(1, F):
-        dn2_pieces[j] = lax.ppermute(dn2_pieces[j], "fsdp", flip_pairs(F, j))
-    both_part = tn(dgu, a2_all).astype(bf16).reshape(2, ff_rows, width)
+    dn2_pieces = send_flips(dn2_pieces, F)
+    both_part = tn(dgu, a2_all).astype(bf16)
+    both_part = both_part.reshape(2, ff_rows, width)
     both = lax.psum_scatter(both_part, "seq", scatter_dimension=1, tiled=True)
     hid_late = after(hid, both_part)
-    down_part = nn(hid_late, down_weight).astype(bf16)
+    down_part = nn(hid_late, w_down).astype(bf16)
 
     dn2_pieces = after(dn2_pieces, down_part)
     dx1, dxl, do_two, gain2_part, shift2_part = mid_back(
@@ -598,51 +661,59 @@
     do = lax.all_to_all(do_two, "seq", split_axis=0, concat_axis=0, tiled=True)
     do = do.reshape(S, seqs, local_len, head_width)
 
-    dxl_all = natural(gather_flips(dxl, F)).reshape(F * rows, width)
+    dxl_pieces = gather_flips(dxl, F)
     o_got = after(o_got, dxl)
     o_pieces = []
     for j in range(F):
         piece = lax.dynamic_slice_in_dim(o_got, 2 * (here ^ j), 2, 0)
         o_pieces.append(lax.ppermute(piece, "fsdp", flip_pairs(F, j)) if j else piece)
-    o_cols = natural(o_pieces).transpose(1, 0, 2, 3).reshape(2, F * rows, head_width)
-    out_part = jnp.concatenate([tn(dxl_all, o_cols[h]) for h in range(2)], axis=1).astype(bf16)
-
-    dq, dk, dv = attend_back(q, k, v, do, tabs)
-    dm = jnp.concatenate([dq, dk, dv], axis=-1).reshape(all_rows, 3 * head_width)
-    down_part = after(down_part, dm).reshape(F, rows, width)
-    down_pieces = send_flips(
-        [lax.dynamic_index_in_dim(down_part, here ^ j, 0, keepdims=False) for j in range(F)], F
-    )
-    joint_part = back_project(dm, w_qkv, out_part)
-    joint = lax.psum_scatter(joint_part, "seq", scatter_dimension=0, tiled=True)
-    dn1 = joint[:, :width].astype(f32)
-    out_result = joint[:, width:].T.astype(f32)
-    a1_late, both = after((a1, both), joint_part)
+
+    dm_parts = [g.reshape(all_rows, head_width) for g in attend_back(q, k, v, do, tabs)]
+    joint_part = joint(*dm_parts, w_qkv, dxl_pieces, o_pieces)
+    joint_sum = lax.psum_scatter(joint_part, "seq", scatter_dimension=0, tiled=True)
+
+    a1_late, dm_parts, both, down_part = after((a1, dm_parts, both, down_part), joint_part)
+    dm = jnp.concatenate(dm_parts, axis=1)
     both_pieces = to_rows(both, F, here)
     qkv_part_grad = tn(a1_late, dm).astype(bf16)
     qkv_part_grad = qkv_part_grad.reshape(F, shard, 3 * head_width)
     qkv_pieces = [
         lax.dynamic_index_in_dim(qkv_part_grad, here ^ j, 0, keepdims=False) for j in range(F)
     ]
-    dm, dn1_late, x_late, down_grad, both_pieces, down_pieces = after(
-        (dm, joint_part, x_all, down_grad, both_pieces, down_pieces), qkv_pieces
-    )
+    down_part, down_grad = after((down_part, down_grad), qkv_pieces)
     qkv_got = send_flips(qkv_pieces, F)
-    qkv_sum = total(qkv_got).astype(bf16)
-    qkv_result = contiguous_thirds(qkv_sum.reshape(shard, 3, head_width), S, me).astype(f32)
-    both = to_columns(natural(both_pieces), S, me).astype(f32)
-    gate_result, up_result = both[0].T, both[1].T
-    layer_out = (x1 + total(down_pieces)).astype(bf16).reshape(tokens.shape)
-    down_result = down_grad.T.astype(f32)
-
-    bias_part = jnp.sum(dm, axis=0, dtype=f32).reshape(3, 1, head_width)
-    bias_full = lax.dynamic_update_slice_in_dim(
-        jnp.zeros((3, S, head_width), f32), bias_part, me, 1
-    ).reshape(3 * width)
+    down_grad = down_grad.reshape(F, ratio * ff_part, head_width)
+    down_grad_pieces = send_flips(
+        [lax.dynamic_index_in_dim(down_grad, here ^ j, 0, keepdims=False) for j in range(F)], F
+    )
+    down_part = down_part.reshape(F, rows, width)
+    down_pieces = send_flips(
+        [lax.dynamic_index_in_dim(down_part, here ^ j, 0, keepdims=False) for j in range(F)], F
+    )
+    dm_late, dn1_late, x_late = after((dm, joint_part, x_all), qkv_pieces)
     xh_all, _ = norm_stats(x_late.astype(f32))
     dn1_late = dn1_late[:, :width].astype(f32)
     attn_gain_part = jnp.sum(dn1_late * xh_all, axis=0)
     attn_shift_part = jnp.sum(dn1_late, axis=0)
+    qkv_got = after(qkv_got, attn_gain_part)
+    qkv_sum = total(qkv_got).astype(bf16)
+    qkv_result = contiguous_thirds(qkv_sum.reshape(shard, 3, head_width), S, me).astype(f32)
+    both_pieces, down_grad_pieces, down_pieces = after(
+        (both_pieces, down_grad_pieces, down_pieces), qkv_sum
+    )
+    both = natural(both_pieces).transpose(1, 0, 2, 3).reshape(2, ff_block, shard).astype(f32)
+    gate_result, up_result = both[0].T, both[1].T
+    down_result = natural(down_grad_pieces).reshape(F, ratio, ff_part, head_width)
+    down_result = down_result.transpose(1, 0, 2, 3).reshape(ff_rows, head_width).astype(f32)
+    layer_out = (x1 + total(down_pieces)).astype(bf16).reshape(tokens.shape)
+    joint_sum = after(joint_sum, qkv_sum, layer_out, gate_result, up_result, down_result)
+    dn1 = joint_sum[:, :width].astype(f32)
+    out_result = joint_sum[:, width:].T.astype(f32)
+
+    bias_part = jnp.sum(dm_late, axis=0, dtype=f32).reshape(3, 1, head_width)
+    bias_full = lax.dynamic_update_slice_in_dim(
+        jnp.zeros((3, S, head_width), f32), bias_part, me, 1
+    ).reshape(3 * width)
     small_parts = [
         attn_gain_part,
         attn_shift_part,
@@ -653,7 +724,9 @@
     ]
     packed = jnp.concatenate([p.reshape(devices, -1) for p in small_parts], axis=1)
     packed = lax.all_to_all(packed, MESH_AXES, split_axis=0, concat_axis=0, tiled=True)
-    packed = jnp.sum(packed, axis=0)
+    xh, r = norm_stats(x_own.astype(f32))
+    tokens_grad = (dx1 + norm_back(dn1, xh, r, gain1)).reshape(tokens.shape)
+    packed = jnp.sum(after(packed, tokens_grad), axis=0)
     results = []
     start = 0
     for p in small_parts:
@@ -662,8 +735,6 @@
         start += size
     gain1_result, shift1_result, bias_result, value_result, gain2_result, shift2_result = results
 
-    xh, r = norm_stats(x_own.astype(f32))
-    tokens_grad = (dx1 + norm_back(dn1, xh, r, gain1)).reshape(tokens.shape)
     return (
         layer_out,
         tokens_grad,

time: 856 us -> 847 us (0.989)
  local copies, waits for them, and re-layouts: 71.8 us -> 105 us
  starting transfers between devices: 96.1 us -> 72.9 us
  waiting for transfers between devices: 398 us -> 375 us
    ppermute x9 -> x6, waiting for transfers between devices: 29.9 us -> 0.02 us  [gather_flips(): lax.ppermute(block, 'fsdp', flip_pairs(parts, j))]
    ppermute x10 -> x9, starting transfers between devices: 39.2 us -> 10.2 us  [the longest x4 4.95 us: relay_near(): return [lax.ppermute(block, 'fsdp', flip_pairs(parts, j)) for j in (1, 2)]]
    all_to_all x0 -> x1, waiting for transfers between devices: none -> 14.9 us  [on_device(): lax.all_to_all(down_half, 'fsdp', split_axis=0, concat_axis=0, tiled=True)]
    unnamed x107 -> x115, local copies, waits for them, and re-layouts: 15.4 us -> 28.3 us
    all_gather x1, waiting for transfers between devices: 26.2 us -> 13.4 us  [on_device(): out_mine = lax.all_gather(out_half, 'fsdp', axis=0)]
    ppermute x10 -> x9, waiting for transfers between devices: 64.6 us -> 53.5 us  [the longest x4 40.6 us: relay_near(): return [lax.ppermute(block, 'fsdp', flip_pairs(parts, j)) for j in (1, 2)]]
    ppermute x6 -> x12, waiting for transfers between devices: 34.8 us -> 42.8 us  [send_flips(): lax.ppermute(pieces[j], 'fsdp', flip_pairs(parts, j))]
    pallas_call x1 -> x2, Pallas kernels: 11.3 us -> 17.6 us  [the longest x1 14.5 us: joint(): pl.pallas_call(functools.partial(joint_kernel, count), grid=(parts,), in_...]
  transfers between devices with their start and end apart: 46 -> 49, of which waited for: 17 -> 18; matrix products, arithmetic and copies ran while one was open for 18% -> 20% of each run, Pallas kernels for 10% -> 11%
where the time goes in v3:
time: 847 us; the launch traced here: 837 us
  waiting for transfers between devices  375 us (44%)
  matrix products  113 us (13%)
  local copies, waits for them, and re-layouts  105 us (12%)
  Pallas kernels  94.4 us (11%)
  starting transfers between devices  72.9 us (9%)
  other arithmetic  52.2 us (6%)
  between operations  25 us (3%)
    all_gather x1, waiting for transfers between devices, on_device(): x_all = lax.all_gather(tokens, 'seq', axis=0).reshape(all_rows, width)  83.5 us
    all_to_all x1, waiting for transfers between devices, on_device(): lax.all_to_all(fetched, 'fsdp', split_axis=0, concat_axis=0, tiled=True)  81.3 us
    ppermute x3, waiting for transfers between devices, on_device(): lax.ppermute(piece, 'fsdp', flip_pairs(F, j))  47.4 us
    ppermute x12, waiting for transfers between devices, send_flips(): lax.ppermute(pieces[j], 'fsdp', flip_pairs(parts, j))  42.8 us
    ppermute x4, waiting for transfers between devices, relay_near(): return [lax.ppermute(block, 'fsdp', flip_pairs(parts, j)) for j in (1, 2)]  40.6 us
    dot_general x3, matrix products, nt(): lax.dot_general(a, b, (((1,), (1,)), ((), ())), preferred_element_type=jn...  39.8 us
    dot_general x3, matrix products, nn(): lax.dot_general(a, b, (((1,), (0,)), ((), ())), preferred_element_type=jn...  36.9 us
    dot_general x3, matrix products, tn(): lax.dot_general(a, b, (((0,), (0,)), ((), ())), preferred_element_type=jn...  36.1 us
  transfers between devices with their start and end apart: 49, of which 18 were waited for; matrix products, arithmetic and copies ran while one was open for 20% of the time, Pallas kernels for 11%

profile of v3, /device:TPU:0, one launch (start us, length us, event | category | flops | bytes accessed | tf_op | source)
XLA Modules:
  0.0 837.3 jit_solution(5391991335088054132)
XLA Ops:
  29.0 19.5 %collective-permute-done.3 = bf16[512,768]{1,0:T(8,128)(2,1)S(1)} collective-permute-done((bf16[512,768]{1,0:T(8,128)(2,1)}, bf16[512,768]{1,0:T(8,128)(2,1)S(1)}, u32[]{:S(2)}, u32[]{:S(2)}) %collective-permute-start.3) | collective-permute-done | bytes 786464 | tf_op jit(solution)/shard_map/ppermute | solution.py:459
  55.9 13.0 %collective-permute-done.5 = bf16[256,768]{1,0:T(8,128)(2,1)S(1)} collective-permute-done((bf16[256,768]{1,0:T(8,128)(2,1)S(1)}, bf16[256,768]{1,0:T(8,128)(2,1)S(1)}, u32[]{:S(2)}, u32[]{:S(2)}) %collective-permute-start.5) | collective-permute-done | bytes 393248 | tf_op jit(solution)/shard_map/ppermute | solution.py:467
  69.6 13.4 %all-gather.10.cloned.1.call-done = bf16[1024,2048]{1,0:T(8,128)(2,1)} async-done(((bf16[256,2048]{1,0:T(8,128)(2,1)}), bf16[1024,2048]{1,0:T(8,128)(2,1)}) %all-gather.10.cloned.1.call-update) | async-done | bytes 4194320 | tf_op jit(solution)/shard_map/all_gather | solution.py:600
  83.8 83.5 %all-gather.8.cloned.1.call-done = bf16[16,128,2048]{2,1,0:T(8,128)(2,1)} async-done(((bf16[2,128,2048]{2,1,0:T(8,128)(2,1)}), bf16[16,128,2048]{2,1,0:T(8,128)(2,1)}) %all-gather.8.cloned.1.call-update) | async-done | bytes 8388624 | tf_op jit(solution)/shard_map/all_gather | solution.py:581
  167.3 15.7 %project.1 = (f32[2048,768]{1,0:T(8,128)}, bf16[2048,2048]{1,0:T(8,128)(2,1)}) custom-call(bf16[2048,2048]{1,0:T(8,128)(2,1)} %bitcast.192, f32[1,2048]{1,0:T(1,128)S(1)} %bitcast.190, f32[1,2048]{1,0:T(1,128)S(1)} %bitcast.189, bf16[2048,768]{1,0:T(8,128)(2,1)} %bitcast.7.w_ref.refs_3_, f32[1,768]{1,0:T(1,128)S(1)} %bitcast.191), custom_call_target="tpu_custom_call" | custom-call | flops 6442450944 | bytes 26214400 | tf_op jit(solution)/shard_map/project/pallas_call | solution.py:498
  183.0 17.9 %attend.1 = (bf16[8,2,128,256]{3,2,1,0:T(8,128)(2,1)S(1)}, bf16[8,2,128,256]{3,2,1,0:T(8,128)(2,1)S(1)}, bf16[8,2,128,256]{3,2,1,0:T(8,128)(2,1)S(1)}, bf16[8,2,128,256]{3,2,1,0:T(8,128)(2,1)}) custom-call(f32[8,2,128,768]{3,2,1,0:T(8,128)} %bitcast.198, f32[8,2,128,768]{3,2,1,0:T(8,128)} %bitcast.199, f32[8,2,128,768]{3,2,1,0:T(8,128)} %bitcast.200, ...), custom_call_target="tpu_custom_call" | custom-call | flops 2147483648 | bytes 10485760 | tf_op jit(solution)/shard_map/attend/pallas_call | solution.py:167
  217.3 15.6 %all-to-all-done = bf16[8,2,128,256]{3,2,1,0:T(8,128)(2,1)S(1)} async-done(((bf16[8,2,128,256]{3,2,1,0:T(8,128)(2,1)}), bf16[8,2,128,256]{3,2,1,0:T(8,128)(2,1)S(1)}, u32[]{:S(2)}, u32[]{:S(2)}) %all-to-all-start) | async-done | bytes 1048608 | tf_op jit(solution)/shard_map/all_to_all | solution.py:609
  238.7 7.2 mid.1
  247.2 81.3 %all-to-all-done.1 = bf16[4,512,1408]{2,1,0:T(8,128)(2,1)} async-done(((bf16[4,512,1408]{2,1,0:T(8,128)(2,1)}), bf16[4,512,1408]{2,1,0:T(8,128)(2,1)}, u32[]{:S(2)}, u32[]{:S(2)}) %all-to-all-start.1) | async-done | bytes 5767200 | tf_op jit(solution)/shard_map/all_to_all | solution.py:602
  337.4 21.0 %collective-permute-done.10 = bf16[256,2048]{1,0:T(8,128)(2,1)} collective-permute-done((bf16[256,2048]{1,0:T(8,128)(2,1)}, bf16[256,2048]{1,0:T(8,128)(2,1)}, u32[]{:S(2)}, u32[]{:S(2)}) %collective-permute-start.10) | collective-permute-done | bytes 1048608 | tf_op jit(solution)/shard_map/ppermute | solution.py:459
  364.3 11.7 %fusion.19 = f32[1024,1408]{1,0:T(8,128)} fusion(bf16[1024,2048]{1,0:T(8,128)(2,1)} %all-gather.6.cloned.1.call-done, bf16[2048,1408]{1,0:T(8,128)(2,1)} %bitcast.15), kind=kOutput, calls=%fused_computation.130 | convolution fusion | flops 5905580032 | bytes 15728640 | tf_op jit(solution)/shard_map/dot_general | solution.py:18
  380.6 13.7 %multiply_convert_fusion.2 = (bf16[1024,1408]{1,0:T(8,128)(2,1)}, f32[1024,1408]{1,0:T(8,128)}) fusion(f32[1024,1408]{1,0:T(8,128)} %fusion.19, pred[]{:T(512)S(6)} %eq.46, bf16[1024,2048]{1,0:T(8,128)(2,1)} %all-gather.6.cloned.1.call-done, bf16[2048,1408]{1,0:T(8,128)(2,1)} %collective-permute-done.13), kind=kOutput, calls=%fused_computation.16 | convolution fusion | flops 5917114368 | bytes 24379392 | tf_op jit(solution)/shard_map/dot_general | solution.py:18
  399.0 14.9 %all-to-all-done.2 = bf16[4,176,2048]{2,1,0:T(8,128)(2,1)} async-done(((bf16[4,176,2048]{2,1,0:T(8,128)(2,1)}), bf16[4,176,2048]{2,1,0:T(8,128)(2,1)}, u32[]{:S(2)}, u32[]{:S(2)}) %all-to-all-start.2) | async-done | bytes 2883616 | tf_op jit(solution)/shard_map/all_to_all | solution.py:625
  417.7 10.5 %convolution_convert_fusion.1 = bf16[1408,2048]{1,0:T(8,128)(2,1)} fusion(bf16[1024,1408]{1,0:T(8,128)(2,1)} %get-tuple-element.90, bf16[1024,2048]{1,0:T(8,128)(2,1)} %bitcast.22), kind=kOutput, calls=%fused_computation.10 | convolution fusion | flops 5908463616 | bytes 12845056 | tf_op jit(solution)/shard_map/dot_general | solution.py:26
  431.8 15.9 %multiply_convert_fusion = (bf16[1024,1408]{1,0:T(8,128)(2,1)S(1)}, bf16[1024,1408]{1,0:T(8,128)(2,1)}) fusion(f32[1024,1408]{1,0:T(8,128)} %fusion.19, f32[1024,1408]{1,0:T(8,128)} %get-tuple-element.244, pred[]{:T(512)S(6)} %eq.46, bf16[1024,2048]{1,0:T(8,128)(2,1)} %bitcast.22, bf16[1408,2048]{1,0:T(8,128)(2,1)S(1)} %bitcast.205), kind=kOutput, calls=%fused_computation.14 | convolution fusion | flops 5927206912 | bytes 27262976 | tf_op jit(solution)/shard_map/dot_general | solution.py:22
  447.7 13.0 %fusion.6 = f32[1024,2048]{1,0:T(8,128)} fusion(bf16[2048,1408]{1,0:T(8,128)(2,1)} %bitcast.15, bf16[1024,1408]{1,0:T(8,128)(2,1)} %get-tuple-element.190, bf16[1024,1408]{1,0:T(8,128)(2,1)S(1)} %get-tuple-element.189, pred[]{:T(512)S(6)} %eq.46), kind=kOutput, calls=%fused_computation.23 | convolution fusion | flops 5907021824 | bytes 19922944 | tf_op jit(solution)/shard_map/dot_general | solution.py:22
  462.9 10.9 %add_convert_fusion = bf16[1024,2048]{1,0:T(8,128)(2,1)S(1)} fusion(f32[1024,2048]{1,0:T(8,128)} %fusion.6, bf16[2048,1408]{1,0:T(8,128)(2,1)} %collective-permute-done.13, bf16[1024,1408]{1,0:T(8,128)(2,1)} %copy-done.29, bf16[1024,1408]{1,0:T(8,128)(2,1)} %get-tuple-element.190, pred[]{:T(512)S(6)} %eq.46), kind=kOutput, calls=%fused_computation.9 | convolution fusion | flops 5911216128 | bytes 24117248 | tf_op jit(solution)/shard_map/dot_general | solution.py:22
  477.5 14.7 %convolution_convert_fusion = bf16[2816,2048]{1,0:T(8,128)(2,1)} fusion(bf16[1024,2816]{1,0:T(8,128)(2,1)S(1)} %pad_maximum_fusion.1, bf16[1024,2048]{1,0:T(8,128)(2,1)S(1)} %copy-done.45), kind=kOutput, calls=%fused_computation.8 | convolution fusion | flops 11816927232 | bytes 21495808 | tf_op jit(solution)/shard_map/dot_general | solution.py:26
  496.3 11.5 %convolution_convert_fusion.2 = bf16[1024,2048]{1,0:T(8,128)(2,1)} fusion(bf16[1024,1408]{1,0:T(8,128)(2,1)} %get-tuple-element.90, bf16[1408,2048]{1,0:T(8,128)(2,1)} %bitcast.206), kind=kOutput, calls=%fused_computation.19 | convolution fusion | flops 5907677184 | bytes 12845056 | tf_op jit(solution)/shard_map/dot_general | solution.py:18
  507.8 12.2 %collective-permute-done.16.refs_3_ = bf16[256,2048]{1,0:T(8,128)(2,1)S(1)} collective-permute-done((bf16[256,2048]{1,0:T(8,128)(2,1)}, bf16[256,2048]{1,0:T(8,128)(2,1)S(1)}, u32[]{:S(2)}, u32[]{:S(2)}) %collective-permute-start.16) | collective-permute-done | bytes 1048608 | tf_op jit(solution)/shard_map/ppermute | solution.py:474
  520.0 21.5 %collective-permute-done.15.refs_2_ = bf16[256,2048]{1,0:T(8,128)(2,1)S(1)} collective-permute-done((bf16[256,2048]{1,0:T(8,128)(2,1)}, bf16[256,2048]{1,0:T(8,128)(2,1)S(1)}, u32[]{:S(2)}, u32[]{:S(2)}) %collective-permute-start.15) | collective-permute-done | bytes 1048608 | tf_op jit(solution)/shard_map/ppermute | solution.py:474
  542.9 11.1 %mid_back.1 = (f32[256,2048]{1,0:T(8,128)}, bf16[256,2048]{1,0:T(8,128)(2,1)}, bf16[8,256,256]{2,1,0:T(8,128)(2,1)}, f32[1,2048]{1,0:T(1,128)}, f32[1,2048]{1,0:T(1,128)}) custom-call(s32[1]{0:T(128)} %bitcast.core_ref, bf16[256,2048]{1,0:T(8,128)(2,1)} %get-tuple-element.91.refs_0_, bf16[256,2048]{1,0:T(8,128)(2,1)} %copy-done.32, ...), custom_call_target="tpu_custom_call" | custom-call | flops 2147483648 | bytes 18874368 | tf_op jit(solution)/shard_map/mid_back/pallas_call | solution.py:280
  565.6 47.4 %collective-permute-done.22.refs_11_ = bf16[2,256,256]{2,1,0:T(8,128)(2,1)S(1)} collective-permute-done((bf16[2,256,256]{2,1,0:T(8,128)(2,1)S(1)}, bf16[2,256,256]{2,1,0:T(8,128)(2,1)S(1)}, u32[]{:S(2)}, u32[]{:S(2)}) %collective-permute-start.22) | collective-permute-done | bytes 262176 | tf_op jit(solution)/shard_map/ppermute | solution.py:669
  618.3 24.9 %attend_back.1 = (bf16[8,2,128,256]{3,2,1,0:T(8,128)(2,1)S(1)}, bf16[8,2,128,256]{3,2,1,0:T(8,128)(2,1)S(1)}, bf16[8,2,128,256]{3,2,1,0:T(8,128)(2,1)S(1)}) custom-call(bf16[8,2,128,256]{3,2,1,0:T(8,128)(2,1)S(1)} %get-tuple-element.77.q_ref, bf16[8,2,128,256]{3,2,1,0:T(8,128)(2,1)} %copy-done.20, bf16[8,2,128,256]{3,2,1,0:T(8,128)(2,1)} %copy-done.21, ...), custom_call_target="tpu_custom_call" | custom-call | flops 5368709120 | bytes 7340032 | tf_op jit(solution)/shard_map/attend_back/pallas_call | solution.py:187
  643.3 14.5 %joint.1 = bf16[2048,2560]{1,0:T(8,128)(2,1)} custom-call(bf16[2048,256]{1,0:T(8,128)(2,1)S(1)} %bitcast.184, bf16[2048,256]{1,0:T(8,128)(2,1)S(1)} %bitcast.182, bf16[2048,256]{1,0:T(8,128)(2,1)S(1)} %bitcast.180, bf16[2048,768]{1,0:T(8,128)(2,1)} %bitcast.7.w_ref.refs_3_, bf16[256,2048]{1,0:T(8,128)(2,1)S(1)} %copy-done.22, ...), custom_call_target="tpu_custom_call" | custom-call | flops 8589934592 | bytes 26214400 | tf_op jit(solution)/shard_map/joint/pallas_call | solution.py:341
  672.9 11.0 %convolution_convert_fusion.3 = bf16[2048,768]{1,0:T(8,128)(2,1)S(1)} fusion(bf16[2048,2048]{1,0:T(8,128)(2,1)} %get-tuple-element.103, bf16[2048,768]{1,0:T(8,128)(2,1)S(1)} %constant_dynamic-update-slice_fusion), kind=kOutput, calls=%fused_computation.20 | convolution fusion | flops 6444023808 | bytes 14680064 | tf_op jit(solution)/shard_map/dot_general | solution.py:26
  701.6 5.7 convert_reduce_fusion
  707.2 5.8 fusion.2
  713.1 7.6 convert_reduce_fusion.1
  720.7 9.0 %collective-permute-done.33 = bf16[512,768]{0,1:T(8,128)(2,1)} collective-permute-done((bf16[512,768]{0,1:T(8,128)(2,1)}, bf16[512,768]{0,1:T(8,128)(2,1)}, u32[]{:S(2)}, u32[]{:S(2)}) %collective-permute-start.33) | collective-permute-done | bytes 786464 | tf_op jit(solution)/shard_map/ppermute | solution.py:474
  784.5 6.9 all-to-all-done.4
  796.9 6.7 collective-permute-done.24
  (320 shorter events, 223.1 us)
Async XLA Ops:
  7.2 75.8 %all-gather.10.cloned.1.call-start = ((), (), s32[]{:S(2)}) async-start(), calls=%async_computation.13 | async-start | bytes 5242880 | tf_op jit(solution)/shard_map/all_gather | solution.py:600
  9.9 157.4 %all-gather.8.cloned.1.call-start = ((), (), s32[]{:S(2)}) async-start(), calls=%async_computation.12 | async-start | bytes 9437184 | tf_op jit(solution)/shard_map/all_gather | solution.py:581
  18.3 30.2 %collective-permute-start.3 = (bf16[512,768]{1,0:T(8,128)(2,1)}, bf16[512,768]{1,0:T(8,128)(2,1)S(1)}, u32[]{:S(2)}, u32[]{:S(2)}) collective-permute-start(bf16[512,768]{1,0:T(8,128)(2,1)} %pad_maximum_fusion.2), channel_id=1, source_target_pairs={{0,1},{1,0},{2,3},{3,2},{4,5},{5,4},{6,7},{7,6},{8,9},{9,8},{10,11... | collective-permute-start | bytes 2359304 | tf_op jit(solution)/shard_map/ppermute | solution.py:459
  48.5 34.5 %collective-permute-start.6 = (bf16[256,768]{1,0:T(8,128)(2,1)S(1)}, bf16[256,768]{1,0:T(8,128)(2,1)S(1)}, u32[]{:S(2)}, u32[]{:S(2)}) collective-permute-start(bf16[256,768]{1,0:T(8,128)(2,1)S(1)} %slice.95), channel_id=1, source_target_pairs={{0,2},{1,3},{2,0},{3,1},{4,6},{5,7},{6,4},{7,5},{8,10},{9,11},{10,... | collective-permute-start | bytes 1179656 | tf_op jit(solution)/shard_map/ppermute | solution.py:468
  83.0 155.6 %collective-permute-start.7 = (bf16[4,256,2048]{2,1,0:T(8,128)(2,1)}, bf16[4,256,2048]{2,1,0:T(8,128)(2,1)}, u32[]{:S(2)}, u32[]{:S(2)}) collective-permute-start(bf16[4,256,2048]{2,1,0:T(8,128)(2,1)} %bitcast.201), channel_id=1, source_target_pairs={{0,4},{4,0},{8,12},{12,8},{16,20},{20,16},{24,28},{28,24},{1,5},{5... | collective-permute-start | bytes 12582920 | tf_op jit(solution)/shard_map/ppermute | solution.py:612
  202.9 30.1 %all-to-all-start = ((bf16[8,2,128,256]{3,2,1,0:T(8,128)(2,1)}), bf16[8,2,128,256]{3,2,1,0:T(8,128)(2,1)S(1)}, u32[]{:S(2)}, u32[]{:S(2)}) async-start(bf16[8,2,128,256]{3,2,1,0:T(8,128)(2,1)} %get-tuple-element.74), calls=%async_computation | async-start | bytes 2097152 | tf_op jit(solution)/shard_map/all_to_all | solution.py:609
  232.9 95.5 %all-to-all-start.1 = ((bf16[4,512,1408]{2,1,0:T(8,128)(2,1)}), bf16[4,512,1408]{2,1,0:T(8,128)(2,1)}, u32[]{:S(2)}, u32[]{:S(2)}) async-start(bf16[4,512,1408]{2,1,0:T(8,128)(2,1)} %copy-done.4), calls=%async_computation.1 | async-start | bytes 11534336 | tf_op jit(solution)/shard_map/all_to_all | solution.py:602
  238.1 120.4 %all-gather.6.cloned.1.call-start = ((), (), s32[]{:S(2)}) async-start(), calls=%async_computation.8 | async-start | bytes 5242880 | tf_op jit(solution)/shard_map/all_gather | solution.py:617
  328.5 52.2 %collective-permute-start.13 = (bf16[2048,1408]{1,0:T(8,128)(2,1)}, bf16[2048,1408]{1,0:T(8,128)(2,1)}, u32[]{:S(2)}, u32[]{:S(2)}) collective-permute-start(bf16[2048,1408]{1,0:T(8,128)(2,1)} %bitcast.15), channel_id=1, source_target_pairs={{0,4},{4,0},{8,12},{12,8},{16,20},{20,16},{24,28},{28,24},{1,5},{5... | collective-permute-start | bytes 17301512 | tf_op jit(solution)/shard_map/ppermute | solution.py:604
  362.3 51.6 %collective-permute-start.11 = (bf16[128,2048]{1,0:T(8,128)(2,1)}, bf16[128,2048]{1,0:T(8,128)(2,1)}, u32[]{:S(2)}, u32[]{:S(2)}) collective-permute-start(bf16[128,2048]{1,0:T(8,128)(2,1)} %slice.77), channel_id=1, source_target_pairs={{0,1},{1,0},{2,3},{3,2},{4,5},{5,4},{6,7},{7,6},{8,9},{9,8},{10,11... | collective-permute-start | bytes 1572872 | tf_op jit(solution)/shard_map/ppermute | solution.py:467
  363.7 52.1 %collective-permute-start.12 = (bf16[128,2048]{1,0:T(8,128)(2,1)}, bf16[128,2048]{1,0:T(8,128)(2,1)}, u32[]{:S(2)}, u32[]{:S(2)}) collective-permute-start(bf16[128,2048]{1,0:T(8,128)(2,1)} %slice.78), channel_id=1, source_target_pairs={{0,2},{1,3},{2,0},{3,1},{4,6},{5,7},{6,4},{7,5},{8,10},{9,11},{10,... | collective-permute-start | bytes 1572872 | tf_op jit(solution)/shard_map/ppermute | solution.py:468
  375.9 37.9 %all-to-all-start.2 = ((bf16[4,176,2048]{2,1,0:T(8,128)(2,1)}), bf16[4,176,2048]{2,1,0:T(8,128)(2,1)}, u32[]{:S(2)}, u32[]{:S(2)}) async-start(bf16[4,176,2048]{2,1,0:T(8,128)(2,1)} %dynamic-slice_bitcast_fusion), calls=%async_computation.2 | async-start | bytes 5767168 | tf_op jit(solution)/shard_map/all_to_all | solution.py:625
  380.6 288.3 %reduce-scatter.4.cloned.1.call-start = ((), (), s32[]{:S(2)}) async-start(), calls=%async_computation.9 | async-start | bytes 12976128 | tf_op jit(solution)/shard_map/reduce_scatter | solution.py:653
  492.2 204.9 %reduce-scatter.6.cloned.1.call-start = ((), (), s32[]{:S(2)}) async-start(), calls=%async_computation.10 | async-start | bytes 6488064 | tf_op jit(solution)/shard_map/reduce_scatter | solution.py:634
  494.3 47.3 %collective-permute-start.15 = (bf16[256,2048]{1,0:T(8,128)(2,1)}, bf16[256,2048]{1,0:T(8,128)(2,1)S(1)}, u32[]{:S(2)}, u32[]{:S(2)}) collective-permute-start(bf16[256,2048]{1,0:T(8,128)(2,1)} %get-tuple-element.201), channel_id=1, source_target_pairs={{0,2},{1,3},{2,0},{3,1},{4,6},{5,7},{6,4},{7,5},{8,10},{9,11},{10,... | collective-permute-start | bytes 3145736 | tf_op jit(solution)/shard_map/ppermute | solution.py:474
  495.8 45.9 %collective-permute-start.14 = (bf16[256,2048]{1,0:T(8,128)(2,1)}, bf16[256,2048]{1,0:T(8,128)(2,1)S(1)}, u32[]{:S(2)}, u32[]{:S(2)}) collective-permute-start(bf16[256,2048]{1,0:T(8,128)(2,1)} %get-tuple-element.202), channel_id=1, source_target_pairs={{0,1},{1,0},{2,3},{3,2},{4,5},{5,4},{6,7},{7,6},{8,9},{9,8},{10,11... | collective-permute-start | bytes 3145736 | tf_op jit(solution)/shard_map/ppermute | solution.py:474
  554.0 61.2 %all-to-all-start.3 = ((bf16[8,256,256]{2,1,0:T(8,128)(2,1)}), bf16[8,256,256]{2,1,0:T(8,128)(2,1)}, u32[]{:S(2)}, u32[]{:S(2)}) async-start(bf16[8,256,256]{2,1,0:T(8,128)(2,1)} %get-tuple-element.95), calls=%async_computation.3 | async-start | bytes 2097152 | tf_op jit(solution)/shard_map/all_to_all | solution.py:661
  558.2 261.1 %reduce-scatter.8.cloned.1.call-start = ((), (), s32[]{:S(2)}) async-start(), calls=%async_computation.11 | async-start | bytes 11796480 | tf_op jit(solution)/shard_map/reduce_scatter | solution.py:673
  558.3 85.0 %collective-permute-start.19 = (bf16[256,2048]{1,0:T(8,128)(2,1)}, bf16[256,2048]{1,0:T(8,128)(2,1)}, u32[]{:S(2)}, u32[]{:S(2)}) collective-permute-start(bf16[256,2048]{1,0:T(8,128)(2,1)} %get-tuple-element.99.refs_4_), channel_id=1, source_target_pairs={{0,3},{1,2},{2,1},{3,0},{4,7},{5,6},{6,5},{7,4},{8,11},{9,10},{10,... | collective-permute-start | bytes 3145736 | tf_op jit(solution)/shard_map/ppermute | solution.py:453
  559.8 83.5 %collective-permute-start.18 = (bf16[256,2048]{1,0:T(8,128)(2,1)}, bf16[256,2048]{1,0:T(8,128)(2,1)}, u32[]{:S(2)}, u32[]{:S(2)}) collective-permute-start(bf16[256,2048]{1,0:T(8,128)(2,1)} %get-tuple-element.99.refs_4_), channel_id=1, source_target_pairs={{0,2},{1,3},{2,0},{3,1},{4,6},{5,7},{6,4},{7,5},{8,10},{9,11},{10,... | collective-permute-start | bytes 3145736 | tf_op jit(solution)/shard_map/ppermute | solution.py:453
  561.3 82.0 %collective-permute-start.17 = (bf16[256,2048]{1,0:T(8,128)(2,1)}, bf16[256,2048]{1,0:T(8,128)(2,1)}, u32[]{:S(2)}, u32[]{:S(2)}) collective-permute-start(bf16[256,2048]{1,0:T(8,128)(2,1)} %get-tuple-element.99.refs_4_), channel_id=1, source_target_pairs={{0,1},{1,0},{2,3},{3,2},{4,5},{5,4},{6,7},{7,6},{8,9},{9,8},{10,11... | collective-permute-start | bytes 3145736 | tf_op jit(solution)/shard_map/ppermute | solution.py:453
  562.7 50.3 %collective-permute-start.22 = (bf16[2,256,256]{2,1,0:T(8,128)(2,1)S(1)}, bf16[2,256,256]{2,1,0:T(8,128)(2,1)S(1)}, u32[]{:S(2)}, u32[]{:S(2)}) collective-permute-start(bf16[2,256,256]{2,1,0:T(8,128)(2,1)S(1)} %get-tuple-element.214), channel_id=1, source_target_pairs={{0,3},{1,2},{2,1},{3,0},{4,7},{5,6},{6,5},{7,4},{8,11},{9,10},{10,... | collective-permute-start | bytes 786440 | tf_op jit(solution)/shard_map/ppermute | solution.py:669
  564.1 79.1 %collective-permute-start.21 = (bf16[2,256,256]{2,1,0:T(8,128)(2,1)}, bf16[2,256,256]{2,1,0:T(8,128)(2,1)}, u32[]{:S(2)}, u32[]{:S(2)}) collective-permute-start(bf16[2,256,256]{2,1,0:T(8,128)(2,1)} %get-tuple-element.215), channel_id=1, source_target_pairs={{0,2},{1,3},{2,0},{3,1},{4,6},{5,7},{6,4},{7,5},{8,10},{9,11},{10,... | collective-permute-start | bytes 786440 | tf_op jit(solution)/shard_map/ppermute | solution.py:669
  671.3 80.9 %collective-permute-start.25 = (bf16[2,176,512]{2,1,0:T(8,128)(2,1)}, bf16[2,176,512]{2,1,0:T(8,128)(2,1)}, u32[]{:S(2)}, u32[]{:S(2)}) collective-permute-start(bf16[2,176,512]{2,1,0:T(8,128)(2,1)} %get-tuple-element.210), channel_id=1, source_target_pairs={{0,3},{1,2},{2,1},{3,0},{4,7},{5,6},{6,5},{7,4},{8,11},{9,10},{10,... | collective-permute-start | bytes 1081352 | tf_op jit(solution)/shard_map/ppermute | solution.py:531
  691.9 37.9 %collective-permute-start.33 = (bf16[512,768]{0,1:T(8,128)(2,1)}, bf16[512,768]{0,1:T(8,128)(2,1)}, u32[]{:S(2)}, u32[]{:S(2)}) collective-permute-start(bf16[512,768]{0,1:T(8,128)(2,1)} %bitcast.224), channel_id=1, source_target_pairs={{0,2},{1,3},{2,0},{3,1},{4,6},{5,7},{6,4},{7,5},{8,10},{9,11},{10,... | collective-permute-start | bytes 2359304 | tf_op jit(solution)/shard_map/ppermute | solution.py:474
  693.4 37.9 %collective-permute-start.34 = (bf16[512,768]{0,1:T(8,128)(2,1)}, bf16[512,768]{0,1:T(8,128)(2,1)}, u32[]{:S(2)}, u32[]{:S(2)}) collective-permute-start(bf16[512,768]{0,1:T(8,128)(2,1)} %bitcast.223), channel_id=1, source_target_pairs={{0,3},{1,2},{2,1},{3,0},{4,7},{5,6},{6,5},{7,4},{8,11},{9,10},{10,... | collective-permute-start | bytes 2359304 | tf_op jit(solution)/shard_map/ppermute | solution.py:474
  699.1 41.7 %collective-permute-start.28 = (bf16[352,256]{1,0:T(8,128)(2,1)}, bf16[352,256]{1,0:T(8,128)(2,1)S(1)}, u32[]{:S(2)}, u32[]{:S(2)}) collective-permute-start(bf16[352,256]{1,0:T(8,128)(2,1)} %get-tuple-element.224), channel_id=1, source_target_pairs={{0,3},{1,2},{2,1},{3,0},{4,7},{5,6},{6,5},{7,4},{8,11},{9,10},{10,... | collective-permute-start | bytes 540680 | tf_op jit(solution)/shard_map/ppermute | solution.py:474
  741.5 62.5 %collective-permute-start.31 = (bf16[256,2048]{1,0:T(8,128)(2,1)}, bf16[256,2048]{1,0:T(8,128)(2,1)S(1)}, u32[]{:S(2)}, u32[]{:S(2)}) collective-permute-start(bf16[256,2048]{1,0:T(8,128)(2,1)} %get-tuple-element.196), channel_id=1, source_target_pairs={{0,3},{1,2},{2,1},{3,0},{4,7},{5,6},{6,5},{7,4},{8,11},{9,10},{10,... | collective-permute-start | bytes 3145736 | tf_op jit(solution)/shard_map/ppermute | solution.py:474
  742.4 61.6 %collective-permute-start.30 = (bf16[256,2048]{1,0:T(8,128)(2,1)}, bf16[256,2048]{1,0:T(8,128)(2,1)}, u32[]{:S(2)}, u32[]{:S(2)}) collective-permute-start(bf16[256,2048]{1,0:T(8,128)(2,1)} %get-tuple-element.197), channel_id=1, source_target_pairs={{0,2},{1,3},{2,0},{3,1},{4,6},{5,7},{6,4},{7,5},{8,10},{9,11},{10,... | collective-permute-start | bytes 3145736 | tf_op jit(solution)/shard_map/ppermute | solution.py:474
  743.5 60.5 %collective-permute-start.29 = (bf16[256,2048]{1,0:T(8,128)(2,1)}, bf16[256,2048]{1,0:T(8,128)(2,1)}, u32[]{:S(2)}, u32[]{:S(2)}) collective-permute-start(bf16[256,2048]{1,0:T(8,128)(2,1)} %get-tuple-element.198), channel_id=1, source_target_pairs={{0,1},{1,0},{2,3},{3,2},{4,5},{5,4},{6,7},{7,6},{8,9},{9,8},{10,11... | collective-permute-start | bytes 3145736 | tf_op jit(solution)/shard_map/ppermute | solution.py:474
  752.2 40.8 %collective-permute-start.36 = (bf16[512,256]{1,0:T(8,128)(2,1)}, bf16[512,256]{1,0:T(8,128)(2,1)}, u32[]{:S(2)}, u32[]{:S(2)}) collective-permute-start(bf16[512,256]{1,0:T(8,128)(2,1)} %bitcast.228), channel_id=1, source_target_pairs={{0,8},{4,12},{8,0},{12,24},{16,16},{20,4},{24,28},{28,20},{1,9},{5... | collective-permute-start | bytes 786440 | tf_op jit(solution)/shard_map/ppermute | solution.py:436
  757.6 35.9 %collective-permute-start.37 = (bf16[512,256]{1,0:T(8,128)(2,1)}, bf16[512,256]{1,0:T(8,128)(2,1)}, u32[]{:S(2)}, u32[]{:S(2)}) collective-permute-start(bf16[512,256]{1,0:T(8,128)(2,1)} %bitcast.227), channel_id=1, source_target_pairs={{0,0},{4,20},{8,12},{12,4},{16,24},{20,16},{24,8},{28,28},{1,1},{5... | collective-permute-start | bytes 786440 | tf_op jit(solution)/shard_map/ppermute | solution.py:436
  (68 other events, 988.9 us)
Sparse Core Ops, SparseCore 0:
  10.5 72.5 all-gather.9
  84.6 82.6 all-gather.7
  247.3 92.7 all-gather.5
  492.3 134.5 reduce-scatter.3
  629.1 67.9 reduce-scatter.5
  699.2 120.0 reduce-scatter.7

commit v4 on v3

--- a/solution.py
+++ b/solution.py
@@ -614,7 +614,9 @@
 
     x_own = tokens.reshape(rows, width)
     x1, a2 = mid(core, o_got, out_mine, out_other, x_own, gain2, shift2)
-    a2_all = lax.all_gather(a2, "fsdp", axis=0, tiled=True)
+    a2_near = relay_near(a2, F)
+    a2_got = relay_far(a2, a2_near, F)
+    a2_all = natural(a2_got).reshape(F * rows, width)
     dy_got = relay_far(dy_own, after(dy_near, a2_all), F)
     first = nn(a2_all, w_mine)
     dy_all = natural(dy_got).reshape(F * rows, width)
@@ -652,9 +654,10 @@
     both_part = both_part.reshape(2, ff_rows, width)
     both = lax.psum_scatter(both_part, "seq", scatter_dimension=1, tiled=True)
     hid_late = after(hid, both_part)
-    down_part = nn(hid_late, w_down).astype(bf16)
-
-    dn2_pieces = after(dn2_pieces, down_part)
+    down_part = nn(hid_late, w_down).astype(bf16).reshape(F, rows, width)
+    down_out = [lax.dynamic_index_in_dim(down_part, here ^ j, 0, keepdims=False) for j in range(F)]
+
+    dn2_pieces = after(dn2_pieces, down_out)
     dx1, dxl, do_two, gain2_part, shift2_part = mid_back(
         core, dn2_pieces, x1, dy_own, gain2, out_mine, out_other
     )
@@ -669,10 +672,12 @@
         o_pieces.append(lax.ppermute(piece, "fsdp", flip_pairs(F, j)) if j else piece)
 
     dm_parts = [g.reshape(all_rows, head_width) for g in attend_back(q, k, v, do, tabs)]
+    down_out = after(down_out, dm_parts)
+    down_pieces = send_flips(down_out, F)
     joint_part = joint(*dm_parts, w_qkv, dxl_pieces, o_pieces)
     joint_sum = lax.psum_scatter(joint_part, "seq", scatter_dimension=0, tiled=True)
 
-    a1_late, dm_parts, both, down_part = after((a1, dm_parts, both, down_part), joint_part)
+    a1_late, dm_parts, both = after((a1, dm_parts, both), joint_part)
     dm = jnp.concatenate(dm_parts, axis=1)
     both_pieces = to_rows(both, F, here)
     qkv_part_grad = tn(a1_late, dm).astype(bf16)
@@ -680,15 +685,11 @@
     qkv_pieces = [
         lax.dynamic_index_in_dim(qkv_part_grad, here ^ j, 0, keepdims=False) for j in range(F)
     ]
-    down_part, down_grad = after((down_part, down_grad), qkv_pieces)
+    down_grad = after(down_grad, qkv_pieces)
     qkv_got = send_flips(qkv_pieces, F)
     down_grad = down_grad.reshape(F, ratio * ff_part, head_width)
     down_grad_pieces = send_flips(
         [lax.dynamic_index_in_dim(down_grad, here ^ j, 0, keepdims=False) for j in range(F)], F
-    )
-    down_part = down_part.reshape(F, rows, width)
-    down_pieces = send_flips(
-        [lax.dynamic_index_in_dim(down_part, here ^ j, 0, keepdims=False) for j in range(F)], F
     )
     dm_late, dn1_late, x_late = after((dm, joint_part, x_all), qkv_pieces)
     xh_all, _ = norm_stats(x_late.astype(f32))

time: 847 us -> 826 us (0.975)
  local copies, waits for them, and re-layouts: 105 us -> 83.8 us
    all_to_all x1, waiting for transfers between devices: 81.3 us -> 0.01 us  [on_device(): lax.all_to_all(fetched, 'fsdp', split_axis=0, concat_axis=0, tiled=True)]
    ppermute x6, waiting for transfers between devices: 0.02 us -> 73.6 us  [gather_flips(): lax.ppermute(block, 'fsdp', flip_pairs(parts, j))]
    all_gather x1, waiting for transfers between devices: 83.5 us -> 58.8 us  [on_device(): x_all = lax.all_gather(tokens, 'seq', axis=0).reshape(all_rows, width)]
    ppermute x2 -> x3, waiting for transfers between devices: 13 us -> 36.8 us  [relay_far(): head = lax.ppermute(two[:half], 'fsdp', flip_pairs(parts, 1))]
    ppermute x12, waiting for transfers between devices: 42.8 us -> 64.7 us  [send_flips(): lax.ppermute(pieces[j], 'fsdp', flip_pairs(parts, j))]
    reduce_scatter x1, waiting for transfers between devices: 4.52 us -> 22.9 us  [on_device(): lax.psum_scatter(joint_part, 'seq', scatter_dimension=0, tiled=True)]
    all_gather x1, waiting for transfers between devices: 13.4 us -> 0.02 us  [on_device(): out_mine = lax.all_gather(out_half, 'fsdp', axis=0)]
    all_to_all x1, waiting for transfers between devices: 15.6 us -> 25.9 us  [on_device(): o_got = lax.all_to_all(o, 'seq', split_axis=0, concat_axis=0, tiled=True)]
  transfers between devices with their start and end apart: 49 -> 52, of which waited for: 18 -> 18; matrix products, arithmetic and copies ran while one was open for 20% -> 19% of each run, Pallas kernels for 11% -> 11%
where the time goes in v4:
time: 826 us; the launch traced here: 816 us
  waiting for transfers between devices  378 us (46%)
  matrix products  111 us (13%)
  Pallas kernels  93.4 us (11%)
  local copies, waits for them, and re-layouts  83.8 us (10%)
  starting transfers between devices  79.8 us (10%)
  other arithmetic  46.1 us (6%)
  between operations  25 us (3%)
    ppermute x6, waiting for transfers between devices, gather_flips(): lax.ppermute(block, 'fsdp', flip_pairs(parts, j))  73.6 us
    ppermute x12, waiting for transfers between devices, send_flips(): lax.ppermute(pieces[j], 'fsdp', flip_pairs(parts, j))  64.7 us
    all_gather x1, waiting for transfers between devices, on_device(): x_all = lax.all_gather(tokens, 'seq', axis=0).reshape(all_rows, width)  58.8 us
    ppermute x3, waiting for transfers between devices, on_device(): lax.ppermute(piece, 'fsdp', flip_pairs(F, j))  47.4 us
    dot_general x3, matrix products, nt(): lax.dot_general(a, b, (((1,), (1,)), ((), ())), preferred_element_type=jn...  39.8 us
    ppermute x3, waiting for transfers between devices, relay_far(): head = lax.ppermute(two[:half], 'fsdp', flip_pairs(parts, 1))  36.8 us
    dot_general x3, matrix products, tn(): lax.dot_general(a, b, (((0,), (0,)), ((), ())), preferred_element_type=jn...  36 us
    dot_general x3, matrix products, nn(): lax.dot_general(a, b, (((1,), (0,)), ((), ())), preferred_element_type=jn...  34.7 us
  transfers between devices with their start and end apart: 52, of which 18 were waited for; matrix products, arithmetic and copies ran while one was open for 19% of the time, Pallas kernels for 11%

profile of v4, /device:TPU:0, one launch (start us, length us, event | category | flops | bytes accessed | tf_op | source)
XLA Modules:
  0.0 816.3 jit_solution(10512660699322074938)
XLA Ops:
  27.9 15.0 %collective-permute-done.3 = bf16[512,768]{1,0:T(8,128)(2,1)S(1)} collective-permute-done((bf16[512,768]{1,0:T(8,128)(2,1)S(1)}, bf16[512,768]{1,0:T(8,128)(2,1)S(1)}, u32[]{:S(2)}, u32[]{:S(2)}) %collective-permute-start.3) | collective-permute-done | bytes 786464 | tf_op jit(solution)/shard_map/ppermute | solution.py:459
  60.8 72.9 %collective-permute-done = bf16[3584]{0:T(1024)(128)(2,1)S(1)} collective-permute-done((bf16[3584]{0:T(1024)(128)(2,1)S(1)}, bf16[3584]{0:T(1024)(128)(2,1)S(1)}, u32[]{:S(2)}, u32[]{:S(2)}) %collective-permute-start) | collective-permute-done | bytes 7200 | tf_op jit(solution)/shard_map/ppermute | solution.py:453
  142.2 6.7 collective-permute-done.5
  150.5 58.8 %all-gather.5.cloned.1.call-done = bf16[16,128,2048]{2,1,0:T(8,128)(2,1)} async-done(((bf16[2,128,2048]{2,1,0:T(8,128)(2,1)}), bf16[16,128,2048]{2,1,0:T(8,128)(2,1)}) %all-gather.5.cloned.1.call-update) | async-done | bytes 8388624 | tf_op jit(solution)/shard_map/all_gather | solution.py:581
  209.3 15.7 %project.1 = (f32[2048,768]{1,0:T(8,128)}, bf16[2048,2048]{1,0:T(8,128)(2,1)}) custom-call(bf16[2048,2048]{1,0:T(8,128)(2,1)} %bitcast.203, f32[1,2048]{1,0:T(1,128)S(1)} %bitcast.201, f32[1,2048]{1,0:T(1,128)S(1)} %bitcast.200, bf16[2048,768]{1,0:T(8,128)(2,1)} %bitcast.7.w_ref.refs_3_, f32[1,768]{1,0:T(1,128)S(1)} %bitcast.202), custom_call_target="tpu_custom_call" | custom-call | flops 6442450944 | bytes 26214400 | tf_op jit(solution)/shard_map/project/pallas_call | solution.py:498
  225.1 17.9 %attend.1 = (bf16[8,2,128,256]{3,2,1,0:T(8,128)(2,1)S(1)}, bf16[8,2,128,256]{3,2,1,0:T(8,128)(2,1)S(1)}, bf16[8,2,128,256]{3,2,1,0:T(8,128)(2,1)S(1)}, bf16[8,2,128,256]{3,2,1,0:T(8,128)(2,1)}) custom-call(f32[8,2,128,768]{3,2,1,0:T(8,128)} %bitcast.209, f32[8,2,128,768]{3,2,1,0:T(8,128)} %bitcast.210, f32[8,2,128,768]{3,2,1,0:T(8,128)} %bitcast.211, ...), custom_call_target="tpu_custom_call" | custom-call | flops 2147483648 | bytes 10485760 | tf_op jit(solution)/shard_map/attend/pallas_call | solution.py:167
  249.4 25.9 %all-to-all-done = bf16[8,2,128,256]{3,2,1,0:T(8,128)(2,1)S(1)} async-done(((bf16[8,2,128,256]{3,2,1,0:T(8,128)(2,1)}), bf16[8,2,128,256]{3,2,1,0:T(8,128)(2,1)S(1)}, u32[]{:S(2)}, u32[]{:S(2)}) %all-to-all-start) | async-done | bytes 1048608 | tf_op jit(solution)/shard_map/all_to_all | solution.py:609
  275.4 6.2 mid.1
  293.7 14.0 %collective-permute-done.9 = bf16[256,2048]{1,0:T(8,128)(2,1)S(1)} collective-permute-done((bf16[256,2048]{1,0:T(8,128)(2,1)S(1)}, bf16[256,2048]{1,0:T(8,128)(2,1)S(1)}, u32[]{:S(2)}, u32[]{:S(2)}) %collective-permute-start.9) | collective-permute-done | bytes 1048608 | tf_op jit(solution)/shard_map/ppermute | solution.py:459
  311.1 30.1 %collective-permute-done.10 = bf16[128,2048]{1,0:T(8,128)(2,1)S(1)} collective-permute-done((bf16[128,2048]{1,0:T(8,128)(2,1)S(1)}, bf16[128,2048]{1,0:T(8,128)(2,1)S(1)}, u32[]{:S(2)}, u32[]{:S(2)}) %collective-permute-start.10) | collective-permute-done | bytes 524320 | tf_op jit(solution)/shard_map/ppermute | solution.py:467
  346.0 10.3 %fusion.19 = f32[1024,1408]{1,0:T(8,128)} fusion(bf16[1024,2048]{1,0:T(8,128)(2,1)S(1)} %bitcast.224, bf16[2048,1408]{1,0:T(8,128)(2,1)} %bitcast.21), kind=kOutput, calls=%fused_computation.135 | convolution fusion | flops 5905580032 | bytes 15728640 | tf_op jit(solution)/shard_map/dot_general | solution.py:18
  361.5 13.9 %multiply_convert_fusion.2 = (bf16[1024,1408]{1,0:T(8,128)(2,1)}, f32[1024,1408]{1,0:T(8,128)}) fusion(f32[1024,1408]{1,0:T(8,128)} %fusion.19, pred[]{:T(512)S(6)} %eq.46, bf16[1024,2048]{1,0:T(8,128)(2,1)} %bitcast.225, bf16[2048,1408]{1,0:T(8,128)(2,1)} %collective-permute-done.17), kind=kOutput, calls=%fused_computation.16 | convolution fusion | flops 5917114368 | bytes 24379392 | tf_op jit(solution)/shard_map/dot_general | solution.py:18
  377.6 14.9 %all-to-all-done.2 = bf16[4,176,2048]{2,1,0:T(8,128)(2,1)} async-done(((bf16[4,176,2048]{2,1,0:T(8,128)(2,1)}), bf16[4,176,2048]{2,1,0:T(8,128)(2,1)}, u32[]{:S(2)}, u32[]{:S(2)}) %all-to-all-start.2) | async-done | bytes 2883616 | tf_op jit(solution)/shard_map/all_to_all | solution.py:627
  396.3 10.4 %convolution_convert_fusion.1 = bf16[1408,2048]{1,0:T(8,128)(2,1)} fusion(bf16[1024,1408]{1,0:T(8,128)(2,1)} %get-tuple-element.92, bf16[1024,2048]{1,0:T(8,128)(2,1)} %bitcast.28), kind=kOutput, calls=%fused_computation.10 | convolution fusion | flops 5908463616 | bytes 12845056 | tf_op jit(solution)/shard_map/dot_general | solution.py:26
  410.4 15.9 %multiply_convert_fusion = (bf16[1024,1408]{1,0:T(8,128)(2,1)S(1)}, bf16[1024,1408]{1,0:T(8,128)(2,1)}) fusion(f32[1024,1408]{1,0:T(8,128)} %fusion.19, f32[1024,1408]{1,0:T(8,128)} %get-tuple-element.248, pred[]{:T(512)S(6)} %eq.46, bf16[1024,2048]{1,0:T(8,128)(2,1)} %bitcast.28, bf16[1408,2048]{1,0:T(8,128)(2,1)S(1)} %bitcast.216), kind=kOutput, calls=%fused_computation.14 | convolution fusion | flops 5927206912 | bytes 27262976 | tf_op jit(solution)/shard_map/dot_general | solution.py:22
  426.3 13.0 %fusion.6 = f32[1024,2048]{1,0:T(8,128)} fusion(bf16[2048,1408]{1,0:T(8,128)(2,1)} %bitcast.21, bf16[1024,1408]{1,0:T(8,128)(2,1)} %get-tuple-element.194, bf16[1024,1408]{1,0:T(8,128)(2,1)S(1)} %get-tuple-element.193, pred[]{:T(512)S(6)} %eq.46), kind=kOutput, calls=%fused_computation.23 | convolution fusion | flops 5907021824 | bytes 19922944 | tf_op jit(solution)/shard_map/dot_general | solution.py:22
  441.5 10.9 %add_convert_fusion = bf16[1024,2048]{1,0:T(8,128)(2,1)S(1)} fusion(f32[1024,2048]{1,0:T(8,128)} %fusion.6, bf16[2048,1408]{1,0:T(8,128)(2,1)} %collective-permute-done.17, bf16[1024,1408]{1,0:T(8,128)(2,1)} %copy-done.31, bf16[1024,1408]{1,0:T(8,128)(2,1)} %get-tuple-element.194, pred[]{:T(512)S(6)} %eq.46), kind=kOutput, calls=%fused_computation.9 | convolution fusion | flops 5911216128 | bytes 24117248 | tf_op jit(solution)/shard_map/dot_general | solution.py:22
  456.1 14.7 %convolution_convert_fusion = bf16[2816,2048]{1,0:T(8,128)(2,1)} fusion(bf16[1024,2816]{1,0:T(8,128)(2,1)S(1)} %pad_maximum_fusion.1, bf16[1024,2048]{1,0:T(8,128)(2,1)S(1)} %bitcast.226), kind=kOutput, calls=%fused_computation.8 | convolution fusion | flops 11816927232 | bytes 21495808 | tf_op jit(solution)/shard_map/dot_general | solution.py:26
  474.9 10.6 %convolution_convert_fusion.2 = bf16[1024,2048]{1,0:T(8,128)(2,1)S(1)} fusion(bf16[1024,1408]{1,0:T(8,128)(2,1)} %get-tuple-element.92, bf16[1408,2048]{1,0:T(8,128)(2,1)} %bitcast.217), kind=kOutput, calls=%fused_computation.19 | convolution fusion | flops 5907677184 | bytes 12845056 | tf_op jit(solution)/shard_map/dot_general | solution.py:18
  487.7 10.9 %collective-permute-done.20.refs_3_ = bf16[256,2048]{1,0:T(8,128)(2,1)S(1)} collective-permute-done((bf16[256,2048]{1,0:T(8,128)(2,1)}, bf16[256,2048]{1,0:T(8,128)(2,1)S(1)}, u32[]{:S(2)}, u32[]{:S(2)}) %collective-permute-start.20) | collective-permute-done | bytes 1048608 | tf_op jit(solution)/shard_map/ppermute | solution.py:474
  498.6 21.5 %collective-permute-done.19.refs_2_ = bf16[256,2048]{1,0:T(8,128)(2,1)S(1)} collective-permute-done((bf16[256,2048]{1,0:T(8,128)(2,1)}, bf16[256,2048]{1,0:T(8,128)(2,1)S(1)}, u32[]{:S(2)}, u32[]{:S(2)}) %collective-permute-start.19) | collective-permute-done | bytes 1048608 | tf_op jit(solution)/shard_map/ppermute | solution.py:474
  521.5 11.1 %mid_back.1 = (f32[256,2048]{1,0:T(8,128)}, bf16[256,2048]{1,0:T(8,128)(2,1)}, bf16[8,256,256]{2,1,0:T(8,128)(2,1)}, f32[1,2048]{1,0:T(1,128)}, f32[1,2048]{1,0:T(1,128)}) custom-call(s32[1]{0:T(128)} %bitcast.core_ref, bf16[256,2048]{1,0:T(8,128)(2,1)} %get-tuple-element.93.refs_0_, bf16[256,2048]{1,0:T(8,128)(2,1)} %copy-done.39, ...), custom_call_target="tpu_custom_call" | custom-call | flops 2147483648 | bytes 18874368 | tf_op jit(solution)/shard_map/mid_back/pallas_call | solution.py:280
  544.2 47.4 %collective-permute-done.26.refs_11_ = bf16[2,256,256]{2,1,0:T(8,128)(2,1)S(1)} collective-permute-done((bf16[2,256,256]{2,1,0:T(8,128)(2,1)S(1)}, bf16[2,256,256]{2,1,0:T(8,128)(2,1)S(1)}, u32[]{:S(2)}, u32[]{:S(2)}) %collective-permute-start.26) | collective-permute-done | bytes 262176 | tf_op jit(solution)/shard_map/ppermute | solution.py:672
  596.9 24.9 %attend_back.1 = (bf16[8,2,128,256]{3,2,1,0:T(8,128)(2,1)S(1)}, bf16[8,2,128,256]{3,2,1,0:T(8,128)(2,1)S(1)}, bf16[8,2,128,256]{3,2,1,0:T(8,128)(2,1)S(1)}) custom-call(bf16[8,2,128,256]{3,2,1,0:T(8,128)(2,1)S(1)} %get-tuple-element.79.q_ref, bf16[8,2,128,256]{3,2,1,0:T(8,128)(2,1)} %copy-done.19, bf16[8,2,128,256]{3,2,1,0:T(8,128)(2,1)} %copy-done.20, ...), custom_call_target="tpu_custom_call" | custom-call | flops 5368709120 | bytes 7340032 | tf_op jit(solution)/shard_map/attend_back/pallas_call | solution.py:187
  621.9 14.4 %joint.1 = bf16[2048,2560]{1,0:T(8,128)(2,1)} custom-call(bf16[2048,256]{1,0:T(8,128)(2,1)S(1)} %bitcast.195, bf16[2048,256]{1,0:T(8,128)(2,1)S(1)} %bitcast.193, bf16[2048,256]{1,0:T(8,128)(2,1)S(1)} %bitcast.191, bf16[2048,768]{1,0:T(8,128)(2,1)} %bitcast.7.w_ref.refs_3_, bf16[256,2048]{1,0:T(8,128)(2,1)S(1)} %copy-done.21, ...), custom_call_target="tpu_custom_call" | custom-call | flops 8589934592 | bytes 26214400 | tf_op jit(solution)/shard_map/joint/pallas_call | solution.py:341
  646.0 10.9 %convolution_convert_fusion.3 = bf16[2048,768]{1,0:T(8,128)(2,1)S(1)} fusion(bf16[2048,2048]{1,0:T(8,128)(2,1)} %get-tuple-element.104, bf16[2048,768]{1,0:T(8,128)(2,1)S(1)} %constant_dynamic-update-slice_fusion), kind=kOutput, calls=%fused_computation.20 | convolution fusion | flops 6444023808 | bytes 14680064 | tf_op jit(solution)/shard_map/dot_general | solution.py:26
  671.2 6.0 fusion.2
  678.8 7.4 convert_reduce_fusion.1
  699.8 7.4 collective-permute-done.36
  707.7 22.6 %collective-permute-done.37 = bf16[512,768]{0,1:T(8,128)(2,1)} collective-permute-done((bf16[512,768]{0,1:T(8,128)(2,1)}, bf16[512,768]{0,1:T(8,128)(2,1)}, u32[]{:S(2)}, u32[]{:S(2)}) %collective-permute-start.37) | collective-permute-done | bytes 786464 | tf_op jit(solution)/shard_map/ppermute | solution.py:474
  757.8 5.8 collective-permute-start.40
  775.4 22.9 %reduce-scatter.8.cloned.1.call-done = bf16[256,2560]{1,0:T(8,128)(2,1)} async-done(((bf16[2048,2560]{1,0:T(8,128)(2,1)}), bf16[256,2560]{1,0:T(8,128)(2,1)}) %reduce-scatter.8.cloned.1.call-update) | async-done | bytes 1310736 | tf_op jit(solution)/shard_map/reduce_scatter | solution.py:678
  (343 shorter events, 200.0 us)
Async XLA Ops:
  7.2 127.7 %all-gather.7.cloned.1.call-start = ((), (), s32[]{:S(2)}) async-start(), calls=%async_computation.12 | async-start | bytes 5242880 | tf_op jit(solution)/shard_map/all_gather | solution.py:600
  9.9 199.4 %all-gather.5.cloned.1.call-start = ((), (), s32[]{:S(2)}) async-start(), calls=%async_computation.11 | async-start | bytes 9437184 | tf_op jit(solution)/shard_map/all_gather | solution.py:581
  45.1 199.9 %all-to-all-start.1 = ((bf16[4,512,1408]{2,1,0:T(8,128)(2,1)}), bf16[4,512,1408]{2,1,0:T(8,128)(2,1)}, u32[]{:S(2)}, u32[]{:S(2)}) async-start(bf16[4,512,1408]{2,1,0:T(8,128)(2,1)} %copy-done.4), calls=%async_computation.1 | async-start | bytes 11534336 | tf_op jit(solution)/shard_map/all_to_all | solution.py:602
  51.2 83.4 %collective-permute-start.2 = (bf16[3584]{0:T(1024)(128)(2,1)S(1)}, bf16[3584]{0:T(1024)(128)(2,1)S(1)}, u32[]{:S(2)}, u32[]{:S(2)}) collective-permute-start(bf16[3584]{0:T(1024)(128)(2,1)S(1)} %constant_dynamic-update-slice_fusion.3), channel_id=1, source_target_pairs={{0,3},{1,2},{2,1},{3,0},{4,7},{5,6},{6,5},{7,4},{8,11},{9,10},{10,... | collective-permute-start | bytes 21512 | tf_op jit(solution)/shard_map/ppermute | solution.py:453
  54.1 80.4 %collective-permute-start.1 = (bf16[3584]{0:T(1024)(128)(2,1)S(1)}, bf16[3584]{0:T(1024)(128)(2,1)S(1)}, u32[]{:S(2)}, u32[]{:S(2)}) collective-permute-start(bf16[3584]{0:T(1024)(128)(2,1)S(1)} %constant_dynamic-update-slice_fusion.3), channel_id=1, source_target_pairs={{0,2},{1,3},{2,0},{3,1},{4,6},{5,7},{6,4},{7,5},{8,10},{9,11},{10,... | collective-permute-start | bytes 21512 | tf_op jit(solution)/shard_map/ppermute | solution.py:453
  54.6 79.1 %collective-permute-start = (bf16[3584]{0:T(1024)(128)(2,1)S(1)}, bf16[3584]{0:T(1024)(128)(2,1)S(1)}, u32[]{:S(2)}, u32[]{:S(2)}) collective-permute-start(bf16[3584]{0:T(1024)(128)(2,1)S(1)} %constant_dynamic-update-slice_fusion.3), channel_id=1, source_target_pairs={{0,1},{1,0},{2,3},{3,2},{4,5},{5,4},{6,7},{7,6},{8,9},{9,8},{10,11... | collective-permute-start | bytes 21512 | tf_op jit(solution)/shard_map/ppermute | solution.py:453
  134.9 114.6 %collective-permute-start.7 = (bf16[4,256,2048]{2,1,0:T(8,128)(2,1)}, bf16[4,256,2048]{2,1,0:T(8,128)(2,1)}, u32[]{:S(2)}, u32[]{:S(2)}) collective-permute-start(bf16[4,256,2048]{2,1,0:T(8,128)(2,1)} %bitcast.212), channel_id=1, source_target_pairs={{0,4},{4,0},{8,12},{12,8},{16,20},{20,16},{24,28},{28,24},{1,5},{5... | collective-permute-start | bytes 12582920 | tf_op jit(solution)/shard_map/ppermute | solution.py:612
  248.9 112.6 %collective-permute-start.17 = (bf16[2048,1408]{1,0:T(8,128)(2,1)}, bf16[2048,1408]{1,0:T(8,128)(2,1)}, u32[]{:S(2)}, u32[]{:S(2)}) collective-permute-start(bf16[2048,1408]{1,0:T(8,128)(2,1)} %bitcast.21), channel_id=1, source_target_pairs={{0,4},{4,0},{8,12},{12,8},{16,20},{20,16},{24,28},{28,24},{1,5},{5... | collective-permute-start | bytes 17301512 | tf_op jit(solution)/shard_map/ppermute | solution.py:604
  292.0 49.3 %collective-permute-start.14 = (bf16[256,2048]{1,0:T(8,128)(2,1)S(1)}, bf16[256,2048]{1,0:T(8,128)(2,1)S(1)}, u32[]{:S(2)}, u32[]{:S(2)}) collective-permute-start(bf16[256,2048]{1,0:T(8,128)(2,1)S(1)} %bitcast.220), channel_id=1, source_target_pairs={{0,2},{1,3},{2,0},{3,1},{4,6},{5,7},{6,4},{7,5},{8,10},{9,11},{10,... | collective-permute-start | bytes 3145736 | tf_op jit(solution)/shard_map/ppermute | solution.py:459
  292.6 48.8 %collective-permute-start.13 = (bf16[256,2048]{1,0:T(8,128)(2,1)S(1)}, bf16[256,2048]{1,0:T(8,128)(2,1)S(1)}, u32[]{:S(2)}, u32[]{:S(2)}) collective-permute-start(bf16[256,2048]{1,0:T(8,128)(2,1)S(1)} %bitcast.221), channel_id=1, source_target_pairs={{0,1},{1,0},{2,3},{3,2},{4,5},{5,4},{6,7},{7,6},{8,9},{9,8},{10,11... | collective-permute-start | bytes 3145736 | tf_op jit(solution)/shard_map/ppermute | solution.py:459
  344.0 48.6 %collective-permute-start.15 = (bf16[128,2048]{1,0:T(8,128)(2,1)}, bf16[128,2048]{1,0:T(8,128)(2,1)}, u32[]{:S(2)}, u32[]{:S(2)}) collective-permute-start(bf16[128,2048]{1,0:T(8,128)(2,1)} %slice.85), channel_id=1, source_target_pairs={{0,1},{1,0},{2,3},{3,2},{4,5},{5,4},{6,7},{7,6},{8,9},{9,8},{10,11... | collective-permute-start | bytes 1572872 | tf_op jit(solution)/shard_map/ppermute | solution.py:467
  345.5 49.0 %collective-permute-start.16 = (bf16[128,2048]{1,0:T(8,128)(2,1)}, bf16[128,2048]{1,0:T(8,128)(2,1)}, u32[]{:S(2)}, u32[]{:S(2)}) collective-permute-start(bf16[128,2048]{1,0:T(8,128)(2,1)} %slice.86), channel_id=1, source_target_pairs={{0,2},{1,3},{2,0},{3,1},{4,6},{5,7},{6,4},{7,5},{8,10},{9,11},{10,... | collective-permute-start | bytes 1572872 | tf_op jit(solution)/shard_map/ppermute | solution.py:468
  360.9 283.6 %reduce-scatter.4.cloned.1.call-start = ((), (), s32[]{:S(2)}) async-start(), calls=%async_computation.8 | async-start | bytes 12976128 | tf_op jit(solution)/shard_map/reduce_scatter | solution.py:655
  470.8 216.1 %reduce-scatter.6.cloned.1.call-start = ((), (), s32[]{:S(2)}) async-start(), calls=%async_computation.9 | async-start | bytes 6488064 | tf_op jit(solution)/shard_map/reduce_scatter | solution.py:636
  472.8 47.3 %collective-permute-start.19 = (bf16[256,2048]{1,0:T(8,128)(2,1)}, bf16[256,2048]{1,0:T(8,128)(2,1)S(1)}, u32[]{:S(2)}, u32[]{:S(2)}) collective-permute-start(bf16[256,2048]{1,0:T(8,128)(2,1)} %get-tuple-element.205), channel_id=1, source_target_pairs={{0,2},{1,3},{2,0},{3,1},{4,6},{5,7},{6,4},{7,5},{8,10},{9,11},{10,... | collective-permute-start | bytes 3145736 | tf_op jit(solution)/shard_map/ppermute | solution.py:474
  474.3 45.9 %collective-permute-start.18 = (bf16[256,2048]{1,0:T(8,128)(2,1)}, bf16[256,2048]{1,0:T(8,128)(2,1)S(1)}, u32[]{:S(2)}, u32[]{:S(2)}) collective-permute-start(bf16[256,2048]{1,0:T(8,128)(2,1)} %get-tuple-element.206), channel_id=1, source_target_pairs={{0,1},{1,0},{2,3},{3,2},{4,5},{5,4},{6,7},{7,6},{8,9},{9,8},{10,11... | collective-permute-start | bytes 3145736 | tf_op jit(solution)/shard_map/ppermute | solution.py:474
  532.6 61.2 %all-to-all-start.3 = ((bf16[8,256,256]{2,1,0:T(8,128)(2,1)}), bf16[8,256,256]{2,1,0:T(8,128)(2,1)}, u32[]{:S(2)}, u32[]{:S(2)}) async-start(bf16[8,256,256]{2,1,0:T(8,128)(2,1)} %get-tuple-element.97), calls=%async_computation.3 | async-start | bytes 2097152 | tf_op jit(solution)/shard_map/all_to_all | solution.py:664
  536.8 261.5 %reduce-scatter.8.cloned.1.call-start = ((), (), s32[]{:S(2)}) async-start(), calls=%async_computation.10 | async-start | bytes 11796480 | tf_op jit(solution)/shard_map/reduce_scatter | solution.py:678
  536.9 84.9 %collective-permute-start.23 = (bf16[256,2048]{1,0:T(8,128)(2,1)}, bf16[256,2048]{1,0:T(8,128)(2,1)}, u32[]{:S(2)}, u32[]{:S(2)}) collective-permute-start(bf16[256,2048]{1,0:T(8,128)(2,1)} %get-tuple-element.101.refs_4_), channel_id=1, source_target_pairs={{0,3},{1,2},{2,1},{3,0},{4,7},{5,6},{6,5},{7,4},{8,11},{9,10},{10,... | collective-permute-start | bytes 3145736 | tf_op jit(solution)/shard_map/ppermute | solution.py:453
  538.3 83.5 %collective-permute-start.22 = (bf16[256,2048]{1,0:T(8,128)(2,1)}, bf16[256,2048]{1,0:T(8,128)(2,1)}, u32[]{:S(2)}, u32[]{:S(2)}) collective-permute-start(bf16[256,2048]{1,0:T(8,128)(2,1)} %get-tuple-element.101.refs_4_), channel_id=1, source_target_pairs={{0,2},{1,3},{2,0},{3,1},{4,6},{5,7},{6,4},{7,5},{8,10},{9,11},{10,... | collective-permute-start | bytes 3145736 | tf_op jit(solution)/shard_map/ppermute | solution.py:453
  539.8 82.0 %collective-permute-start.21 = (bf16[256,2048]{1,0:T(8,128)(2,1)}, bf16[256,2048]{1,0:T(8,128)(2,1)}, u32[]{:S(2)}, u32[]{:S(2)}) collective-permute-start(bf16[256,2048]{1,0:T(8,128)(2,1)} %get-tuple-element.101.refs_4_), channel_id=1, source_target_pairs={{0,1},{1,0},{2,3},{3,2},{4,5},{5,4},{6,7},{7,6},{8,9},{9,8},{10,11... | collective-permute-start | bytes 3145736 | tf_op jit(solution)/shard_map/ppermute | solution.py:453
  541.3 50.3 %collective-permute-start.26 = (bf16[2,256,256]{2,1,0:T(8,128)(2,1)S(1)}, bf16[2,256,256]{2,1,0:T(8,128)(2,1)S(1)}, u32[]{:S(2)}, u32[]{:S(2)}) collective-permute-start(bf16[2,256,256]{2,1,0:T(8,128)(2,1)S(1)} %get-tuple-element.218), channel_id=1, source_target_pairs={{0,3},{1,2},{2,1},{3,0},{4,7},{5,6},{6,5},{7,4},{8,11},{9,10},{10,... | collective-permute-start | bytes 786440 | tf_op jit(solution)/shard_map/ppermute | solution.py:672
  542.7 79.2 %collective-permute-start.25 = (bf16[2,256,256]{2,1,0:T(8,128)(2,1)}, bf16[2,256,256]{2,1,0:T(8,128)(2,1)}, u32[]{:S(2)}, u32[]{:S(2)}) collective-permute-start(bf16[2,256,256]{2,1,0:T(8,128)(2,1)} %get-tuple-element.219), channel_id=1, source_target_pairs={{0,2},{1,3},{2,0},{3,1},{4,6},{5,7},{6,4},{7,5},{8,10},{9,11},{10,... | collective-permute-start | bytes 786440 | tf_op jit(solution)/shard_map/ppermute | solution.py:672
  641.5 55.6 %collective-permute-start.34 = (bf16[256,2048]{1,0:T(8,128)(2,1)}, bf16[256,2048]{1,0:T(8,128)(2,1)}, u32[]{:S(2)}, u32[]{:S(2)}) collective-permute-start(bf16[256,2048]{1,0:T(8,128)(2,1)} %get-tuple-element.111), channel_id=1, source_target_pairs={{0,2},{1,3},{2,0},{3,1},{4,6},{5,7},{6,4},{7,5},{8,10},{9,11},{10,... | collective-permute-start | bytes 3145736 | tf_op jit(solution)/shard_map/ppermute | solution.py:474
  643.0 103.6 %collective-permute-start.35 = (bf16[256,2048]{1,0:T(8,128)(2,1)}, bf16[256,2048]{1,0:T(8,128)(2,1)}, u32[]{:S(2)}, u32[]{:S(2)}) collective-permute-start(bf16[256,2048]{1,0:T(8,128)(2,1)} %get-tuple-element.112), channel_id=1, source_target_pairs={{0,3},{1,2},{2,1},{3,0},{4,7},{5,6},{6,5},{7,4},{8,11},{9,10},{10,... | collective-permute-start | bytes 3145736 | tf_op jit(solution)/shard_map/ppermute | solution.py:474
  665.0 65.3 %collective-permute-start.37 = (bf16[512,768]{0,1:T(8,128)(2,1)}, bf16[512,768]{0,1:T(8,128)(2,1)}, u32[]{:S(2)}, u32[]{:S(2)}) collective-permute-start(bf16[512,768]{0,1:T(8,128)(2,1)} %bitcast.238), channel_id=1, source_target_pairs={{0,2},{1,3},{2,0},{3,1},{4,6},{5,7},{6,4},{7,5},{8,10},{9,11},{10,... | collective-permute-start | bytes 2359304 | tf_op jit(solution)/shard_map/ppermute | solution.py:474
  677.2 54.6 %collective-permute-start.38 = (bf16[512,768]{0,1:T(8,128)(2,1)S(1)}, bf16[512,768]{0,1:T(8,128)(2,1)}, u32[]{:S(2)}, u32[]{:S(2)}) collective-permute-start(bf16[512,768]{0,1:T(8,128)(2,1)S(1)} %bitcast.237), channel_id=1, source_target_pairs={{0,3},{1,2},{2,1},{3,0},{4,7},{5,6},{6,5},{7,4},{8,11},{9,10},{10,... | collective-permute-start | bytes 2359304 | tf_op jit(solution)/shard_map/ppermute | solution.py:474
  687.9 58.6 %all-to-all-start.4 = ((f32[32,1,448]{2,1,0:T(1,128)}), f32[32,1,448]{2,1,0:T(1,128)S(1)}, u32[]{:S(2)}, u32[]{:S(2)}) async-start(f32[32,1,448]{2,1,0:T(1,128)} %all_to_all.24), calls=%async_computation.7 | async-start | bytes 131072 | tf_op jit(solution)/shard_map/all_to_all | solution.py:727
  697.1 55.3 %collective-permute-start.29 = (bf16[2,176,512]{2,1,0:T(8,128)(2,1)}, bf16[2,176,512]{2,1,0:T(8,128)(2,1)}, u32[]{:S(2)}, u32[]{:S(2)}) collective-permute-start(bf16[2,176,512]{2,1,0:T(8,128)(2,1)} %get-tuple-element.214), channel_id=1, source_target_pairs={{0,3},{1,2},{2,1},{3,0},{4,7},{5,6},{6,5},{7,4},{8,11},{9,10},{10,... | collective-permute-start | bytes 1081352 | tf_op jit(solution)/shard_map/ppermute | solution.py:531
  707.2 45.2 %collective-permute-start.28 = (bf16[2,176,512]{2,1,0:T(8,128)(2,1)}, bf16[2,176,512]{2,1,0:T(8,128)(2,1)}, u32[]{:S(2)}, u32[]{:S(2)}) collective-permute-start(bf16[2,176,512]{2,1,0:T(8,128)(2,1)} %get-tuple-element.215), channel_id=1, source_target_pairs={{0,2},{1,3},{2,0},{3,1},{4,6},{5,7},{6,4},{7,5},{8,10},{9,11},{10,... | collective-permute-start | bytes 1081352 | tf_op jit(solution)/shard_map/ppermute | solution.py:531
  755.8 51.3 %collective-permute-start.39 = (bf16[512,256]{1,0:T(8,128)(2,1)}, bf16[512,256]{1,0:T(8,128)(2,1)}, u32[]{:S(2)}, u32[]{:S(2)}) collective-permute-start(bf16[512,256]{1,0:T(8,128)(2,1)} %bitcast.85), channel_id=1, source_target_pairs={{0,20},{4,0},{8,24},{12,12},{16,4},{20,28},{24,16},{28,8},{1,21},{... | collective-permute-start | bytes 786440 | tf_op jit(solution)/shard_map/ppermute | solution.py:436
  757.8 49.3 %collective-permute-start.40 = (bf16[512,256]{1,0:T(8,128)(2,1)}, bf16[512,256]{1,0:T(8,128)(2,1)}, u32[]{:S(2)}, u32[]{:S(2)}) collective-permute-start(bf16[512,256]{1,0:T(8,128)(2,1)} %bitcast.88), channel_id=1, source_target_pairs={{0,8},{4,12},{8,0},{12,24},{16,16},{20,4},{24,28},{28,20},{1,9},{5... | collective-permute-start | bytes 786440 | tf_op jit(solution)/shard_map/ppermute | solution.py:436
  (76 other events, 1651.0 us)
Sparse Core Ops, SparseCore 0:
  10.4 115.7 all-gather.6
  127.8 81.4 all-gather.4
  470.9 135.0 reduce-scatter.3
  608.1 67.9 reduce-scatter.5
  678.3 120.0 reduce-scatter.7

commit v5 on v4

--- a/solution.py
+++ b/solution.py
@@ -459,14 +459,19 @@
     return [lax.ppermute(block, "fsdp", flip_pairs(parts, j)) for j in (1, 2)]
 
 
-def relay_far(block, near, parts):
+def relay_halves(near, parts):
     if parts != 4:
+        return []
+    one, two = near
+    half = one.shape[0] // 2
+    return [two[:half], one[half:]]
+
+
+def relay_far(block, near, halves):
+    if not halves:
         return [block, *near]
-    one, two = near
-    half = block.shape[0] // 2
-    head = lax.ppermute(two[:half], "fsdp", flip_pairs(parts, 1))
-    tail = lax.ppermute(one[half:], "fsdp", flip_pairs(parts, 2))
-    return [block, one, two, (head, tail)]
+    got = [lax.ppermute(halves[j - 1], "fsdp", flip_pairs(4, j)) for j in (1, 2)]
+    return [block, *near, tuple(got)]
 
 
 def send_flips(pieces, parts):
@@ -593,7 +598,7 @@
         axis=1,
     )
     qkv_near = relay_near(qkv_part, F)
-    qkv_got = relay_far(qkv_part, qkv_near, F)
+    qkv_got = relay_far(qkv_part, qkv_near, relay_halves(qkv_near, F))
     w_qkv = natural(qkv_got).reshape(width, 3 * head_width)
 
     out_half = lax.dynamic_slice_in_dim(out_weight, me % 2 * head_width, head_width, 0)
@@ -615,9 +620,11 @@
     x_own = tokens.reshape(rows, width)
     x1, a2 = mid(core, o_got, out_mine, out_other, x_own, gain2, shift2)
     a2_near = relay_near(a2, F)
-    a2_got = relay_far(a2, a2_near, F)
+    a2_got = relay_far(a2, a2_near, relay_halves(a2_near, F))
+    dy_halves = relay_halves(dy_near, F)
+    a2_got[-1], dy_halves = after((a2_got[-1], dy_halves), dy_halves)
     a2_all = natural(a2_got).reshape(F * rows, width)
-    dy_got = relay_far(dy_own, after(dy_near, a2_all), F)
+    dy_got = relay_far(dy_own, dy_near, after(dy_halves, a2_all))
     first = nn(a2_all, w_mine)
     dy_all = natural(dy_got).reshape(F * rows, width)
     down_half = lax.dynamic_index_in_dim(
@@ -707,7 +714,7 @@
     down_result = natural(down_grad_pieces).reshape(F, ratio, ff_part, head_width)
     down_result = down_result.transpose(1, 0, 2, 3).reshape(ff_rows, head_width).astype(f32)
     layer_out = (x1 + total(down_pieces)).astype(bf16).reshape(tokens.shape)
-    joint_sum = after(joint_sum, qkv_sum, layer_out, gate_result, up_result, down_result)
+    joint_sum = after(joint_sum, qkv_result, layer_out, gate_result, up_result, down_result)
     dn1 = joint_sum[:, :width].astype(f32)
     out_result = joint_sum[:, width:].T.astype(f32)
 

time: 826 us -> 803 us (0.972)
  waiting for transfers between devices: 378 us -> 351 us
    ppermute x6, waiting for transfers between devices: 36.8 us -> 18.3 us  [relay_far(): lax.ppermute(halves[j - 1], 'fsdp', flip_pairs(4, j))]
    all_to_all x1, waiting for transfers between devices: 25.9 us -> 15.9 us  [on_device(): o_got = lax.all_to_all(o, 'seq', split_axis=0, concat_axis=0, tiled=True)]
    unnamed x125 -> x121, local copies, waits for them, and re-layouts: 25.1 us -> 25.8 us
  transfers between devices with their start and end apart: 52 -> 52, of which waited for: 18 -> 20; matrix products, arithmetic and copies ran while one was open for 19% -> 18% of each run, Pallas kernels for 11% -> 12%
where the time goes in v5:
time: 803 us; the launch traced here: 793 us
  waiting for transfers between devices  351 us (44%)
  matrix products  110 us (14%)
  Pallas kernels  93.3 us (12%)
  local copies, waits for them, and re-layouts  86.1 us (11%)
  starting transfers between devices  81.5 us (10%)
  other arithmetic  46 us (6%)
  between operations  24.9 us (3%)
    ppermute x6, waiting for transfers between devices, gather_flips(): lax.ppermute(block, 'fsdp', flip_pairs(parts, j))  73.7 us
    ppermute x12, waiting for transfers between devices, send_flips(): lax.ppermute(pieces[j], 'fsdp', flip_pairs(parts, j))  64 us
    all_gather x1, waiting for transfers between devices, on_device(): x_all = lax.all_gather(tokens, 'seq', axis=0).reshape(all_rows, width)  58.7 us
    ppermute x3, waiting for transfers between devices, on_device(): lax.ppermute(piece, 'fsdp', flip_pairs(F, j))  47.5 us
    dot_general x3, matrix products, nt(): lax.dot_general(a, b, (((1,), (1,)), ((), ())), preferred_element_type=jn...  39.8 us
    dot_general x3, matrix products, tn(): lax.dot_general(a, b, (((0,), (0,)), ((), ())), preferred_element_type=jn...  36.1 us
    dot_general x3, matrix products, nn(): lax.dot_general(a, b, (((1,), (0,)), ((), ())), preferred_element_type=jn...  34.6 us
    ppermute x6, waiting for transfers between devices, relay_near(): return [lax.ppermute(block, 'fsdp', flip_pairs(parts, j)) for j in (1, 2)]  29.7 us
  transfers between devices with their start and end apart: 52, of which 20 were waited for; matrix products, arithmetic and copies ran while one was open for 18% of the time, Pallas kernels for 12%

profile of v5, /device:TPU:0, one launch (start us, length us, event | category | flops | bytes accessed | tf_op | source)
XLA Modules:
  0.0 793.3 jit_solution(4880574576928941324)
XLA Ops:
  27.9 15.0 %collective-permute-done.3 = bf16[512,768]{1,0:T(8,128)(2,1)S(1)} collective-permute-done((bf16[512,768]{1,0:T(8,128)(2,1)S(1)}, bf16[512,768]{1,0:T(8,128)(2,1)S(1)}, u32[]{:S(2)}, u32[]{:S(2)}) %collective-permute-start.3) | collective-permute-done | bytes 786464 | tf_op jit(solution)/shard_map/ppermute | solution.py:459
  61.5 73.1 %collective-permute-done = bf16[3584]{0:T(1024)(128)(2,1)S(1)} collective-permute-done((bf16[3584]{0:T(1024)(128)(2,1)S(1)}, bf16[3584]{0:T(1024)(128)(2,1)S(1)}, u32[]{:S(2)}, u32[]{:S(2)}) %collective-permute-start) | collective-permute-done | bytes 7200 | tf_op jit(solution)/shard_map/ppermute | solution.py:453
  142.0 7.8 collective-permute-done.5
  151.4 58.7 %all-gather.5.cloned.1.call-done = bf16[16,128,2048]{2,1,0:T(8,128)(2,1)} async-done(((bf16[2,128,2048]{2,1,0:T(8,128)(2,1)}), bf16[16,128,2048]{2,1,0:T(8,128)(2,1)}) %all-gather.5.cloned.1.call-update) | async-done | bytes 8388624 | tf_op jit(solution)/shard_map/all_gather | solution.py:586
  210.0 15.7 %project.1 = (f32[2048,768]{1,0:T(8,128)}, bf16[2048,2048]{1,0:T(8,128)(2,1)}) custom-call(bf16[2048,2048]{1,0:T(8,128)(2,1)} %bitcast.203, f32[1,2048]{1,0:T(1,128)S(1)} %bitcast.201, f32[1,2048]{1,0:T(1,128)S(1)} %bitcast.200, bf16[2048,768]{1,0:T(8,128)(2,1)} %bitcast.7.w_ref.refs_3_, f32[1,768]{1,0:T(1,128)S(1)} %bitcast.202), custom_call_target="tpu_custom_call" | custom-call | flops 6442450944 | bytes 26214400 | tf_op jit(solution)/shard_map/project/pallas_call | solution.py:503
  225.8 17.9 %attend.1 = (bf16[8,2,128,256]{3,2,1,0:T(8,128)(2,1)S(1)}, bf16[8,2,128,256]{3,2,1,0:T(8,128)(2,1)S(1)}, bf16[8,2,128,256]{3,2,1,0:T(8,128)(2,1)S(1)}, bf16[8,2,128,256]{3,2,1,0:T(8,128)(2,1)}) custom-call(f32[8,2,128,768]{3,2,1,0:T(8,128)} %bitcast.209, f32[8,2,128,768]{3,2,1,0:T(8,128)} %bitcast.210, f32[8,2,128,768]{3,2,1,0:T(8,128)} %bitcast.211, ...), custom_call_target="tpu_custom_call" | custom-call | flops 2147483648 | bytes 10485760 | tf_op jit(solution)/shard_map/attend/pallas_call | solution.py:167
  260.3 15.9 %all-to-all-done = bf16[8,2,128,256]{3,2,1,0:T(8,128)(2,1)S(1)} async-done(((bf16[8,2,128,256]{3,2,1,0:T(8,128)(2,1)}), bf16[8,2,128,256]{3,2,1,0:T(8,128)(2,1)S(1)}, u32[]{:S(2)}, u32[]{:S(2)}) %all-to-all-start) | async-done | bytes 1048608 | tf_op jit(solution)/shard_map/all_to_all | solution.py:614
  276.2 6.2 mid.1
  294.5 12.6 %collective-permute-done.9 = bf16[256,2048]{1,0:T(8,128)(2,1)S(1)} collective-permute-done((bf16[256,2048]{1,0:T(8,128)(2,1)S(1)}, bf16[256,2048]{1,0:T(8,128)(2,1)S(1)}, u32[]{:S(2)}, u32[]{:S(2)}) %collective-permute-start.9) | collective-permute-done | bytes 1048608 | tf_op jit(solution)/shard_map/ppermute | solution.py:459
  310.5 9.2 %collective-permute-done.10 = bf16[128,2048]{1,0:T(8,128)(2,1)S(1)} collective-permute-done((bf16[128,2048]{1,0:T(8,128)(2,1)S(1)}, bf16[128,2048]{1,0:T(8,128)(2,1)S(1)}, u32[]{:S(2)}, u32[]{:S(2)}) %collective-permute-start.10) | collective-permute-done | bytes 524320 | tf_op jit(solution)/shard_map/ppermute | solution.py:473
  323.2 10.3 %fusion.19 = f32[1024,1408]{1,0:T(8,128)} fusion(bf16[1024,2048]{1,0:T(8,128)(2,1)S(1)} %bitcast.224, bf16[2048,1408]{1,0:T(8,128)(2,1)} %bitcast.22), kind=kOutput, calls=%fused_computation.135 | convolution fusion | flops 5905580032 | bytes 15728640 | tf_op jit(solution)/shard_map/dot_general | solution.py:18
  338.7 13.7 %multiply_convert_fusion.2 = (bf16[1024,1408]{1,0:T(8,128)(2,1)}, f32[1024,1408]{1,0:T(8,128)}) fusion(f32[1024,1408]{1,0:T(8,128)} %fusion.19, pred[]{:T(512)S(6)} %eq.46, bf16[1024,2048]{1,0:T(8,128)(2,1)} %bitcast.225, bf16[2048,1408]{1,0:T(8,128)(2,1)} %collective-permute-done.17), kind=kOutput, calls=%fused_computation.16 | convolution fusion | flops 5917114368 | bytes 24379392 | tf_op jit(solution)/shard_map/dot_general | solution.py:18
  352.4 16.9 %all-to-all-done.2 = bf16[4,176,2048]{2,1,0:T(8,128)(2,1)} async-done(((bf16[4,176,2048]{2,1,0:T(8,128)(2,1)}), bf16[4,176,2048]{2,1,0:T(8,128)(2,1)}, u32[]{:S(2)}, u32[]{:S(2)}) %all-to-all-start.2) | async-done | bytes 2883616 | tf_op jit(solution)/shard_map/all_to_all | solution.py:634
  373.1 10.4 %convolution_convert_fusion.1 = bf16[1408,2048]{1,0:T(8,128)(2,1)} fusion(bf16[1024,1408]{1,0:T(8,128)(2,1)} %get-tuple-element.100, bf16[1024,2048]{1,0:T(8,128)(2,1)} %bitcast.28), kind=kOutput, calls=%fused_computation.10 | convolution fusion | flops 5908463616 | bytes 12845056 | tf_op jit(solution)/shard_map/dot_general | solution.py:26
  387.2 15.9 %multiply_convert_fusion = (bf16[1024,1408]{1,0:T(8,128)(2,1)S(1)}, bf16[1024,1408]{1,0:T(8,128)(2,1)}) fusion(f32[1024,1408]{1,0:T(8,128)} %fusion.19, f32[1024,1408]{1,0:T(8,128)} %get-tuple-element.256, pred[]{:T(512)S(6)} %eq.46, bf16[1024,2048]{1,0:T(8,128)(2,1)} %bitcast.28, bf16[1408,2048]{1,0:T(8,128)(2,1)S(1)} %bitcast.216), kind=kOutput, calls=%fused_computation.14 | convolution fusion | flops 5927206912 | bytes 27262976 | tf_op jit(solution)/shard_map/dot_general | solution.py:22
  403.1 13.0 %fusion.6 = f32[1024,2048]{1,0:T(8,128)} fusion(bf16[2048,1408]{1,0:T(8,128)(2,1)} %bitcast.22, bf16[1024,1408]{1,0:T(8,128)(2,1)} %get-tuple-element.202, bf16[1024,1408]{1,0:T(8,128)(2,1)S(1)} %get-tuple-element.201, pred[]{:T(512)S(6)} %eq.46), kind=kOutput, calls=%fused_computation.23 | convolution fusion | flops 5907021824 | bytes 19922944 | tf_op jit(solution)/shard_map/dot_general | solution.py:22
  418.4 10.9 %add_convert_fusion = bf16[1024,2048]{1,0:T(8,128)(2,1)S(1)} fusion(f32[1024,2048]{1,0:T(8,128)} %fusion.6, bf16[2048,1408]{1,0:T(8,128)(2,1)} %collective-permute-done.17, bf16[1024,1408]{1,0:T(8,128)(2,1)} %copy-done.32, bf16[1024,1408]{1,0:T(8,128)(2,1)} %get-tuple-element.202, pred[]{:T(512)S(6)} %eq.46), kind=kOutput, calls=%fused_computation.9 | convolution fusion | flops 5911216128 | bytes 24117248 | tf_op jit(solution)/shard_map/dot_general | solution.py:22
  433.0 14.7 %convolution_convert_fusion = bf16[2816,2048]{1,0:T(8,128)(2,1)} fusion(bf16[1024,2816]{1,0:T(8,128)(2,1)S(1)} %pad_maximum_fusion.1, bf16[1024,2048]{1,0:T(8,128)(2,1)S(1)} %bitcast.226), kind=kOutput, calls=%fused_computation.8 | convolution fusion | flops 11816927232 | bytes 21495808 | tf_op jit(solution)/shard_map/dot_general | solution.py:26
  451.8 10.6 %convolution_convert_fusion.2 = bf16[1024,2048]{1,0:T(8,128)(2,1)S(1)} fusion(bf16[1024,1408]{1,0:T(8,128)(2,1)} %get-tuple-element.100, bf16[1408,2048]{1,0:T(8,128)(2,1)} %bitcast.217), kind=kOutput, calls=%fused_computation.19 | convolution fusion | flops 5907677184 | bytes 12845056 | tf_op jit(solution)/shard_map/dot_general | solution.py:18
  464.6 10.9 %collective-permute-done.20.refs_3_ = bf16[256,2048]{1,0:T(8,128)(2,1)S(1)} collective-permute-done((bf16[256,2048]{1,0:T(8,128)(2,1)}, bf16[256,2048]{1,0:T(8,128)(2,1)S(1)}, u32[]{:S(2)}, u32[]{:S(2)}) %collective-permute-start.20) | collective-permute-done | bytes 1048608 | tf_op jit(solution)/shard_map/ppermute | solution.py:479
  475.5 21.5 %collective-permute-done.19.refs_2_ = bf16[256,2048]{1,0:T(8,128)(2,1)S(1)} collective-permute-done((bf16[256,2048]{1,0:T(8,128)(2,1)}, bf16[256,2048]{1,0:T(8,128)(2,1)S(1)}, u32[]{:S(2)}, u32[]{:S(2)}) %collective-permute-start.19) | collective-permute-done | bytes 1048608 | tf_op jit(solution)/shard_map/ppermute | solution.py:479
  498.3 11.1 %mid_back.1 = (f32[256,2048]{1,0:T(8,128)}, bf16[256,2048]{1,0:T(8,128)(2,1)}, bf16[8,256,256]{2,1,0:T(8,128)(2,1)}, f32[1,2048]{1,0:T(1,128)}, f32[1,2048]{1,0:T(1,128)}) custom-call(s32[1]{0:T(128)} %bitcast.core_ref, bf16[256,2048]{1,0:T(8,128)(2,1)} %get-tuple-element.101.refs_0_, bf16[256,2048]{1,0:T(8,128)(2,1)} %copy-done.37, ...), custom_call_target="tpu_custom_call" | custom-call | flops 2147483648 | bytes 18874368 | tf_op jit(solution)/shard_map/mid_back/pallas_call | solution.py:280
  521.0 47.5 %collective-permute-done.26.refs_11_ = bf16[2,256,256]{2,1,0:T(8,128)(2,1)S(1)} collective-permute-done((bf16[2,256,256]{2,1,0:T(8,128)(2,1)S(1)}, bf16[2,256,256]{2,1,0:T(8,128)(2,1)S(1)}, u32[]{:S(2)}, u32[]{:S(2)}) %collective-permute-start.26) | collective-permute-done | bytes 262176 | tf_op jit(solution)/shard_map/ppermute | solution.py:679
  573.8 24.8 %attend_back.1 = (bf16[8,2,128,256]{3,2,1,0:T(8,128)(2,1)S(1)}, bf16[8,2,128,256]{3,2,1,0:T(8,128)(2,1)S(1)}, bf16[8,2,128,256]{3,2,1,0:T(8,128)(2,1)S(1)}) custom-call(bf16[8,2,128,256]{3,2,1,0:T(8,128)(2,1)S(1)} %get-tuple-element.83.q_ref, bf16[8,2,128,256]{3,2,1,0:T(8,128)(2,1)} %copy-done.19, bf16[8,2,128,256]{3,2,1,0:T(8,128)(2,1)} %copy-done.20, ...), custom_call_target="tpu_custom_call" | custom-call | flops 5368709120 | bytes 7340032 | tf_op jit(solution)/shard_map/attend_back/pallas_call | solution.py:187
  598.7 14.4 %joint.1 = bf16[2048,2560]{1,0:T(8,128)(2,1)} custom-call(bf16[2048,256]{1,0:T(8,128)(2,1)S(1)} %bitcast.195, bf16[2048,256]{1,0:T(8,128)(2,1)S(1)} %bitcast.193, bf16[2048,256]{1,0:T(8,128)(2,1)S(1)} %bitcast.191, bf16[2048,768]{1,0:T(8,128)(2,1)} %bitcast.7.w_ref.refs_3_, bf16[256,2048]{1,0:T(8,128)(2,1)S(1)} %copy-done.21, ...), custom_call_target="tpu_custom_call" | custom-call | flops 8589934592 | bytes 26214400 | tf_op jit(solution)/shard_map/joint/pallas_call | solution.py:341
  622.8 10.9 %convolution_convert_fusion.3 = bf16[2048,768]{1,0:T(8,128)(2,1)S(1)} fusion(bf16[2048,2048]{1,0:T(8,128)(2,1)} %get-tuple-element.112, bf16[2048,768]{1,0:T(8,128)(2,1)S(1)} %constant_dynamic-update-slice_fusion), kind=kOutput, calls=%fused_computation.20 | convolution fusion | flops 6444023808 | bytes 14680064 | tf_op jit(solution)/shard_map/dot_general | solution.py:26
  655.6 7.4 convert_reduce_fusion.1
  676.5 7.6 collective-permute-done.36
  684.5 22.5 %collective-permute-done.37 = bf16[512,768]{0,1:T(8,128)(2,1)} collective-permute-done((bf16[512,768]{0,1:T(8,128)(2,1)}, bf16[512,768]{0,1:T(8,128)(2,1)}, u32[]{:S(2)}, u32[]{:S(2)}) %collective-permute-start.37) | collective-permute-done | bytes 786464 | tf_op jit(solution)/shard_map/ppermute | solution.py:479
  732.9 6.0 collective-permute-start.40
  749.3 8.2 %collective-permute-done.40 = bf16[512,256]{1,0:T(8,128)(2,1)S(1)} collective-permute-done((bf16[512,256]{1,0:T(8,128)(2,1)S(1)}, bf16[512,256]{1,0:T(8,128)(2,1)S(1)}, u32[]{:S(2)}, u32[]{:S(2)}) %collective-permute-start.40) | collective-permute-done | bytes 262176 | tf_op jit(solution)/shard_map/ppermute | solution.py:436
  758.9 16.8 %reduce-scatter.8.cloned.1.call-done = bf16[256,2560]{1,0:T(8,128)(2,1)} async-done(((bf16[2048,2560]{1,0:T(8,128)(2,1)}), bf16[256,2560]{1,0:T(8,128)(2,1)}) %reduce-scatter.8.cloned.1.call-update) | async-done | bytes 1310736 | tf_op jit(solution)/shard_map/reduce_scatter | solution.py:685
  (339 shorter events, 210.0 us)
Async XLA Ops:
  7.2 128.5 %all-gather.7.cloned.1.call-start = ((), (), s32[]{:S(2)}) async-start(), calls=%async_computation.12 | async-start | bytes 5242880 | tf_op jit(solution)/shard_map/all_gather | solution.py:605
  9.9 200.2 %all-gather.5.cloned.1.call-start = ((), (), s32[]{:S(2)}) async-start(), calls=%async_computation.11 | async-start | bytes 9437184 | tf_op jit(solution)/shard_map/all_gather | solution.py:586
  45.9 199.8 %all-to-all-start.1 = ((bf16[4,512,1408]{2,1,0:T(8,128)(2,1)}), bf16[4,512,1408]{2,1,0:T(8,128)(2,1)}, u32[]{:S(2)}, u32[]{:S(2)}) async-start(bf16[4,512,1408]{2,1,0:T(8,128)(2,1)} %copy-done.4), calls=%async_computation.1 | async-start | bytes 11534336 | tf_op jit(solution)/shard_map/all_to_all | solution.py:607
  52.0 83.6 %collective-permute-start.2 = (bf16[3584]{0:T(1024)(128)(2,1)S(1)}, bf16[3584]{0:T(1024)(128)(2,1)S(1)}, u32[]{:S(2)}, u32[]{:S(2)}) collective-permute-start(bf16[3584]{0:T(1024)(128)(2,1)S(1)} %constant_dynamic-update-slice_fusion.3), channel_id=1, source_target_pairs={{0,3},{1,2},{2,1},{3,0},{4,7},{5,6},{6,5},{7,4},{8,11},{9,10},{10,... | collective-permute-start | bytes 21512 | tf_op jit(solution)/shard_map/ppermute | solution.py:453
  54.8 80.5 %collective-permute-start.1 = (bf16[3584]{0:T(1024)(128)(2,1)S(1)}, bf16[3584]{0:T(1024)(128)(2,1)S(1)}, u32[]{:S(2)}, u32[]{:S(2)}) collective-permute-start(bf16[3584]{0:T(1024)(128)(2,1)S(1)} %constant_dynamic-update-slice_fusion.3), channel_id=1, source_target_pairs={{0,2},{1,3},{2,0},{3,1},{4,6},{5,7},{6,4},{7,5},{8,10},{9,11},{10,... | collective-permute-start | bytes 21512 | tf_op jit(solution)/shard_map/ppermute | solution.py:453
  55.4 79.2 %collective-permute-start = (bf16[3584]{0:T(1024)(128)(2,1)S(1)}, bf16[3584]{0:T(1024)(128)(2,1)S(1)}, u32[]{:S(2)}, u32[]{:S(2)}) collective-permute-start(bf16[3584]{0:T(1024)(128)(2,1)S(1)} %constant_dynamic-update-slice_fusion.3), channel_id=1, source_target_pairs={{0,1},{1,0},{2,3},{3,2},{4,5},{5,4},{6,7},{7,6},{8,9},{9,8},{10,11... | collective-permute-start | bytes 21512 | tf_op jit(solution)/shard_map/ppermute | solution.py:453
  135.7 124.5 %collective-permute-start.7 = (bf16[4,256,2048]{2,1,0:T(8,128)(2,1)}, bf16[4,256,2048]{2,1,0:T(8,128)(2,1)}, u32[]{:S(2)}, u32[]{:S(2)}) collective-permute-start(bf16[4,256,2048]{2,1,0:T(8,128)(2,1)} %bitcast.212), channel_id=1, source_target_pairs={{0,4},{4,0},{8,12},{12,8},{16,20},{20,16},{24,28},{28,24},{1,5},{5... | collective-permute-start | bytes 12582920 | tf_op jit(solution)/shard_map/ppermute | solution.py:617
  251.2 38.4 %collective-permute-start.12 = (bf16[256,2048]{1,0:T(8,128)(2,1)}, bf16[256,2048]{1,0:T(8,128)(2,1)}, u32[]{:S(2)}, u32[]{:S(2)}) collective-permute-start(bf16[256,2048]{1,0:T(8,128)(2,1)} %bitcast.219), channel_id=1, source_target_pairs={{0,2},{1,3},{2,0},{3,1},{4,6},{5,7},{6,4},{7,5},{8,10},{9,11},{10,... | collective-permute-start | bytes 3145736 | tf_op jit(solution)/shard_map/ppermute | solution.py:459
  260.2 78.5 %collective-permute-start.17 = (bf16[2048,1408]{1,0:T(8,128)(2,1)}, bf16[2048,1408]{1,0:T(8,128)(2,1)}, u32[]{:S(2)}, u32[]{:S(2)}) collective-permute-start(bf16[2048,1408]{1,0:T(8,128)(2,1)} %bitcast.22), channel_id=1, source_target_pairs={{0,4},{4,0},{8,12},{12,8},{16,20},{20,16},{24,28},{28,24},{1,5},{5... | collective-permute-start | bytes 17301512 | tf_op jit(solution)/shard_map/ppermute | solution.py:609
  321.1 48.2 %collective-permute-start.15 = (bf16[128,2048]{1,0:T(8,128)(2,1)}, bf16[128,2048]{1,0:T(8,128)(2,1)}, u32[]{:S(2)}, u32[]{:S(2)}) collective-permute-start(bf16[128,2048]{1,0:T(8,128)(2,1)} %slice.109), channel_id=1, source_target_pairs={{0,1},{1,0},{2,3},{3,2},{4,5},{5,4},{6,7},{7,6},{8,9},{9,8},{10,11... | collective-permute-start | bytes 1572872 | tf_op jit(solution)/shard_map/ppermute | solution.py:473
  322.3 49.0 %collective-permute-start.16 = (bf16[128,2048]{1,0:T(8,128)(2,1)}, bf16[128,2048]{1,0:T(8,128)(2,1)}, u32[]{:S(2)}, u32[]{:S(2)}) collective-permute-start(bf16[128,2048]{1,0:T(8,128)(2,1)} %slice.110), channel_id=1, source_target_pairs={{0,2},{1,3},{2,0},{3,1},{4,6},{5,7},{6,4},{7,5},{8,10},{9,11},{10,... | collective-permute-start | bytes 1572872 | tf_op jit(solution)/shard_map/ppermute | solution.py:473
  333.5 35.8 %all-to-all-start.2 = ((bf16[4,176,2048]{2,1,0:T(8,128)(2,1)}), bf16[4,176,2048]{2,1,0:T(8,128)(2,1)}, u32[]{:S(2)}, u32[]{:S(2)}) async-start(bf16[4,176,2048]{2,1,0:T(8,128)(2,1)} %dynamic-slice_bitcast_fusion), calls=%async_computation.2 | async-start | bytes 5767168 | tf_op jit(solution)/shard_map/all_to_all | solution.py:634
  338.1 283.2 %reduce-scatter.4.cloned.1.call-start = ((), (), s32[]{:S(2)}) async-start(), calls=%async_computation.8 | async-start | bytes 12976128 | tf_op jit(solution)/shard_map/reduce_scatter | solution.py:662
  447.7 216.0 %reduce-scatter.6.cloned.1.call-start = ((), (), s32[]{:S(2)}) async-start(), calls=%async_computation.9 | async-start | bytes 6488064 | tf_op jit(solution)/shard_map/reduce_scatter | solution.py:643
  449.7 47.3 %collective-permute-start.19 = (bf16[256,2048]{1,0:T(8,128)(2,1)}, bf16[256,2048]{1,0:T(8,128)(2,1)S(1)}, u32[]{:S(2)}, u32[]{:S(2)}) collective-permute-start(bf16[256,2048]{1,0:T(8,128)(2,1)} %get-tuple-element.213), channel_id=1, source_target_pairs={{0,2},{1,3},{2,0},{3,1},{4,6},{5,7},{6,4},{7,5},{8,10},{9,11},{10,... | collective-permute-start | bytes 3145736 | tf_op jit(solution)/shard_map/ppermute | solution.py:479
  451.2 45.9 %collective-permute-start.18 = (bf16[256,2048]{1,0:T(8,128)(2,1)}, bf16[256,2048]{1,0:T(8,128)(2,1)S(1)}, u32[]{:S(2)}, u32[]{:S(2)}) collective-permute-start(bf16[256,2048]{1,0:T(8,128)(2,1)} %get-tuple-element.214), channel_id=1, source_target_pairs={{0,1},{1,0},{2,3},{3,2},{4,5},{5,4},{6,7},{7,6},{8,9},{9,8},{10,11... | collective-permute-start | bytes 3145736 | tf_op jit(solution)/shard_map/ppermute | solution.py:479
  509.5 61.1 %all-to-all-start.3 = ((bf16[8,256,256]{2,1,0:T(8,128)(2,1)}), bf16[8,256,256]{2,1,0:T(8,128)(2,1)}, u32[]{:S(2)}, u32[]{:S(2)}) async-start(bf16[8,256,256]{2,1,0:T(8,128)(2,1)} %get-tuple-element.105), calls=%async_computation.3 | async-start | bytes 2097152 | tf_op jit(solution)/shard_map/all_to_all | solution.py:671
  513.7 262.0 %reduce-scatter.8.cloned.1.call-start = ((), (), s32[]{:S(2)}) async-start(), calls=%async_computation.10 | async-start | bytes 11796480 | tf_op jit(solution)/shard_map/reduce_scatter | solution.py:685
  513.8 84.9 %collective-permute-start.23 = (bf16[256,2048]{1,0:T(8,128)(2,1)}, bf16[256,2048]{1,0:T(8,128)(2,1)}, u32[]{:S(2)}, u32[]{:S(2)}) collective-permute-start(bf16[256,2048]{1,0:T(8,128)(2,1)} %get-tuple-element.109.refs_4_), channel_id=1, source_target_pairs={{0,3},{1,2},{2,1},{3,0},{4,7},{5,6},{6,5},{7,4},{8,11},{9,10},{10,... | collective-permute-start | bytes 3145736 | tf_op jit(solution)/shard_map/ppermute | solution.py:453
  515.1 83.5 %collective-permute-start.22 = (bf16[256,2048]{1,0:T(8,128)(2,1)}, bf16[256,2048]{1,0:T(8,128)(2,1)}, u32[]{:S(2)}, u32[]{:S(2)}) collective-permute-start(bf16[256,2048]{1,0:T(8,128)(2,1)} %get-tuple-element.109.refs_4_), channel_id=1, source_target_pairs={{0,2},{1,3},{2,0},{3,1},{4,6},{5,7},{6,4},{7,5},{8,10},{9,11},{10,... | collective-permute-start | bytes 3145736 | tf_op jit(solution)/shard_map/ppermute | solution.py:453
  516.7 81.9 %collective-permute-start.21 = (bf16[256,2048]{1,0:T(8,128)(2,1)}, bf16[256,2048]{1,0:T(8,128)(2,1)}, u32[]{:S(2)}, u32[]{:S(2)}) collective-permute-start(bf16[256,2048]{1,0:T(8,128)(2,1)} %get-tuple-element.109.refs_4_), channel_id=1, source_target_pairs={{0,1},{1,0},{2,3},{3,2},{4,5},{5,4},{6,7},{7,6},{8,9},{9,8},{10,11... | collective-permute-start | bytes 3145736 | tf_op jit(solution)/shard_map/ppermute | solution.py:453
  518.2 50.3 %collective-permute-start.26 = (bf16[2,256,256]{2,1,0:T(8,128)(2,1)S(1)}, bf16[2,256,256]{2,1,0:T(8,128)(2,1)S(1)}, u32[]{:S(2)}, u32[]{:S(2)}) collective-permute-start(bf16[2,256,256]{2,1,0:T(8,128)(2,1)S(1)} %get-tuple-element.226), channel_id=1, source_target_pairs={{0,3},{1,2},{2,1},{3,0},{4,7},{5,6},{6,5},{7,4},{8,11},{9,10},{10,... | collective-permute-start | bytes 786440 | tf_op jit(solution)/shard_map/ppermute | solution.py:679
  519.5 79.2 %collective-permute-start.25 = (bf16[2,256,256]{2,1,0:T(8,128)(2,1)}, bf16[2,256,256]{2,1,0:T(8,128)(2,1)}, u32[]{:S(2)}, u32[]{:S(2)}) collective-permute-start(bf16[2,256,256]{2,1,0:T(8,128)(2,1)} %get-tuple-element.227), channel_id=1, source_target_pairs={{0,2},{1,3},{2,0},{3,1},{4,6},{5,7},{6,4},{7,5},{8,10},{9,11},{10,... | collective-permute-start | bytes 786440 | tf_op jit(solution)/shard_map/ppermute | solution.py:679
  617.8 36.2 %collective-permute-start.33 = (bf16[256,2048]{1,0:T(8,128)(2,1)}, bf16[256,2048]{1,0:T(8,128)(2,1)}, u32[]{:S(2)}, u32[]{:S(2)}) collective-permute-start(bf16[256,2048]{1,0:T(8,128)(2,1)} %get-tuple-element.118), channel_id=1, source_target_pairs={{0,1},{1,0},{2,3},{3,2},{4,5},{5,4},{6,7},{7,6},{8,9},{9,8},{10,11... | collective-permute-start | bytes 3145736 | tf_op jit(solution)/shard_map/ppermute | solution.py:479
  618.5 55.3 %collective-permute-start.34 = (bf16[256,2048]{1,0:T(8,128)(2,1)}, bf16[256,2048]{1,0:T(8,128)(2,1)}, u32[]{:S(2)}, u32[]{:S(2)}) collective-permute-start(bf16[256,2048]{1,0:T(8,128)(2,1)} %get-tuple-element.119), channel_id=1, source_target_pairs={{0,2},{1,3},{2,0},{3,1},{4,6},{5,7},{6,4},{7,5},{8,10},{9,11},{10,... | collective-permute-start | bytes 3145736 | tf_op jit(solution)/shard_map/ppermute | solution.py:479
  619.9 103.2 %collective-permute-start.35 = (bf16[256,2048]{1,0:T(8,128)(2,1)}, bf16[256,2048]{1,0:T(8,128)(2,1)}, u32[]{:S(2)}, u32[]{:S(2)}) collective-permute-start(bf16[256,2048]{1,0:T(8,128)(2,1)} %get-tuple-element.120), channel_id=1, source_target_pairs={{0,3},{1,2},{2,1},{3,0},{4,7},{5,6},{6,5},{7,4},{8,11},{9,10},{10,... | collective-permute-start | bytes 3145736 | tf_op jit(solution)/shard_map/ppermute | solution.py:479
  641.2 42.9 %collective-permute-start.36 = (bf16[512,768]{0,1:T(8,128)(2,1)}, bf16[512,768]{0,1:T(8,128)(2,1)}, u32[]{:S(2)}, u32[]{:S(2)}) collective-permute-start(bf16[512,768]{0,1:T(8,128)(2,1)} %bitcast.239), channel_id=1, source_target_pairs={{0,1},{1,0},{2,3},{3,2},{4,5},{5,4},{6,7},{7,6},{8,9},{9,8},{10,11... | collective-permute-start | bytes 2359304 | tf_op jit(solution)/shard_map/ppermute | solution.py:479
  641.9 65.1 %collective-permute-start.37 = (bf16[512,768]{0,1:T(8,128)(2,1)}, bf16[512,768]{0,1:T(8,128)(2,1)}, u32[]{:S(2)}, u32[]{:S(2)}) collective-permute-start(bf16[512,768]{0,1:T(8,128)(2,1)} %bitcast.238), channel_id=1, source_target_pairs={{0,2},{1,3},{2,0},{3,1},{4,6},{5,7},{6,4},{7,5},{8,10},{9,11},{10,... | collective-permute-start | bytes 2359304 | tf_op jit(solution)/shard_map/ppermute | solution.py:479
  654.1 55.0 %collective-permute-start.38 = (bf16[512,768]{0,1:T(8,128)(2,1)S(1)}, bf16[512,768]{0,1:T(8,128)(2,1)}, u32[]{:S(2)}, u32[]{:S(2)}) collective-permute-start(bf16[512,768]{0,1:T(8,128)(2,1)S(1)} %bitcast.237), channel_id=1, source_target_pairs={{0,3},{1,2},{2,1},{3,0},{4,7},{5,6},{6,5},{7,4},{8,11},{9,10},{10,... | collective-permute-start | bytes 2359304 | tf_op jit(solution)/shard_map/ppermute | solution.py:479
  664.7 58.4 %all-to-all-start.4 = ((f32[32,1,448]{2,1,0:T(1,128)}), f32[32,1,448]{2,1,0:T(1,128)S(1)}, u32[]{:S(2)}, u32[]{:S(2)}) async-start(f32[32,1,448]{2,1,0:T(1,128)} %all_to_all.24), calls=%async_computation.7 | async-start | bytes 131072 | tf_op jit(solution)/shard_map/all_to_all | solution.py:734
  673.8 55.2 %collective-permute-start.29 = (bf16[2,176,512]{2,1,0:T(8,128)(2,1)}, bf16[2,176,512]{2,1,0:T(8,128)(2,1)}, u32[]{:S(2)}, u32[]{:S(2)}) collective-permute-start(bf16[2,176,512]{2,1,0:T(8,128)(2,1)} %get-tuple-element.222), channel_id=1, source_target_pairs={{0,3},{1,2},{2,1},{3,0},{4,7},{5,6},{6,5},{7,4},{8,11},{9,10},{10,... | collective-permute-start | bytes 1081352 | tf_op jit(solution)/shard_map/ppermute | solution.py:536
  684.1 44.9 %collective-permute-start.28 = (bf16[2,176,512]{2,1,0:T(8,128)(2,1)}, bf16[2,176,512]{2,1,0:T(8,128)(2,1)}, u32[]{:S(2)}, u32[]{:S(2)}) collective-permute-start(bf16[2,176,512]{2,1,0:T(8,128)(2,1)} %get-tuple-element.223), channel_id=1, source_target_pairs={{0,2},{1,3},{2,0},{3,1},{4,6},{5,7},{6,4},{7,5},{8,10},{9,11},{10,... | collective-permute-start | bytes 1081352 | tf_op jit(solution)/shard_map/ppermute | solution.py:536
  (74 other events, 1555.6 us)
Sparse Core Ops, SparseCore 0:
  10.4 116.4 all-gather.6
  128.5 81.5 all-gather.4
  447.8 135.5 reduce-scatter.3
  585.5 67.9 reduce-scatter.5
  655.6 120.0 reduce-scatter.7
